TPU v7x, 32 devices: a whole 2x2x4 slice. The times are simulated.
32 devices in a mesh: seg: 4 (over z), sec: 8 (over y, x, core).
Axes of the slice: x: 2, y: 2, z: 4, core: 2. Of those that a mesh axis runs over, the one named last changes fastest.
Arguments:
- wave_first: float32 [4, 64, 128, 128], P('seg', 'sec')
- wave_second: float32 [4, 64, 128, 128], P('seg', 'sec')
- onsite_first: float32 [4, 64, 128, 128], P('seg', 'sec'), may hold values from 0.5 to 4
- onsite_second: float32 [4, 64, 128, 128], P('seg', 'sec'), may hold values from 0.5 to 4
- left_first: bfloat16 [4, 64, 16, 128, 128], P('seg', 'sec'), may hold values from -0.5 to 0.5
- right_first: bfloat16 [4, 64, 16, 128, 128], P('seg', 'sec'), may hold values from -0.125 to 0.125
- left_base: bfloat16 [4, 64, 16, 128, 128], P('seg', 'sec'), may hold values from -0.5 to 0.5
- right_second: bfloat16 [4, 64, 16, 128, 128], P('seg', 'sec'), may hold values from -0.125 to 0.125
- sources: int32 [64, 16], P('sec'), may hold values from 0 to 63, as said below
- block_dims: int32 [64], P('sec'), may hold values from 8 to 128, as said below
Outputs:
- result_first: float32 [4, 64, 128, 128], P('seg', 'sec')
- result_second: float32 [4, 64, 128, 128], P('seg', 'sec')
Inputs may be any that keep to these rules, and one draw needn't show every extreme that they name: `sources`: each entry names a block whose index differs from its row's block by at most 8, and that difference is reached. `block_dims`: a multiple of 8.
All inputs are finite; a program needn't handle non-finite values.
Results may differ from a plain program's by a relative error of at most 0.015.
Values may be sent and summed in bfloat16 or wider, within the bound.
No kernel may reach another device: no remote copies, remote signals or barrier semaphores. Data moves between devices by JAX's collectives and lax.ppermute only.
A program may use at most 128 MiB of HBM per device.

v0:
```python
import functools

import jax
import jax.numpy as jnp
from jax import lax
from jax.experimental import pallas as pl
from jax.experimental.pallas import tpu as pltpu
from jax.sharding import PartitionSpec as P

STEPS = 3
EPS = 1e-6
F32 = jnp.float32
BF16 = jnp.bfloat16


def even_pairs(count):
    return [(i, i ^ 1) for i in range(count) if i ^ 1 < count]


def odd_pairs(count):
    pairs = [(i, i + 1 if i % 2 else i - 1) for i in range(1, count)]
    return [(i, j) for i, j in pairs if j < count]


def swapped(block):
    count = lax.axis_size("sec")
    odd = lax.ppermute(block, "sec", odd_pairs(count))
    even = lax.ppermute(block, "sec", even_pairs(count))
    return even, odd


def gathered_parts(partial):
    count = lax.axis_size("sec")
    if count & (count - 1) or count < 2:
        return [lax.psum(partial, "sec")]
    pair = partial + lax.ppermute(partial, "sec", even_pairs(count))
    parts = [pair]
    for m in range(1, count // 2):
        parts += [lax.ppermute(pair, "sec", [(i, i ^ (2 * m)) for i in range(count)])]
    return parts


def live_of(dim, width):
    rows = lax.broadcasted_iota(jnp.int32, (width, width), 0)
    cols = lax.broadcasted_iota(jnp.int32, (width, width), 1)
    return (rows < dim) & (cols < dim)


def folded(value):
    rows, lanes = value.shape
    return jnp.sum(value.reshape(rows // 8, 8, lanes), axis=0)


def put_row(ref, row, value):
    ref[row : row + 1, :] = jnp.sum(value, axis=0, keepdims=True)


def scalar_row(value, lanes):
    lane = lax.broadcasted_iota(jnp.int32, (1, lanes), 1)
    return jnp.where(lane == 0, value, 0.0)


def totals(refs):
    total = refs[0][...]
    for ref in refs[1:]:
        total = total + ref[...]
    return [jnp.sum(total[r : r + 1, :], axis=1, keepdims=True) for r in range(8)]


def apply_terms(src, dims, x, left, right, lxs, blocks, terms, width, emit, ready=None):
    lanes = len(lxs)

    def body(i, carry):
        if ready is not None:
            ready(i)
        for j in range(lanes):
            b = i * lanes + j
            for k in range(terms):
                part = jnp.dot(left[b, k], x[src[b, k]], preferred_element_type=F32)
                lxs[j][:, k * width : (k + 1) * width] = part.astype(BF16)
            total = jnp.dot(
                lxs[j][...],
                right[b].reshape(terms * width, width),
                preferred_element_type=F32,
            )
            emit(b, jnp.where(live_of(dims[b], width), total, 0.0))
        return carry

    lax.fori_loop(0, blocks // lanes, body, 0)


def prepare_kernel(dims, wave, u, packed, sems):
    blocks, width, _ = u.shape
    copies = [pltpu.make_async_copy(wave.at[b], u.at[b], sems.at[b]) for b in range(blocks)]
    for copy in copies:
        copy.start()
    for b in range(blocks):
        copies[b].wait()
        value = jnp.where(live_of(dims[b], width), u[b], 0.0)
        u[b] = value
        packed[b] = value.astype(BF16)


def send_kernel(dims, packed, onsite_hbm, later_hbm, wave_hbm, *rest):
    weight, bundle, onsite, later, wave, sems = rest
    del packed
    pairs = ((onsite_hbm, onsite), (wave_hbm, wave), (later_hbm, later))
    copies = [pltpu.make_async_copy(s, t, sems.at[i]) for i, (s, t) in enumerate(pairs)]
    for copy in copies:
        copy.start()
    blocks, width, _ = wave.shape
    copies[0].wait()

    def first(b, carry):
        weight[b] = (1.0 / (onsite[b] + 1.0)).astype(BF16)
        return carry

    lax.fori_loop(0, blocks, first, 0)
    copies[1].wait()
    copies[2].wait()

    def second(b, carry):
        bundle[b] = jnp.where(live_of(dims[b], width), wave[b], 0.0).astype(BF16)
        bundle[blocks + b] = (1.0 / (later[b] + 1.0)).astype(BF16)
        return carry

    lax.fori_loop(0, blocks, second, 0)


def start_kernel(src, dims, even, odd, u, onsite_hbm, left_hbm, right_hbm, *rest):
    term, sent, stats, onsite, left, right, x, acc, sems, *lxs = rest
    blocks, terms, width, _ = left.shape
    lanes = len(lxs)

    def copies_of(group):
        part = pl.ds(group * lanes, lanes)
        pairs = ((left_hbm, left), (right_hbm, right), (onsite_hbm, onsite))
        return [
            pltpu.make_async_copy(s.at[part], t.at[part], sems.at[i, group])
            for i, (s, t) in enumerate(pairs)
        ]

    for group in range(blocks // lanes):
        for copy in copies_of(group):
            copy.start()
    x[:blocks] = even[...]
    x[2 * blocks :] = odd[...]

    def first(b, carry):
        x[blocks + b] = u[b].astype(BF16)
        return carry

    lax.fori_loop(0, blocks, first, 0)
    acc[...] = jnp.zeros_like(acc)

    def emit(b, value):
        term[b] = value
        sent[b] = value.astype(BF16)
        mine = u[b]
        acc[0] += folded(mine * mine)
        acc[1] += folded(mine * (onsite[b] * mine + value))

    def ready(group):
        for copy in copies_of(group):
            copy.wait()

    apply_terms(src, dims, x, left, right, lxs, blocks, terms, width, emit, ready)
    stats[...] = jnp.zeros_like(stats)
    for row in range(2):
        put_row(stats, row, acc[row])


def ahead_kernel(src, dims, even, odd, wave, right, u, y, x):
    blocks, terms, width, _ = right.shape
    x[:blocks] = even[...]
    x[2 * blocks :] = odd[...]

    def first(b, carry):
        value = jnp.where(live_of(dims[b], width), wave[b], 0.0)
        u[b] = value
        x[blocks + b] = value.astype(BF16)
        return carry

    lax.fori_loop(0, blocks, first, 0)

    def body(b, carry):
        for k in range(terms):
            part = jnp.dot(x[src[b, k]], right[b, k], preferred_element_type=F32)
            y[b, k * width : (k + 1) * width, :] = part.astype(BF16)
        return carry

    lax.fori_loop(0, blocks, body, 0)


def build_kernel(dims, handed, base, y, u, onsite, term, sent, stats, left, acc, *works):
    blocks, terms, width, _ = base.shape
    lanes = len(works)
    acc[...] = jnp.zeros_like(acc)

    def body(i, carry):
        for j in range(lanes):
            b = i * lanes + j
            work = works[j]
            block = handed[b]
            flipped = (block.astype(F32).T * (1.0 / width)).astype(BF16)
            carried = jnp.dot(
                base[b].reshape(terms * width, width), block, preferred_element_type=F32
            )
            work[...] = carried.astype(BF16)
            pieces = []
            for k in range(terms):
                added = jnp.dot(
                    flipped, work[k * width : (k + 1) * width, :], preferred_element_type=F32
                )
                piece = (base[b, k].astype(F32) + added).astype(BF16)
                left[b, k] = piece
                pieces.append(piece)
            total = jnp.dot(jnp.concatenate(pieces, axis=1), y[b], preferred_element_type=F32)
            value = jnp.where(live_of(dims[b], width), total, 0.0)
            term[b] = value
            sent[b] = value.astype(BF16)
            mine = u[b]
            acc[0] += folded(mine * mine)
            acc[1] += folded(mine * (onsite[b] * mine + value))
        return carry

    lax.fori_loop(0, blocks // lanes, body, 0)
    stats[...] = jnp.zeros_like(stats)
    for row in range(2):
        put_row(stats, row, acc[row])


def next_kernel(n_parts, entries, share, first, last, *refs):
    src, dims, *rest = refs
    parts, rest = rest[:n_parts], rest[n_parts:]
    (u, term, onsite, left, right, u_even, u_odd, t_even, t_odd, w_even, w_odd, *rest) = rest
    if last:
        un, tn, stats, x, acc, *lxs = rest
    else:
        un, tn, sent, stats, un_even, un_odd, x, acc, *lxs = rest
    blocks, width = u.shape[0], u.shape[1]
    terms = left.shape[1]
    sums = totals(parts)
    quotient = sums[1] / sums[0]
    eps = EPS if first else sums[5]
    scale = 1.0 / jnp.sqrt(sums[0] / entries + eps)
    grow = (1.0 + quotient) * scale

    def others(w, before, t, after, at):
        def body(b, carry):
            value = w[b].astype(F32) * (
                grow * before[b].astype(F32) - scale * t[b].astype(F32)
            )
            if not last:
                after[b] = value
            x[at + b] = value.astype(BF16)
            return carry

        lax.fori_loop(0, blocks, body, 0)

    others(w_even, u_even, t_even, None if last else un_even, 0)
    others(w_odd, u_odd, t_odd, None if last else un_odd, 2 * blocks)

    def own(b, carry):
        value = (grow * u[b] - scale * term[b]) / (onsite[b] + 1.0)
        un[b] = value
        x[blocks + b] = value.astype(BF16)
        return carry

    lax.fori_loop(0, blocks, own, 0)
    acc[...] = jnp.zeros_like(acc)

    def emit(b, value):
        tn[b] = value
        mine = un[b]
        acc[0] += folded(mine * mine)
        acc[1] += folded(mine * (onsite[b] * mine + value))
        if last:
            weight = 1.0 / (onsite[b] + 1.0)
            along = weight * mine
            guess = (1.0 + quotient) * along - weight * value
            acc[2] += folded(guess * guess)
            acc[3] += folded(guess * along)
            acc[4] += folded(along * along)
        else:
            sent[b] = value.astype(BF16)

    apply_terms(src, dims, x, left, right, lxs, blocks, terms, width, emit)
    stats[...] = jnp.zeros_like(stats)
    for row in range(5 if last else 2):
        put_row(stats, row, acc[row])
    lanes = stats.shape[1]
    if last:
        stats[5:6, :] = scalar_row(quotient * share, lanes)
    else:
        stats[5:6, :] = scalar_row((EPS * scale * scale if first else EPS) * share, lanes)


def final_kernel(n_parts, entries, *refs):
    parts, rest = refs[:n_parts], refs[n_parts:]
    u, term, onsite, *outs = rest
    sums = totals(parts)
    quotient = sums[1] / sums[0]
    scale = 1.0 / jnp.sqrt(sums[0] / entries + EPS)
    delta = quotient - sums[5]
    length = sums[2] + 2.0 * delta * sums[3] + delta * delta * sums[4]
    scale = scale / jnp.sqrt(length * scale * scale / entries + EPS)
    grow = (1.0 + quotient) * scale

    def body(b, carry):
        value = (grow * u[b] - scale * term[b]) / (onsite[b] + 1.0)
        outs[0][b] = value
        if len(outs) > 1:
            outs[1][b] = value.astype(BF16)
        return carry

    lax.fori_loop(0, u.shape[0], body, 0)


VMEM = pl.BlockSpec(memory_space=pltpu.VMEM)
SMEM = pl.BlockSpec(memory_space=pltpu.SMEM)
HBM = pl.BlockSpec(memory_space=pltpu.HBM)


def call(kernel, scalars, arrays, outs, scratch, far=()):
    return pl.pallas_call(
        kernel,
        out_shape=outs,
        in_specs=[SMEM] * len(scalars) + [VMEM] * len(arrays) + [HBM] * len(far),
        out_specs=[VMEM] * len(outs),
        scratch_shapes=scratch,
        compiler_params=pltpu.CompilerParams(vmem_limit_bytes=16 << 20),
    )(*scalars, *arrays, *[pltpu.with_memory_space_constraint(a, pltpu.HBM) for a in far])


def like(shape, dtype):
    return jax.ShapeDtypeStruct(shape, dtype)


def both_updates(*args):
    (
        wave_first,
        wave_second,
        onsite_first,
        onsite_second,
        left_first,
        right_first,
        left_base,
        right_second,
        sources,
        block_dims,
    ) = [a[0] if a.ndim > 3 else a for a in args]
    block_dims = pltpu.with_memory_space_constraint(block_dims, pltpu.HBM)
    blocks, width = wave_first.shape[0], wave_first.shape[1]
    terms = left_first.shape[1]
    count = lax.axis_size("sec")
    entries = float(blocks * count * width * width)

    lanes = max(j for j in (1, 2, 4) if blocks % j == 0)
    vec = (blocks, width, width)
    lxs = [pltpu.VMEM((width, terms * width), BF16)] * lanes
    x_shape = pltpu.VMEM((3 * blocks, width, width), BF16)
    acc_shape = pltpu.VMEM((5, 8, width), F32)
    stats_shape = like((8, width), F32)

    def later_steps(u, term, sent, stats, onsite, left, right, u_halo, w_halo, bundle=None):
        for step in range(1, STEPS):
            last = step == STEPS - 1
            t_halo = swapped(sent)
            parts = gathered_parts(stats)
            if last and bundle is not None:
                arrived = swapped(bundle)
            outs = [like(vec, F32), like(vec, F32)]
            if last:
                outs += [stats_shape]
            else:
                outs += [like(vec, BF16), stats_shape, like(vec, F32), like(vec, F32)]
            res = call(
                functools.partial(
                    next_kernel, len(parts), entries, 1.0 / count, step == 1, last
                ),
                [src, block_dims],
                [*parts, u, term, onsite, left, right, *u_halo, *t_halo, *w_halo],
                outs,
                [x_shape, acc_shape, *lxs],
            )
            if last:
                u, term, stats = res
            else:
                u, term, sent, stats, *u_halo = res
        out = (u, term, gathered_parts(stats))
        return out if bundle is None else (*out, arrived)

    def final(u, term, parts, onsite, narrow):
        outs = [like(vec, F32)] + ([like(vec, BF16)] if narrow else [])
        return call(
            functools.partial(final_kernel, len(parts), entries),
            [],
            [*parts, u, term, onsite],
            outs,
            [],
        )

    u, packed = call(
        prepare_kernel,
        [block_dims],
        [],
        [like(vec, F32), like(vec, BF16)],
        [pltpu.SemaphoreType.DMA((blocks,))],
        [wave_first],
    )
    halo_first = swapped(packed)
    weight, bundle = call(
        send_kernel,
        [block_dims],
        [packed],
        [like(vec, BF16), like((2 * blocks, width, width), BF16)],
        [pltpu.VMEM(vec, F32)] * 3 + [pltpu.SemaphoreType.DMA((3,))],
        [onsite_first, onsite_second, wave_second],
    )
    w_first = swapped(weight)
    here = lax.axis_index("sec")
    local = sources - here * blocks + blocks
    group = local // blocks
    src = jnp.where(here % 2 == 0, (2 - group) * blocks + local % blocks, local)

    pairs = max(j for j in (1, 2) if blocks % j == 0)
    term, sent, stats = call(
        start_kernel,
        [src, block_dims],
        [*halo_first, u],
        [like(vec, F32), like(vec, BF16), stats_shape],
        [
            pltpu.VMEM(vec, F32),
            pltpu.VMEM(left_first.shape, BF16),
            pltpu.VMEM(right_first.shape, BF16),
            x_shape,
            acc_shape,
            pltpu.SemaphoreType.DMA((3, blocks // pairs)),
            *lxs[:pairs],
        ],
        [onsite_first, left_first, right_first],
    )
    onsite, left, right = onsite_first, left_first, right_first
    u, term, parts, second = later_steps(
        u, term, sent, stats, onsite, left, right, halo_first, w_first, bundle
    )
    result_first, handed = final(u, term, parts, onsite, True)
    segs = lax.axis_size("seg")
    handed = lax.ppermute(handed, "seg", [(s, s + 1) for s in range(segs - 1)])

    halo_second = [part[:blocks] for part in second]
    w_second = [part[blocks:] for part in second]
    u, y = call(
        ahead_kernel,
        [src, block_dims],
        [*halo_second, wave_second, right_second],
        [like(vec, F32), like((blocks, terms * width, width), BF16)],
        [x_shape],
    )
    term, sent, stats, left_second = call(
        build_kernel,
        [block_dims],
        [handed, left_base, y, u, onsite_second],
        [like(vec, F32), like(vec, BF16), stats_shape, like(left_base.shape, BF16)],
        [acc_shape] + [pltpu.VMEM((terms * width, width), BF16)] * pairs,
    )
    u, term, parts = later_steps(
        u, term, sent, stats, onsite_second, left_second, right_second, halo_second, w_second
    )
    (result_second,) = final(u, term, parts, onsite_second, False)
    return result_first[None], result_second[None]


def solution(mesh):
    vector = P("seg", "sec", None, None)
    matrices = P("seg", "sec", None, None, None)
    placed = (vector,) * 4 + (matrices,) * 4 + (P("sec", None), P("sec"))
    return jax.shard_map(
        both_updates,
        mesh=mesh,
        in_specs=placed,
        out_specs=(vector, vector),
        check_vma=False,
    )
```

profile of v0, /device:TPU:0, one launch (start us, length us, event | category | flops | bytes accessed | tf_op | source)
XLA Modules:
  0.0 139.3 jit_solution(10370721931213662079)
XLA Ops:
  0.6 1.8 %shard_map.113 = (f32[8,128,128]{2,1,0:T(8,128)S(1)}, bf16[8,128,128]{2,1,0:T(8,128)(2,1)S(1)}) custom-call(s32[8]{0:T(128)} %refs_1_.7, f32[8,128,128]{2,1,0:T(8,128)} %bitcast.32), custom_call_target="tpu_custom_call" | custom-call | tf_op jit(solution)/shard_map/pallas_call | solution.py:326
  2.4 0.7 collective-permute-start.1
  3.1 4.4 %collective-permute-start = (bf16[8,128,128]{2,1,0:T(8,128)(2,1)S(1)}, bf16[8,128,128]{2,1,0:T(8,128)(2,1)S(1)}, u32[]{:S(2)}, u32[]{:S(2)}) collective-permute-start(bf16[8,128,128]{2,1,0:T(8,128)(2,1)S(1)} %get-tuple-element.35.packed), channel_id=1, source_target_pairs={{0,1},{1,0},{2,3},{3,2},{4,5},{5,4},{6,7},{7,6},{8,9},{9,8},{10,11... | collective-permute-start | bytes 786440 | tf_op jit(solution)/shard_map/ppermute | solution.py:28
  7.5 2.3 %shard_map.115 = (bf16[8,128,128]{2,1,0:T(8,128)(2,1)S(1)}, bf16[16,128,128]{2,1,0:T(8,128)(2,1)S(1)}) custom-call(s32[8]{0:T(128)} %refs_1_.7, bf16[8,128,128]{2,1,0:T(8,128)(2,1)S(1)} %get-tuple-element.35.packed, f32[8,128,128]{2,1,0:T(8,128)} %bitcast.19, f32[8,128,128]{2,1,0:T(8,128)} %bitcast.24, f32[8,128,128]{2,1,0:T(8,128)} %bitcast.30), custom_call_target="tpu_custom_call" | custom-call | tf_op jit(solution)/shard_map/pallas_call | solution.py:326
  9.8 0.7 collective-permute-start.9
  10.5 2.9 %collective-permute-start.8 = (bf16[8,128,128]{2,1,0:T(8,128)(2,1)S(1)}, bf16[8,128,128]{2,1,0:T(8,128)(2,1)S(1)}, u32[]{:S(2)}, u32[]{:S(2)}) collective-permute-start(bf16[8,128,128]{2,1,0:T(8,128)(2,1)S(1)} %get-tuple-element.40), channel_id=1, source_target_pairs={{0,1},{1,0},{2,3},{3,2},{4,5},{5,4},{6,7},{7,6},{8,9},{9,8},{10,11... | collective-permute-start | bytes 786440 | tf_op jit(solution)/shard_map/ppermute | solution.py:28
  13.4 0.7 fusion.3.src.refs_0_
  14.1 6.2 %shard_map.114 = (f32[8,128,128]{2,1,0:T(8,128)S(1)}, bf16[8,128,128]{2,1,0:T(8,128)(2,1)S(1)}, f32[8,128]{1,0:T(8,128)S(1)}) custom-call(s32[8,16]{1,0:T(8,128)S(1)} %fusion.3.src.refs_0_, s32[8]{0:T(128)} %refs_1_.7, bf16[8,128,128]{2,1,0:T(8,128)(2,1)S(1)} %collective-permute-done.even.refs_11_, ...), custom_call_target="tpu_custom_call" | custom-call | tf_op jit(solution)/shard_map/pallas_call | solution.py:326
  20.4 0.7 collective-permute-start.7
  21.0 2.9 %collective-permute-start.6 = (bf16[8,128,128]{2,1,0:T(8,128)(2,1)S(1)}, bf16[8,128,128]{2,1,0:T(8,128)(2,1)S(1)}, u32[]{:S(2)}, u32[]{:S(2)}) collective-permute-start(bf16[8,128,128]{2,1,0:T(8,128)(2,1)S(1)} %get-tuple-element.39), channel_id=1, source_target_pairs={{0,1},{1,0},{2,3},{3,2},{4,5},{5,4},{6,7},{7,6},{8,9},{9,8},{10,11... | collective-permute-start | bytes 786440 | tf_op jit(solution)/shard_map/ppermute | solution.py:28
  24.0 1.1 collective-permute-done.2
  25.1 0.7 collective-permute-start.22
  25.8 4.8 %collective-permute-start.5 = (f32[8,128]{1,0:T(8,128)S(1)}, f32[8,128]{1,0:T(8,128)S(1)}, u32[]{:S(2)}, u32[]{:S(2)}) collective-permute-start(f32[8,128]{1,0:T(8,128)S(1)} %add.39.refs_2_), channel_id=1, source_target_pairs={{0,6},{1,7},{2,4},{3,5},{4,2},{5,3},{6,0},{7,1},{8,14},{9,15},{10,... | collective-permute-start | bytes 12296 | tf_op jit(solution)/shard_map/ppermute | solution.py:39
  30.6 7.1 %collective-permute-done.5.refs_5_ = f32[8,128]{1,0:T(8,128)S(1)} collective-permute-done((f32[8,128]{1,0:T(8,128)S(1)}, f32[8,128]{1,0:T(8,128)S(1)}, u32[]{:S(2)}, u32[]{:S(2)}) %collective-permute-start.5) | collective-permute-done | bytes 4128 | tf_op jit(solution)/shard_map/ppermute | solution.py:39
  37.8 5.4 %collective-permute-start.4 = (f32[8,128]{1,0:T(8,128)S(1)}, f32[8,128]{1,0:T(8,128)S(1)}, u32[]{:S(2)}, u32[]{:S(2)}) collective-permute-start(f32[8,128]{1,0:T(8,128)S(1)} %add.39.refs_2_), channel_id=1, source_target_pairs={{0,4},{1,5},{2,6},{3,7},{4,0},{5,1},{6,2},{7,3},{8,12},{9,13},{10,... | collective-permute-start | bytes 12296 | tf_op jit(solution)/shard_map/ppermute | solution.py:39
  43.2 1.6 %collective-permute-done.4.refs_4_ = f32[8,128]{1,0:T(8,128)S(1)} collective-permute-done((f32[8,128]{1,0:T(8,128)S(1)}, f32[8,128]{1,0:T(8,128)S(1)}, u32[]{:S(2)}, u32[]{:S(2)}) %collective-permute-start.4) | collective-permute-done | bytes 4128 | tf_op jit(solution)/shard_map/ppermute | solution.py:39
  44.8 3.7 %collective-permute-start.3 = (f32[8,128]{1,0:T(8,128)S(1)}, f32[8,128]{1,0:T(8,128)S(1)}, u32[]{:S(2)}, u32[]{:S(2)}) collective-permute-start(f32[8,128]{1,0:T(8,128)S(1)} %add.39.refs_2_), channel_id=1, source_target_pairs={{0,2},{1,3},{2,0},{3,1},{4,6},{5,7},{6,4},{7,5},{8,10},{9,11},{10,... | collective-permute-start | bytes 12296 | tf_op jit(solution)/shard_map/ppermute | solution.py:39
  48.5 1.6 %collective-permute-done.3.refs_3_ = f32[8,128]{1,0:T(8,128)S(1)} collective-permute-done((f32[8,128]{1,0:T(8,128)S(1)}, f32[8,128]{1,0:T(8,128)S(1)}, u32[]{:S(2)}, u32[]{:S(2)}) %collective-permute-start.3) | collective-permute-done | bytes 4128 | tf_op jit(solution)/shard_map/ppermute | solution.py:39
  50.1 4.5 %shard_map.116 = (f32[8,128,128]{2,1,0:T(8,128)S(1)}, f32[8,128,128]{2,1,0:T(8,128)S(1)}, bf16[8,128,128]{2,1,0:T(8,128)(2,1)S(1)}, f32[8,128]{1,0:T(8,128)S(1)}...) custom-call(s32[8,16]{1,0:T(8,128)S(1)} %fusion.3.src.refs_0_, s32[8]{0:T(128)} %refs_1_.7, ...), custom_call_target="tpu_custom_call" | custom-call | tf_op jit(solution)/shard_map/pallas_call | solution.py:326
  54.6 0.7 collective-permute-start.15
  55.3 3.4 %collective-permute-start.14 = (bf16[8,128,128]{2,1,0:T(8,128)(2,1)S(1)}, bf16[8,128,128]{2,1,0:T(8,128)(2,1)S(1)}, u32[]{:S(2)}, u32[]{:S(2)}) collective-permute-start(bf16[8,128,128]{2,1,0:T(8,128)(2,1)S(1)} %get-tuple-element.46), channel_id=1, source_target_pairs={{0,1},{1,0},{2,3},{3,2},{4,5},{5,4},{6,7},{7,6},{8,9},{9,8},{10,11... | collective-permute-start | bytes 786440 | tf_op jit(solution)/shard_map/ppermute | solution.py:28
  58.8 1.1 collective-permute-done.10
  59.9 4.5 %collective-permute-done.13.refs_5_ = f32[8,128]{1,0:T(8,128)S(1)} collective-permute-done((f32[8,128]{1,0:T(8,128)S(1)}, f32[8,128]{1,0:T(8,128)S(1)}, u32[]{:S(2)}, u32[]{:S(2)}) %collective-permute-start.13) | collective-permute-done | bytes 4128 | tf_op jit(solution)/shard_map/ppermute | solution.py:39
  64.4 2.0 %collective-permute-start.12 = (f32[8,128]{1,0:T(8,128)S(1)}, f32[8,128]{1,0:T(8,128)S(1)}, u32[]{:S(2)}, u32[]{:S(2)}) collective-permute-start(f32[8,128]{1,0:T(8,128)S(1)} %add.40.refs_2_), channel_id=1, source_target_pairs={{0,4},{1,5},{2,6},{3,7},{4,0},{5,1},{6,2},{7,3},{8,12},{9,13},{10,... | collective-permute-start | bytes 12296 | tf_op jit(solution)/shard_map/ppermute | solution.py:39
  66.4 1.6 %collective-permute-done.12.refs_4_ = f32[8,128]{1,0:T(8,128)S(1)} collective-permute-done((f32[8,128]{1,0:T(8,128)S(1)}, f32[8,128]{1,0:T(8,128)S(1)}, u32[]{:S(2)}, u32[]{:S(2)}) %collective-permute-start.12) | collective-permute-done | bytes 4128 | tf_op jit(solution)/shard_map/ppermute | solution.py:39
  68.3 3.3 %collective-permute-done.11.refs_3_ = f32[8,128]{1,0:T(8,128)S(1)} collective-permute-done((f32[8,128]{1,0:T(8,128)S(1)}, f32[8,128]{1,0:T(8,128)S(1)}, u32[]{:S(2)}, u32[]{:S(2)}) %collective-permute-start.11) | collective-permute-done | bytes 4128 | tf_op jit(solution)/shard_map/ppermute | solution.py:39
  71.6 4.8 %shard_map.117 = (f32[8,128,128]{2,1,0:T(8,128)S(1)}, f32[8,128,128]{2,1,0:T(8,128)S(1)}, f32[8,128]{1,0:T(8,128)S(1)}) custom-call(s32[8,16]{1,0:T(8,128)S(1)} %fusion.3.src.refs_0_, s32[8]{0:T(128)} %refs_1_.7, f32[8,128]{1,0:T(8,128)S(1)} %add.40.refs_2_, f32[8,128]{1,0:T(8,128)S(1)} %collective-permute-done.11.refs_3_, ...), custom_call_target="tpu_custom_call" | custom-call | tf_op jit(solution)/shard_map/pallas_call | solution.py:326
  76.5 1.2 collective-permute-done.16
  77.6 1.4 %collective-permute-start.19 = (f32[8,128]{1,0:T(8,128)S(1)}, f32[8,128]{1,0:T(8,128)S(1)}, u32[]{:S(2)}, u32[]{:S(2)}) collective-permute-start(f32[8,128]{1,0:T(8,128)S(1)} %add.41.refs_0_), channel_id=1, source_target_pairs={{0,6},{1,7},{2,4},{3,5},{4,2},{5,3},{6,0},{7,1},{8,14},{9,15},{10,... | collective-permute-start | bytes 12296 | tf_op jit(solution)/shard_map/ppermute | solution.py:39
  79.0 0.6 collective-permute-start.18
  79.6 1.5 %collective-permute-start.17 = (f32[8,128]{1,0:T(8,128)S(1)}, f32[8,128]{1,0:T(8,128)S(1)}, u32[]{:S(2)}, u32[]{:S(2)}) collective-permute-start(f32[8,128]{1,0:T(8,128)S(1)} %add.41.refs_0_), channel_id=1, source_target_pairs={{0,2},{1,3},{2,0},{3,1},{4,6},{5,7},{6,4},{7,5},{8,10},{9,11},{10,... | collective-permute-start | bytes 12296 | tf_op jit(solution)/shard_map/ppermute | solution.py:39
  81.1 1.0 collective-permute-done.19.refs_3_
  82.7 0.6 collective-permute-done.17.refs_1_
  83.2 1.3 shard_map.118
  84.6 3.6 %collective-permute-start.20 = (bf16[8,128,128]{2,1,0:T(8,128)(2,1)S(1)}, bf16[8,128,128]{2,1,0:T(8,128)(2,1)S(1)}, u32[]{:S(2)}, u32[]{:S(2)}) collective-permute-start(bf16[8,128,128]{2,1,0:T(8,128)(2,1)S(1)} %get-tuple-element.51), channel_id=1, source_target_pairs={{0,8},{8,16},{16,24},{1,9},{9,17},{17,25},{2,10},{10,18},{18,26},{... | collective-permute-start | bytes 786440 | tf_op jit(solution)/shard_map/ppermute | solution.py:450
  88.3 3.3 %shard_map.119 = (f32[8,128,128]{2,1,0:T(8,128)S(1)}, bf16[8,2048,128]{2,1,0:T(8,128)(2,1)S(1)}) custom-call(s32[8,16]{1,0:T(8,128)S(1)} %fusion.3.src.refs_0_, s32[8]{0:T(128)} %refs_1_.7, bf16[8,128,128]{2,1,0:T(8,128)(2,1)S(1)} %get-tuple-element.71.even.refs_11_, bf16[8,128,128]{2,1,0:T(8,128)(2,1)S(1)} %get-tuple-element.69.odd.refs_12_, ...), custom_call_target="tpu_custom_call" | custom-call | tf_op jit(solution)/shard_map/pallas_call | solution.py:326
  91.6 1.3 collective-permute-done.20.handed
  92.9 6.4 %shard_map.120 = (f32[8,128,128]{2,1,0:T(8,128)S(1)}, bf16[8,128,128]{2,1,0:T(8,128)(2,1)S(1)}, f32[8,128]{1,0:T(8,128)S(1)}, bf16[8,16,128,128]{3,2,1,0:T(8,128)(2,1)S(1)}) custom-call(s32[8]{0:T(128)} %refs_1_.7, bf16[8,128,128]{2,1,0:T(8,128)(2,1)S(1)} %collective-permute-done.20.handed, bf16[8,16,128,128]{3,2,1,0:T(8,128)(2,1)S(1)} %bitcast.29, ...), custom_call_target="tpu_custom_call" | custom-call | tf_op jit(solution)/shard_map/pallas_call | solution.py:326
  99.3 0.7 collective-permute-start.28
  100.0 2.6 %collective-permute-start.27 = (bf16[8,128,128]{2,1,0:T(8,128)(2,1)S(1)}, bf16[8,128,128]{2,1,0:T(8,128)(2,1)S(1)}, u32[]{:S(2)}, u32[]{:S(2)}) collective-permute-start(bf16[8,128,128]{2,1,0:T(8,128)(2,1)S(1)} %get-tuple-element.58), channel_id=1, source_target_pairs={{0,1},{1,0},{2,3},{3,2},{4,5},{5,4},{6,7},{7,6},{8,9},{9,8},{10,11... | collective-permute-start | bytes 786440 | tf_op jit(solution)/shard_map/ppermute | solution.py:28
  102.6 1.1 collective-permute-done.23
  103.7 1.4 %collective-permute-start.26 = (f32[8,128]{1,0:T(8,128)S(1)}, f32[8,128]{1,0:T(8,128)S(1)}, u32[]{:S(2)}, u32[]{:S(2)}) collective-permute-start(f32[8,128]{1,0:T(8,128)S(1)} %add.42.refs_2_), channel_id=1, source_target_pairs={{0,6},{1,7},{2,4},{3,5},{4,2},{5,3},{6,0},{7,1},{8,14},{9,15},{10,... | collective-permute-start | bytes 12296 | tf_op jit(solution)/shard_map/ppermute | solution.py:39
  105.2 1.5 %collective-permute-start.25 = (f32[8,128]{1,0:T(8,128)S(1)}, f32[8,128]{1,0:T(8,128)S(1)}, u32[]{:S(2)}, u32[]{:S(2)}) collective-permute-start(f32[8,128]{1,0:T(8,128)S(1)} %add.42.refs_2_), channel_id=1, source_target_pairs={{0,4},{1,5},{2,6},{3,7},{4,0},{5,1},{6,2},{7,3},{8,12},{9,13},{10,... | collective-permute-start | bytes 12296 | tf_op jit(solution)/shard_map/ppermute | solution.py:39
  106.7 0.6 collective-permute-start.24
  107.2 1.0 collective-permute-done.26.refs_5_
  108.2 0.5 collective-permute-done.25.refs_4_
  108.8 1.5 %collective-permute-done.24.refs_3_ = f32[8,128]{1,0:T(8,128)S(1)} collective-permute-done((f32[8,128]{1,0:T(8,128)S(1)}, f32[8,128]{1,0:T(8,128)S(1)}, u32[]{:S(2)}, u32[]{:S(2)}) %collective-permute-start.24) | collective-permute-done | bytes 4128 | tf_op jit(solution)/shard_map/ppermute | solution.py:39
  110.3 4.5 %shard_map.121 = (f32[8,128,128]{2,1,0:T(8,128)S(1)}, f32[8,128,128]{2,1,0:T(8,128)S(1)}, bf16[8,128,128]{2,1,0:T(8,128)(2,1)S(1)}, f32[8,128]{1,0:T(8,128)S(1)}...) custom-call(s32[8,16]{1,0:T(8,128)S(1)} %fusion.3.src.refs_0_, s32[8]{0:T(128)} %refs_1_.7, ...), custom_call_target="tpu_custom_call" | custom-call | tf_op jit(solution)/shard_map/pallas_call | solution.py:326
  114.8 0.7 collective-permute-start.34
  115.4 2.0 %collective-permute-start.33 = (bf16[8,128,128]{2,1,0:T(8,128)(2,1)S(1)}, bf16[8,128,128]{2,1,0:T(8,128)(2,1)S(1)}, u32[]{:S(2)}, u32[]{:S(2)}) collective-permute-start(bf16[8,128,128]{2,1,0:T(8,128)(2,1)S(1)} %get-tuple-element.64), channel_id=1, source_target_pairs={{0,1},{1,0},{2,3},{3,2},{4,5},{5,4},{6,7},{7,6},{8,9},{9,8},{10,11... | collective-permute-start | bytes 786440 | tf_op jit(solution)/shard_map/ppermute | solution.py:28
  117.5 1.1 collective-permute-done.29
  118.6 1.7 %collective-permute-start.32 = (f32[8,128]{1,0:T(8,128)S(1)}, f32[8,128]{1,0:T(8,128)S(1)}, u32[]{:S(2)}, u32[]{:S(2)}) collective-permute-start(f32[8,128]{1,0:T(8,128)S(1)} %add.43.refs_2_), channel_id=1, source_target_pairs={{0,6},{1,7},{2,4},{3,5},{4,2},{5,3},{6,0},{7,1},{8,14},{9,15},{10,... | collective-permute-start | bytes 12296 | tf_op jit(solution)/shard_map/ppermute | solution.py:39
  120.3 1.5 %collective-permute-start.31 = (f32[8,128]{1,0:T(8,128)S(1)}, f32[8,128]{1,0:T(8,128)S(1)}, u32[]{:S(2)}, u32[]{:S(2)}) collective-permute-start(f32[8,128]{1,0:T(8,128)S(1)} %add.43.refs_2_), channel_id=1, source_target_pairs={{0,4},{1,5},{2,6},{3,7},{4,0},{5,1},{6,2},{7,3},{8,12},{9,13},{10,... | collective-permute-start | bytes 12296 | tf_op jit(solution)/shard_map/ppermute | solution.py:39
  122.1 1.0 collective-permute-done.32.refs_5_
  123.1 0.8 collective-permute-done.31.refs_4_
  123.9 1.5 %collective-permute-done.30.refs_3_ = f32[8,128]{1,0:T(8,128)S(1)} collective-permute-done((f32[8,128]{1,0:T(8,128)S(1)}, f32[8,128]{1,0:T(8,128)S(1)}, u32[]{:S(2)}, u32[]{:S(2)}) %collective-permute-start.30) | collective-permute-done | bytes 4128 | tf_op jit(solution)/shard_map/ppermute | solution.py:39
  125.4 4.6 %shard_map.122 = (f32[8,128,128]{2,1,0:T(8,128)S(1)}, f32[8,128,128]{2,1,0:T(8,128)S(1)}, f32[8,128]{1,0:T(8,128)S(1)}) custom-call(s32[8,16]{1,0:T(8,128)S(1)} %fusion.3.src.refs_0_, s32[8]{0:T(128)} %refs_1_.7, f32[8,128]{1,0:T(8,128)S(1)} %add.43.refs_2_, f32[8,128]{1,0:T(8,128)S(1)} %collective-permute-done.30.refs_3_, ...), custom_call_target="tpu_custom_call" | custom-call | tf_op jit(solution)/shard_map/pallas_call | solution.py:326
  130.0 1.2 collective-permute-done.35
  131.2 1.8 %collective-permute-start.38 = (f32[8,128]{1,0:T(8,128)S(1)}, f32[8,128]{1,0:T(8,128)S(1)}, u32[]{:S(2)}, u32[]{:S(2)}) collective-permute-start(f32[8,128]{1,0:T(8,128)S(1)} %add.44.refs_0_), channel_id=1, source_target_pairs={{0,6},{1,7},{2,4},{3,5},{4,2},{5,3},{6,0},{7,1},{8,14},{9,15},{10,... | collective-permute-start | bytes 12296 | tf_op jit(solution)/shard_map/ppermute | solution.py:39
  133.0 1.4 %collective-permute-start.37 = (f32[8,128]{1,0:T(8,128)S(1)}, f32[8,128]{1,0:T(8,128)S(1)}, u32[]{:S(2)}, u32[]{:S(2)}) collective-permute-start(f32[8,128]{1,0:T(8,128)S(1)} %add.44.refs_0_), channel_id=1, source_target_pairs={{0,4},{1,5},{2,6},{3,7},{4,0},{5,1},{6,2},{7,3},{8,12},{9,13},{10,... | collective-permute-start | bytes 12296 | tf_op jit(solution)/shard_map/ppermute | solution.py:39
  134.7 1.0 collective-permute-done.38.refs_3_
  135.7 0.9 collective-permute-done.37.refs_2_
  136.6 1.4 %collective-permute-done.36.refs_1_ = f32[8,128]{1,0:T(8,128)S(1)} collective-permute-done((f32[8,128]{1,0:T(8,128)S(1)}, f32[8,128]{1,0:T(8,128)S(1)}, u32[]{:S(2)}, u32[]{:S(2)}) %collective-permute-start.36) | collective-permute-done | bytes 4128 | tf_op jit(solution)/shard_map/ppermute | solution.py:39
  138.0 1.3 shard_map.123
  (48 shorter events, 2.0 us)
Async XLA Ops:
  2.4 11.6 %collective-permute-start.1 = (bf16[8,128,128]{2,1,0:T(8,128)(2,1)S(1)}, bf16[8,128,128]{2,1,0:T(8,128)(2,1)S(1)}, u32[]{:S(2)}, u32[]{:S(2)}) collective-permute-start(bf16[8,128,128]{2,1,0:T(8,128)(2,1)S(1)} %get-tuple-element.35.packed), channel_id=1, source_target_pairs={{1,2},{2,1},{3,4},{4,3},{5,6},{6,5},{9,10},{10,9},{11,12},{12,11},... | collective-permute-start | bytes 786440 | tf_op jit(solution)/shard_map/ppermute | solution.py:27
  3.1 11.0 %collective-permute-start = (bf16[8,128,128]{2,1,0:T(8,128)(2,1)S(1)}, bf16[8,128,128]{2,1,0:T(8,128)(2,1)S(1)}, u32[]{:S(2)}, u32[]{:S(2)}) collective-permute-start(bf16[8,128,128]{2,1,0:T(8,128)(2,1)S(1)} %get-tuple-element.35.packed), channel_id=1, source_target_pairs={{0,1},{1,0},{2,3},{3,2},{4,5},{5,4},{6,7},{7,6},{8,9},{9,8},{10,11... | collective-permute-start | bytes 786440 | tf_op jit(solution)/shard_map/ppermute | solution.py:28
  9.8 16.0 %collective-permute-start.9 = (bf16[8,128,128]{2,1,0:T(8,128)(2,1)S(1)}, bf16[8,128,128]{2,1,0:T(8,128)(2,1)S(1)}, u32[]{:S(2)}, u32[]{:S(2)}) collective-permute-start(bf16[8,128,128]{2,1,0:T(8,128)(2,1)S(1)} %get-tuple-element.40), channel_id=1, source_target_pairs={{1,2},{2,1},{3,4},{4,3},{5,6},{6,5},{9,10},{10,9},{11,12},{12,11},... | collective-permute-start | bytes 786440 | tf_op jit(solution)/shard_map/ppermute | solution.py:27
  10.5 20.2 %collective-permute-start.8 = (bf16[8,128,128]{2,1,0:T(8,128)(2,1)S(1)}, bf16[8,128,128]{2,1,0:T(8,128)(2,1)S(1)}, u32[]{:S(2)}, u32[]{:S(2)}) collective-permute-start(bf16[8,128,128]{2,1,0:T(8,128)(2,1)S(1)} %get-tuple-element.40), channel_id=1, source_target_pairs={{0,1},{1,0},{2,3},{3,2},{4,5},{5,4},{6,7},{7,6},{8,9},{9,8},{10,11... | collective-permute-start | bytes 786440 | tf_op jit(solution)/shard_map/ppermute | solution.py:28
  14.1 36.0 %copy-start = (bf16[1,8,16,128,128]{4,3,2,1,0:T(8,128)(2,1)S(1)}, bf16[1,8,16,128,128]{4,3,2,1,0:T(8,128)(2,1)}, u32[]{:S(2)}) copy-start(bf16[1,8,16,128,128]{4,3,2,1,0:T(8,128)(2,1)} %param.14) | copy-start | bytes 12582916
  14.1 36.0 %copy-start.1 = (bf16[1,8,16,128,128]{4,3,2,1,0:T(8,128)(2,1)S(1)}, bf16[1,8,16,128,128]{4,3,2,1,0:T(8,128)(2,1)}, u32[]{:S(2)}) copy-start(bf16[1,8,16,128,128]{4,3,2,1,0:T(8,128)(2,1)} %param.15) | copy-start | bytes 12582916
  14.1 36.0 %copy-start.3 = (f32[1,8,128,128]{3,2,1,0:T(8,128)S(1)}, f32[1,8,128,128]{3,2,1,0:T(8,128)}, u32[]{:S(2)}) copy-start(f32[1,8,128,128]{3,2,1,0:T(8,128)} %param.12) | copy-start | bytes 1572868
  20.4 29.7 %collective-permute-start.7 = (bf16[8,128,128]{2,1,0:T(8,128)(2,1)S(1)}, bf16[8,128,128]{2,1,0:T(8,128)(2,1)S(1)}, u32[]{:S(2)}, u32[]{:S(2)}) collective-permute-start(bf16[8,128,128]{2,1,0:T(8,128)(2,1)S(1)} %get-tuple-element.39), channel_id=1, source_target_pairs={{1,2},{2,1},{3,4},{4,3},{5,6},{6,5},{9,10},{10,9},{11,12},{12,11},... | collective-permute-start | bytes 786440 | tf_op jit(solution)/shard_map/ppermute | solution.py:27
  21.0 29.0 %collective-permute-start.6 = (bf16[8,128,128]{2,1,0:T(8,128)(2,1)S(1)}, bf16[8,128,128]{2,1,0:T(8,128)(2,1)S(1)}, u32[]{:S(2)}, u32[]{:S(2)}) collective-permute-start(bf16[8,128,128]{2,1,0:T(8,128)(2,1)S(1)} %get-tuple-element.39), channel_id=1, source_target_pairs={{0,1},{1,0},{2,3},{3,2},{4,5},{5,4},{6,7},{7,6},{8,9},{9,8},{10,11... | collective-permute-start | bytes 786440 | tf_op jit(solution)/shard_map/ppermute | solution.py:28
  24.0 1.2 collective-permute-start.2
  25.1 63.1 %collective-permute-start.22 = (bf16[16,128,128]{2,1,0:T(8,128)(2,1)S(1)}, bf16[16,128,128]{2,1,0:T(8,128)(2,1)S(1)}, u32[]{:S(2)}, u32[]{:S(2)}) collective-permute-start(bf16[16,128,128]{2,1,0:T(8,128)(2,1)S(1)} %get-tuple-element.52), channel_id=1, source_target_pairs={{1,2},{2,1},{3,4},{4,3},{5,6},{6,5},{9,10},{10,9},{11,12},{12,11},... | collective-permute-start | bytes 1572872 | tf_op jit(solution)/shard_map/ppermute | solution.py:27
  25.8 11.9 %collective-permute-start.5 = (f32[8,128]{1,0:T(8,128)S(1)}, f32[8,128]{1,0:T(8,128)S(1)}, u32[]{:S(2)}, u32[]{:S(2)}) collective-permute-start(f32[8,128]{1,0:T(8,128)S(1)} %add.39.refs_2_), channel_id=1, source_target_pairs={{0,6},{1,7},{2,4},{3,5},{4,2},{5,3},{6,0},{7,1},{8,14},{9,15},{10,... | collective-permute-start | bytes 12296 | tf_op jit(solution)/shard_map/ppermute | solution.py:39
  30.6 57.6 %collective-permute-start.21 = (bf16[16,128,128]{2,1,0:T(8,128)(2,1)S(1)}, bf16[16,128,128]{2,1,0:T(8,128)(2,1)S(1)}, u32[]{:S(2)}, u32[]{:S(2)}) collective-permute-start(bf16[16,128,128]{2,1,0:T(8,128)(2,1)S(1)} %get-tuple-element.52), channel_id=1, source_target_pairs={{0,1},{1,0},{2,3},{3,2},{4,5},{5,4},{6,7},{7,6},{8,9},{9,8},{10,11... | collective-permute-start | bytes 1572872 | tf_op jit(solution)/shard_map/ppermute | solution.py:28
  37.8 7.0 %collective-permute-start.4 = (f32[8,128]{1,0:T(8,128)S(1)}, f32[8,128]{1,0:T(8,128)S(1)}, u32[]{:S(2)}, u32[]{:S(2)}) collective-permute-start(f32[8,128]{1,0:T(8,128)S(1)} %add.39.refs_2_), channel_id=1, source_target_pairs={{0,4},{1,5},{2,6},{3,7},{4,0},{5,1},{6,2},{7,3},{8,12},{9,13},{10,... | collective-permute-start | bytes 12296 | tf_op jit(solution)/shard_map/ppermute | solution.py:39
  44.8 5.3 %collective-permute-start.3 = (f32[8,128]{1,0:T(8,128)S(1)}, f32[8,128]{1,0:T(8,128)S(1)}, u32[]{:S(2)}, u32[]{:S(2)}) collective-permute-start(f32[8,128]{1,0:T(8,128)S(1)} %add.39.refs_2_), channel_id=1, source_target_pairs={{0,2},{1,3},{2,0},{3,1},{4,6},{5,7},{6,4},{7,5},{8,10},{9,11},{10,... | collective-permute-start | bytes 12296 | tf_op jit(solution)/shard_map/ppermute | solution.py:39
  54.6 17.0 %collective-permute-start.15 = (bf16[8,128,128]{2,1,0:T(8,128)(2,1)S(1)}, bf16[8,128,128]{2,1,0:T(8,128)(2,1)S(1)}, u32[]{:S(2)}, u32[]{:S(2)}) collective-permute-start(bf16[8,128,128]{2,1,0:T(8,128)(2,1)S(1)} %get-tuple-element.46), channel_id=1, source_target_pairs={{1,2},{2,1},{3,4},{4,3},{5,6},{6,5},{9,10},{10,9},{11,12},{12,11},... | collective-permute-start | bytes 786440 | tf_op jit(solution)/shard_map/ppermute | solution.py:27
  55.3 16.3 %collective-permute-start.14 = (bf16[8,128,128]{2,1,0:T(8,128)(2,1)S(1)}, bf16[8,128,128]{2,1,0:T(8,128)(2,1)S(1)}, u32[]{:S(2)}, u32[]{:S(2)}) collective-permute-start(bf16[8,128,128]{2,1,0:T(8,128)(2,1)S(1)} %get-tuple-element.46), channel_id=1, source_target_pairs={{0,1},{1,0},{2,3},{3,2},{4,5},{5,4},{6,7},{7,6},{8,9},{9,8},{10,11... | collective-permute-start | bytes 786440 | tf_op jit(solution)/shard_map/ppermute | solution.py:28
  58.7 1.2 collective-permute-start.10
  59.9 4.5 %collective-permute-start.13 = (f32[8,128]{1,0:T(8,128)S(1)}, f32[8,128]{1,0:T(8,128)S(1)}, u32[]{:S(2)}, u32[]{:S(2)}) collective-permute-start(f32[8,128]{1,0:T(8,128)S(1)} %add.40.refs_2_), channel_id=1, source_target_pairs={{0,6},{1,7},{2,4},{3,5},{4,2},{5,3},{6,0},{7,1},{8,14},{9,15},{10,... | collective-permute-start | bytes 12296 | tf_op jit(solution)/shard_map/ppermute | solution.py:39
  64.4 3.6 %collective-permute-start.12 = (f32[8,128]{1,0:T(8,128)S(1)}, f32[8,128]{1,0:T(8,128)S(1)}, u32[]{:S(2)}, u32[]{:S(2)}) collective-permute-start(f32[8,128]{1,0:T(8,128)S(1)} %add.40.refs_2_), channel_id=1, source_target_pairs={{0,4},{1,5},{2,6},{3,7},{4,0},{5,1},{6,2},{7,3},{8,12},{9,13},{10,... | collective-permute-start | bytes 12296 | tf_op jit(solution)/shard_map/ppermute | solution.py:39
  68.0 3.6 %collective-permute-start.11 = (f32[8,128]{1,0:T(8,128)S(1)}, f32[8,128]{1,0:T(8,128)S(1)}, u32[]{:S(2)}, u32[]{:S(2)}) collective-permute-start(f32[8,128]{1,0:T(8,128)S(1)} %add.40.refs_2_), channel_id=1, source_target_pairs={{0,2},{1,3},{2,0},{3,1},{4,6},{5,7},{6,4},{7,5},{8,10},{9,11},{10,... | collective-permute-start | bytes 12296 | tf_op jit(solution)/shard_map/ppermute | solution.py:39
  71.6 16.7 %copy-start.2 = (bf16[1,8,16,128,128]{4,3,2,1,0:T(8,128)(2,1)S(1)}, bf16[1,8,16,128,128]{4,3,2,1,0:T(8,128)(2,1)}, u32[]{:S(2)}) copy-start(bf16[1,8,16,128,128]{4,3,2,1,0:T(8,128)(2,1)} %param.17) | copy-start | bytes 12582916
  71.6 16.7 %copy-start.6 = (f32[1,8,128,128]{3,2,1,0:T(8,128)S(1)}, f32[1,8,128,128]{3,2,1,0:T(8,128)}, u32[]{:S(2)}) copy-start(f32[1,8,128,128]{3,2,1,0:T(8,128)} %param.11) | copy-start | bytes 1572868
  76.4 1.2 collective-permute-start.16
  77.6 4.5 %collective-permute-start.19 = (f32[8,128]{1,0:T(8,128)S(1)}, f32[8,128]{1,0:T(8,128)S(1)}, u32[]{:S(2)}, u32[]{:S(2)}) collective-permute-start(f32[8,128]{1,0:T(8,128)S(1)} %add.41.refs_0_), channel_id=1, source_target_pairs={{0,6},{1,7},{2,4},{3,5},{4,2},{5,3},{6,0},{7,1},{8,14},{9,15},{10,... | collective-permute-start | bytes 12296 | tf_op jit(solution)/shard_map/ppermute | solution.py:39
  79.0 3.6 %collective-permute-start.18 = (f32[8,128]{1,0:T(8,128)S(1)}, f32[8,128]{1,0:T(8,128)S(1)}, u32[]{:S(2)}, u32[]{:S(2)}) collective-permute-start(f32[8,128]{1,0:T(8,128)S(1)} %add.41.refs_0_), channel_id=1, source_target_pairs={{0,4},{1,5},{2,6},{3,7},{4,0},{5,1},{6,2},{7,3},{8,12},{9,13},{10,... | collective-permute-start | bytes 12296 | tf_op jit(solution)/shard_map/ppermute | solution.py:39
  79.6 3.6 %collective-permute-start.17 = (f32[8,128]{1,0:T(8,128)S(1)}, f32[8,128]{1,0:T(8,128)S(1)}, u32[]{:S(2)}, u32[]{:S(2)}) collective-permute-start(f32[8,128]{1,0:T(8,128)S(1)} %add.41.refs_0_), channel_id=1, source_target_pairs={{0,2},{1,3},{2,0},{3,1},{4,6},{5,7},{6,4},{7,5},{8,10},{9,11},{10,... | collective-permute-start | bytes 12296 | tf_op jit(solution)/shard_map/ppermute | solution.py:39
  83.2 9.7 %copy-start.4 = (f32[1,8,128,128]{3,2,1,0:T(8,128)S(1)}, f32[1,8,128,128]{3,2,1,0:T(8,128)}, u32[]{:S(2)}) copy-start(f32[1,8,128,128]{3,2,1,0:T(8,128)} %param.13) | copy-start | bytes 1572868
  83.2 9.7 %copy-start.5 = (bf16[1,8,16,128,128]{4,3,2,1,0:T(8,128)(2,1)S(1)}, bf16[1,8,16,128,128]{4,3,2,1,0:T(8,128)(2,1)}, u32[]{:S(2)}) copy-start(bf16[1,8,16,128,128]{4,3,2,1,0:T(8,128)(2,1)} %param.16) | copy-start | bytes 12582916
  84.6 8.3 %collective-permute-start.20 = (bf16[8,128,128]{2,1,0:T(8,128)(2,1)S(1)}, bf16[8,128,128]{2,1,0:T(8,128)(2,1)S(1)}, u32[]{:S(2)}, u32[]{:S(2)}) collective-permute-start(bf16[8,128,128]{2,1,0:T(8,128)(2,1)S(1)} %get-tuple-element.51), channel_id=1, source_target_pairs={{0,8},{8,16},{16,24},{1,9},{9,17},{17,25},{2,10},{10,18},{18,26},{... | collective-permute-start | bytes 786440 | tf_op jit(solution)/shard_map/ppermute | solution.py:450
  99.3 11.0 %collective-permute-start.28 = (bf16[8,128,128]{2,1,0:T(8,128)(2,1)S(1)}, bf16[8,128,128]{2,1,0:T(8,128)(2,1)S(1)}, u32[]{:S(2)}, u32[]{:S(2)}) collective-permute-start(bf16[8,128,128]{2,1,0:T(8,128)(2,1)S(1)} %get-tuple-element.58), channel_id=1, source_target_pairs={{1,2},{2,1},{3,4},{4,3},{5,6},{6,5},{9,10},{10,9},{11,12},{12,11},... | collective-permute-start | bytes 786440 | tf_op jit(solution)/shard_map/ppermute | solution.py:27
  100.0 10.3 %collective-permute-start.27 = (bf16[8,128,128]{2,1,0:T(8,128)(2,1)S(1)}, bf16[8,128,128]{2,1,0:T(8,128)(2,1)S(1)}, u32[]{:S(2)}, u32[]{:S(2)}) collective-permute-start(bf16[8,128,128]{2,1,0:T(8,128)(2,1)S(1)} %get-tuple-element.58), channel_id=1, source_target_pairs={{0,1},{1,0},{2,3},{3,2},{4,5},{5,4},{6,7},{7,6},{8,9},{9,8},{10,11... | collective-permute-start | bytes 786440 | tf_op jit(solution)/shard_map/ppermute | solution.py:28
  102.6 1.2 collective-permute-start.23
  103.7 4.5 %collective-permute-start.26 = (f32[8,128]{1,0:T(8,128)S(1)}, f32[8,128]{1,0:T(8,128)S(1)}, u32[]{:S(2)}, u32[]{:S(2)}) collective-permute-start(f32[8,128]{1,0:T(8,128)S(1)} %add.42.refs_2_), channel_id=1, source_target_pairs={{0,6},{1,7},{2,4},{3,5},{4,2},{5,3},{6,0},{7,1},{8,14},{9,15},{10,... | collective-permute-start | bytes 12296 | tf_op jit(solution)/shard_map/ppermute | solution.py:39
  105.2 3.6 %collective-permute-start.25 = (f32[8,128]{1,0:T(8,128)S(1)}, f32[8,128]{1,0:T(8,128)S(1)}, u32[]{:S(2)}, u32[]{:S(2)}) collective-permute-start(f32[8,128]{1,0:T(8,128)S(1)} %add.42.refs_2_), channel_id=1, source_target_pairs={{0,4},{1,5},{2,6},{3,7},{4,0},{5,1},{6,2},{7,3},{8,12},{9,13},{10,... | collective-permute-start | bytes 12296 | tf_op jit(solution)/shard_map/ppermute | solution.py:39
  106.7 3.6 %collective-permute-start.24 = (f32[8,128]{1,0:T(8,128)S(1)}, f32[8,128]{1,0:T(8,128)S(1)}, u32[]{:S(2)}, u32[]{:S(2)}) collective-permute-start(f32[8,128]{1,0:T(8,128)S(1)} %add.42.refs_2_), channel_id=1, source_target_pairs={{0,2},{1,3},{2,0},{3,1},{4,6},{5,7},{6,4},{7,5},{8,10},{9,11},{10,... | collective-permute-start | bytes 12296 | tf_op jit(solution)/shard_map/ppermute | solution.py:39
  114.8 10.6 %collective-permute-start.34 = (bf16[8,128,128]{2,1,0:T(8,128)(2,1)S(1)}, bf16[8,128,128]{2,1,0:T(8,128)(2,1)S(1)}, u32[]{:S(2)}, u32[]{:S(2)}) collective-permute-start(bf16[8,128,128]{2,1,0:T(8,128)(2,1)S(1)} %get-tuple-element.64), channel_id=1, source_target_pairs={{1,2},{2,1},{3,4},{4,3},{5,6},{6,5},{9,10},{10,9},{11,12},{12,11},... | collective-permute-start | bytes 786440 | tf_op jit(solution)/shard_map/ppermute | solution.py:27
  115.4 9.9 %collective-permute-start.33 = (bf16[8,128,128]{2,1,0:T(8,128)(2,1)S(1)}, bf16[8,128,128]{2,1,0:T(8,128)(2,1)S(1)}, u32[]{:S(2)}, u32[]{:S(2)}) collective-permute-start(bf16[8,128,128]{2,1,0:T(8,128)(2,1)S(1)} %get-tuple-element.64), channel_id=1, source_target_pairs={{0,1},{1,0},{2,3},{3,2},{4,5},{5,4},{6,7},{7,6},{8,9},{9,8},{10,11... | collective-permute-start | bytes 786440 | tf_op jit(solution)/shard_map/ppermute | solution.py:28
  117.4 1.2 collective-permute-start.29
  118.6 4.5 %collective-permute-start.32 = (f32[8,128]{1,0:T(8,128)S(1)}, f32[8,128]{1,0:T(8,128)S(1)}, u32[]{:S(2)}, u32[]{:S(2)}) collective-permute-start(f32[8,128]{1,0:T(8,128)S(1)} %add.43.refs_2_), channel_id=1, source_target_pairs={{0,6},{1,7},{2,4},{3,5},{4,2},{5,3},{6,0},{7,1},{8,14},{9,15},{10,... | collective-permute-start | bytes 12296 | tf_op jit(solution)/shard_map/ppermute | solution.py:39
  120.3 3.6 %collective-permute-start.31 = (f32[8,128]{1,0:T(8,128)S(1)}, f32[8,128]{1,0:T(8,128)S(1)}, u32[]{:S(2)}, u32[]{:S(2)}) collective-permute-start(f32[8,128]{1,0:T(8,128)S(1)} %add.43.refs_2_), channel_id=1, source_target_pairs={{0,4},{1,5},{2,6},{3,7},{4,0},{5,1},{6,2},{7,3},{8,12},{9,13},{10,... | collective-permute-start | bytes 12296 | tf_op jit(solution)/shard_map/ppermute | solution.py:39
  121.8 3.6 %collective-permute-start.30 = (f32[8,128]{1,0:T(8,128)S(1)}, f32[8,128]{1,0:T(8,128)S(1)}, u32[]{:S(2)}, u32[]{:S(2)}) collective-permute-start(f32[8,128]{1,0:T(8,128)S(1)} %add.43.refs_2_), channel_id=1, source_target_pairs={{0,2},{1,3},{2,0},{3,1},{4,6},{5,7},{6,4},{7,5},{8,10},{9,11},{10,... | collective-permute-start | bytes 12296 | tf_op jit(solution)/shard_map/ppermute | solution.py:39
  130.0 1.2 collective-permute-start.35
  131.2 4.5 %collective-permute-start.38 = (f32[8,128]{1,0:T(8,128)S(1)}, f32[8,128]{1,0:T(8,128)S(1)}, u32[]{:S(2)}, u32[]{:S(2)}) collective-permute-start(f32[8,128]{1,0:T(8,128)S(1)} %add.44.refs_0_), channel_id=1, source_target_pairs={{0,6},{1,7},{2,4},{3,5},{4,2},{5,3},{6,0},{7,1},{8,14},{9,15},{10,... | collective-permute-start | bytes 12296 | tf_op jit(solution)/shard_map/ppermute | solution.py:39
  133.0 3.6 %collective-permute-start.37 = (f32[8,128]{1,0:T(8,128)S(1)}, f32[8,128]{1,0:T(8,128)S(1)}, u32[]{:S(2)}, u32[]{:S(2)}) collective-permute-start(f32[8,128]{1,0:T(8,128)S(1)} %add.44.refs_0_), channel_id=1, source_target_pairs={{0,4},{1,5},{2,6},{3,7},{4,0},{5,1},{6,2},{7,3},{8,12},{9,13},{10,... | collective-permute-start | bytes 12296 | tf_op jit(solution)/shard_map/ppermute | solution.py:39
  134.4 3.6 %collective-permute-start.36 = (f32[8,128]{1,0:T(8,128)S(1)}, f32[8,128]{1,0:T(8,128)S(1)}, u32[]{:S(2)}, u32[]{:S(2)}) collective-permute-start(f32[8,128]{1,0:T(8,128)S(1)} %add.44.refs_0_), channel_id=1, source_target_pairs={{0,2},{1,3},{2,0},{3,1},{4,6},{5,7},{6,4},{7,5},{8,10},{9,11},{10,... | collective-permute-start | bytes 12296 | tf_op jit(solution)/shard_map/ppermute | solution.py:39
where the time goes:
time: 140 us; the launch traced here: 139 us
  starting transfers between devices  57.1 us (41%)
  Pallas kernels  41 us (29%)
  waiting for transfers between devices  39.4 us (28%)
    pallas_call x11, Pallas kernels, call(): pl.pallas_call(kernel, out_shape=outs, in_specs=[SMEM] * len(scalars) + [...  41 us
    ppermute x18, waiting for transfers between devices, gathered_parts(): parts += [lax.ppermute(pair, 'sec', [(i, i ^ 2 * m) for i in range(count)])]  31.5 us
    ppermute x18, starting transfers between devices, gathered_parts(): parts += [lax.ppermute(pair, 'sec', [(i, i ^ 2 * m) for i in range(count)])]  30.2 us
    ppermute x7, starting transfers between devices, swapped(): even = lax.ppermute(block, 'sec', even_pairs(count))  18.2 us
    ppermute x6, waiting for transfers between devices, gathered_parts(): pair = partial + lax.ppermute(partial, 'sec', even_pairs(count))  6.66 us
    ppermute x7, starting transfers between devices, swapped(): odd = lax.ppermute(block, 'sec', odd_pairs(count))  4.75 us
    ppermute x1, starting transfers between devices, both_updates(): handed = lax.ppermute(handed, 'seg', [(s, s + 1) for s in range(segs - 1)])  3.62 us
  transfers between devices with their start and end apart: 39, of which 25 were waited for; matrix products, arithmetic and copies ran while one was open for 1% of the time, Pallas kernels for 16%

commit v1 on v0

--- a/solution.py
+++ b/solution.py
@@ -38,6 +38,10 @@
     for m in range(1, count // 2):
         parts += [lax.ppermute(pair, "sec", [(i, i ^ (2 * m)) for i in range(count)])]
     return parts
+
+
+def after(value, *others):
+    return lax.optimization_barrier((value, *others))[0]
 
 
 def live_of(dim, width):
@@ -246,28 +250,21 @@
     scale = 1.0 / jnp.sqrt(sums[0] / entries + eps)
     grow = (1.0 + quotient) * scale
 
-    def others(w, before, t, after, at):
-        def body(b, carry):
-            value = w[b].astype(F32) * (
-                grow * before[b].astype(F32) - scale * t[b].astype(F32)
-            )
-            if not last:
-                after[b] = value
-            x[at + b] = value.astype(BF16)
-            return carry
-
-        lax.fori_loop(0, blocks, body, 0)
-
-    others(w_even, u_even, t_even, None if last else un_even, 0)
-    others(w_odd, u_odd, t_odd, None if last else un_odd, 2 * blocks)
-
-    def own(b, carry):
+    def neighbour(b, w, before, t, kept_at, at):
+        value = w[b].astype(F32) * (grow * before[b].astype(F32) - scale * t[b].astype(F32))
+        if kept_at is not None:
+            kept_at[b] = value
+        x[at + b] = value.astype(BF16)
+
+    def move(b, carry):
+        neighbour(b, w_even, u_even, t_even, None if last else un_even, 0)
+        neighbour(b, w_odd, u_odd, t_odd, None if last else un_odd, 2 * blocks)
         value = (grow * u[b] - scale * term[b]) / (onsite[b] + 1.0)
         un[b] = value
         x[blocks + b] = value.astype(BF16)
         return carry
 
-    lax.fori_loop(0, blocks, own, 0)
+    lax.fori_loop(0, blocks, move, 0, unroll=2 if blocks % 2 == 0 else 1)
     acc[...] = jnp.zeros_like(acc)
 
     def emit(b, value):
@@ -298,7 +295,7 @@
 
 def final_kernel(n_parts, entries, *refs):
     parts, rest = refs[:n_parts], refs[n_parts:]
-    u, term, onsite, *outs = rest
+    u, term, onsite, out, *held = rest
     sums = totals(parts)
     quotient = sums[1] / sums[0]
     scale = 1.0 / jnp.sqrt(sums[0] / entries + EPS)
@@ -306,15 +303,25 @@
     length = sums[2] + 2.0 * delta * sums[3] + delta * delta * sums[4]
     scale = scale / jnp.sqrt(length * scale * scale / entries + EPS)
     grow = (1.0 + quotient) * scale
-
-    def body(b, carry):
-        value = (grow * u[b] - scale * term[b]) / (onsite[b] + 1.0)
-        outs[0][b] = value
-        if len(outs) > 1:
-            outs[1][b] = value.astype(BF16)
-        return carry
-
-    lax.fori_loop(0, u.shape[0], body, 0)
+    blocks = u.shape[0]
+    lanes = 2 if blocks % 2 == 0 else 1
+
+    def copy_of(i):
+        part = pl.ds(i * lanes, lanes)
+        return pltpu.make_async_copy(held[0].at[part], out.at[part], held[1].at[i])
+
+    for i in range(blocks // lanes):
+        for b in range(i * lanes, (i + 1) * lanes):
+            value = (grow * u[b] - scale * term[b]) / (onsite[b] + 1.0)
+            if held:
+                held[0][b] = value
+            else:
+                out[b] = value.astype(out.dtype)
+        if held:
+            copy_of(i).start()
+    if held:
+        for i in range(blocks // lanes):
+            copy_of(i).wait()
 
 
 VMEM = pl.BlockSpec(memory_space=pltpu.VMEM)
@@ -322,12 +329,12 @@
 HBM = pl.BlockSpec(memory_space=pltpu.HBM)
 
 
-def call(kernel, scalars, arrays, outs, scratch, far=()):
+def call(kernel, scalars, arrays, outs, scratch, far=(), out_spec=None):
     return pl.pallas_call(
         kernel,
         out_shape=outs,
         in_specs=[SMEM] * len(scalars) + [VMEM] * len(arrays) + [HBM] * len(far),
-        out_specs=[VMEM] * len(outs),
+        out_specs=[out_spec or VMEM] * len(outs),
         scratch_shapes=scratch,
         compiler_params=pltpu.CompilerParams(vmem_limit_bytes=16 << 20),
     )(*scalars, *arrays, *[pltpu.with_memory_space_constraint(a, pltpu.HBM) for a in far])
@@ -392,14 +399,17 @@
         return out if bundle is None else (*out, arrived)
 
     def final(u, term, parts, onsite, narrow):
-        outs = [like(vec, F32)] + ([like(vec, BF16)] if narrow else [])
-        return call(
+        held = [] if narrow else [pltpu.VMEM(vec, F32), pltpu.SemaphoreType.DMA((blocks,))]
+        (out,) = call(
             functools.partial(final_kernel, len(parts), entries),
             [],
             [*parts, u, term, onsite],
-            outs,
-            [],
+            [like(vec, BF16 if narrow else F32)],
+            held,
+            (),
+            VMEM if narrow else HBM,
         )
+        return out
 
     u, packed = call(
         prepare_kernel,
@@ -445,7 +455,8 @@
     u, term, parts, second = later_steps(
         u, term, sent, stats, onsite, left, right, halo_first, w_first, bundle
     )
-    result_first, handed = final(u, term, parts, onsite, True)
+    handed = final(u, term, parts, onsite, True)
+    ended = (u, term, parts, onsite)
     segs = lax.axis_size("seg")
     handed = lax.ppermute(handed, "seg", [(s, s + 1) for s in range(segs - 1)])
 
@@ -463,12 +474,14 @@
         [block_dims],
         [handed, left_base, y, u, onsite_second],
         [like(vec, F32), like(vec, BF16), stats_shape, like(left_base.shape, BF16)],
-        [acc_shape] + [pltpu.VMEM((terms * width, width), BF16)] * pairs,
-    )
+        [acc_shape] + [pltpu.VMEM((terms * width, width), BF16)] * lanes,
+    )
+    u_first, term_first, parts_first, onsite = ended
+    result_first = final(after(u_first, stats), term_first, parts_first, onsite, False)
     u, term, parts = later_steps(
         u, term, sent, stats, onsite_second, left_second, right_second, halo_second, w_second
     )
-    (result_second,) = final(u, term, parts, onsite_second, False)
+    result_second = final(u, term, parts, onsite_second, False)
     return result_first[None], result_second[None]
 
 

time: 140 us -> 138 us (0.986)
  Pallas kernels: 41 us -> 39.5 us
    pallas_call x11 -> x12, Pallas kernels: 41 us -> 39.5 us  [call(): pl.pallas_call(kernel, out_shape=outs, in_specs=[SMEM] * len(scalars) + [...]
  transfers between devices with their start and end apart: 39 -> 39, of which waited for: 25 -> 24; matrix products, arithmetic and copies ran while one was open for 1% -> 1% of each run, Pallas kernels for 16% -> 16%
where the time goes in v1:
time: 138 us; the launch traced here: 137 us
  starting transfers between devices  57.4 us (42%)
  Pallas kernels  39.5 us (29%)
  waiting for transfers between devices  38.2 us (28%)
    pallas_call x12, Pallas kernels, call(): pl.pallas_call(kernel, out_shape=outs, in_specs=[SMEM] * len(scalars) + [...  39.5 us
    ppermute x18, waiting for transfers between devices, gathered_parts(): parts += [lax.ppermute(pair, 'sec', [(i, i ^ 2 * m) for i in range(count)])]  30.2 us
    ppermute x18, starting transfers between devices, gathered_parts(): parts += [lax.ppermute(pair, 'sec', [(i, i ^ 2 * m) for i in range(count)])]  30.2 us
    ppermute x7, starting transfers between devices, swapped(): even = lax.ppermute(block, 'sec', even_pairs(count))  18.2 us
    ppermute x6, waiting for transfers between devices, gathered_parts(): pair = partial + lax.ppermute(partial, 'sec', even_pairs(count))  6.66 us
    ppermute x7, starting transfers between devices, swapped(): odd = lax.ppermute(block, 'sec', odd_pairs(count))  4.93 us
    ppermute x1, starting transfers between devices, both_updates(): handed = lax.ppermute(handed, 'seg', [(s, s + 1) for s in range(segs - 1)])  3.76 us
  transfers between devices with their start and end apart: 39, of which 24 were waited for; matrix products, arithmetic and copies ran while one was open for 1% of the time, Pallas kernels for 16%

profile of v1, /device:TPU:0, one launch (start us, length us, event | category | flops | bytes accessed | tf_op | source)
XLA Modules:
  0.0 137.1 jit_solution(12873523206391144762)
XLA Ops:
  0.6 1.8 %shard_map.113 = (f32[8,128,128]{2,1,0:T(8,128)S(1)}, bf16[8,128,128]{2,1,0:T(8,128)(2,1)S(1)}) custom-call(s32[8]{0:T(128)} %refs_1_.7, f32[8,128,128]{2,1,0:T(8,128)} %bitcast.33), custom_call_target="tpu_custom_call" | custom-call | tf_op jit(solution)/shard_map/pallas_call | solution.py:333
  2.4 0.7 collective-permute-start.1
  3.1 4.4 %collective-permute-start = (bf16[8,128,128]{2,1,0:T(8,128)(2,1)S(1)}, bf16[8,128,128]{2,1,0:T(8,128)(2,1)S(1)}, u32[]{:S(2)}, u32[]{:S(2)}) collective-permute-start(bf16[8,128,128]{2,1,0:T(8,128)(2,1)S(1)} %get-tuple-element.34.packed), channel_id=1, source_target_pairs={{0,1},{1,0},{2,3},{3,2},{4,5},{5,4},{6,7},{7,6},{8,9},{9,8},{10,11... | collective-permute-start | bytes 786440 | tf_op jit(solution)/shard_map/ppermute | solution.py:28
  7.5 2.3 %shard_map.115 = (bf16[8,128,128]{2,1,0:T(8,128)(2,1)S(1)}, bf16[16,128,128]{2,1,0:T(8,128)(2,1)S(1)}) custom-call(s32[8]{0:T(128)} %refs_1_.7, bf16[8,128,128]{2,1,0:T(8,128)(2,1)S(1)} %get-tuple-element.34.packed, f32[8,128,128]{2,1,0:T(8,128)} %bitcast.19, f32[8,128,128]{2,1,0:T(8,128)} %bitcast.25, f32[8,128,128]{2,1,0:T(8,128)} %bitcast.31), custom_call_target="tpu_custom_call" | custom-call | tf_op jit(solution)/shard_map/pallas_call | solution.py:333
  9.8 0.7 collective-permute-start.9
  10.5 2.9 %collective-permute-start.8 = (bf16[8,128,128]{2,1,0:T(8,128)(2,1)S(1)}, bf16[8,128,128]{2,1,0:T(8,128)(2,1)S(1)}, u32[]{:S(2)}, u32[]{:S(2)}) collective-permute-start(bf16[8,128,128]{2,1,0:T(8,128)(2,1)S(1)} %get-tuple-element.39), channel_id=1, source_target_pairs={{0,1},{1,0},{2,3},{3,2},{4,5},{5,4},{6,7},{7,6},{8,9},{9,8},{10,11... | collective-permute-start | bytes 786440 | tf_op jit(solution)/shard_map/ppermute | solution.py:28
  13.4 0.7 fusion.3.src.refs_0_
  14.1 6.2 %shard_map.114 = (f32[8,128,128]{2,1,0:T(8,128)S(1)}, bf16[8,128,128]{2,1,0:T(8,128)(2,1)S(1)}, f32[8,128]{1,0:T(8,128)S(1)}) custom-call(s32[8,16]{1,0:T(8,128)S(1)} %fusion.3.src.refs_0_, s32[8]{0:T(128)} %refs_1_.7, bf16[8,128,128]{2,1,0:T(8,128)(2,1)S(1)} %collective-permute-done.even.refs_11_, ...), custom_call_target="tpu_custom_call" | custom-call | tf_op jit(solution)/shard_map/pallas_call | solution.py:333
  20.4 0.7 collective-permute-start.7
  21.0 2.9 %collective-permute-start.6 = (bf16[8,128,128]{2,1,0:T(8,128)(2,1)S(1)}, bf16[8,128,128]{2,1,0:T(8,128)(2,1)S(1)}, u32[]{:S(2)}, u32[]{:S(2)}) collective-permute-start(bf16[8,128,128]{2,1,0:T(8,128)(2,1)S(1)} %get-tuple-element.38), channel_id=1, source_target_pairs={{0,1},{1,0},{2,3},{3,2},{4,5},{5,4},{6,7},{7,6},{8,9},{9,8},{10,11... | collective-permute-start | bytes 786440 | tf_op jit(solution)/shard_map/ppermute | solution.py:28
  24.0 1.1 collective-permute-done.2
  25.1 0.7 collective-permute-start.22
  25.8 4.8 %collective-permute-start.5 = (f32[8,128]{1,0:T(8,128)S(1)}, f32[8,128]{1,0:T(8,128)S(1)}, u32[]{:S(2)}, u32[]{:S(2)}) collective-permute-start(f32[8,128]{1,0:T(8,128)S(1)} %add.39.refs_2_), channel_id=1, source_target_pairs={{0,6},{1,7},{2,4},{3,5},{4,2},{5,3},{6,0},{7,1},{8,14},{9,15},{10,... | collective-permute-start | bytes 12296 | tf_op jit(solution)/shard_map/ppermute | solution.py:39
  30.6 7.1 %collective-permute-done.5.refs_5_ = f32[8,128]{1,0:T(8,128)S(1)} collective-permute-done((f32[8,128]{1,0:T(8,128)S(1)}, f32[8,128]{1,0:T(8,128)S(1)}, u32[]{:S(2)}, u32[]{:S(2)}) %collective-permute-start.5) | collective-permute-done | bytes 4128 | tf_op jit(solution)/shard_map/ppermute | solution.py:39
  37.8 5.4 %collective-permute-start.4 = (f32[8,128]{1,0:T(8,128)S(1)}, f32[8,128]{1,0:T(8,128)S(1)}, u32[]{:S(2)}, u32[]{:S(2)}) collective-permute-start(f32[8,128]{1,0:T(8,128)S(1)} %add.39.refs_2_), channel_id=1, source_target_pairs={{0,4},{1,5},{2,6},{3,7},{4,0},{5,1},{6,2},{7,3},{8,12},{9,13},{10,... | collective-permute-start | bytes 12296 | tf_op jit(solution)/shard_map/ppermute | solution.py:39
  43.2 1.6 %collective-permute-done.4.refs_4_ = f32[8,128]{1,0:T(8,128)S(1)} collective-permute-done((f32[8,128]{1,0:T(8,128)S(1)}, f32[8,128]{1,0:T(8,128)S(1)}, u32[]{:S(2)}, u32[]{:S(2)}) %collective-permute-start.4) | collective-permute-done | bytes 4128 | tf_op jit(solution)/shard_map/ppermute | solution.py:39
  44.8 3.8 %collective-permute-start.3 = (f32[8,128]{1,0:T(8,128)S(1)}, f32[8,128]{1,0:T(8,128)S(1)}, u32[]{:S(2)}, u32[]{:S(2)}) collective-permute-start(f32[8,128]{1,0:T(8,128)S(1)} %add.39.refs_2_), channel_id=1, source_target_pairs={{0,2},{1,3},{2,0},{3,1},{4,6},{5,7},{6,4},{7,5},{8,10},{9,11},{10,... | collective-permute-start | bytes 12296 | tf_op jit(solution)/shard_map/ppermute | solution.py:39
  48.5 1.6 %collective-permute-done.3.refs_3_ = f32[8,128]{1,0:T(8,128)S(1)} collective-permute-done((f32[8,128]{1,0:T(8,128)S(1)}, f32[8,128]{1,0:T(8,128)S(1)}, u32[]{:S(2)}, u32[]{:S(2)}) %collective-permute-start.3) | collective-permute-done | bytes 4128 | tf_op jit(solution)/shard_map/ppermute | solution.py:39
  50.1 4.3 %shard_map.116 = (f32[8,128,128]{2,1,0:T(8,128)S(1)}, f32[8,128,128]{2,1,0:T(8,128)S(1)}, bf16[8,128,128]{2,1,0:T(8,128)(2,1)S(1)}, f32[8,128]{1,0:T(8,128)S(1)}...) custom-call(s32[8,16]{1,0:T(8,128)S(1)} %fusion.3.src.refs_0_, s32[8]{0:T(128)} %refs_1_.7, ...), custom_call_target="tpu_custom_call" | custom-call | tf_op jit(solution)/shard_map/pallas_call | solution.py:333
  54.4 0.7 collective-permute-start.15
  55.1 3.4 %collective-permute-start.14 = (bf16[8,128,128]{2,1,0:T(8,128)(2,1)S(1)}, bf16[8,128,128]{2,1,0:T(8,128)(2,1)S(1)}, u32[]{:S(2)}, u32[]{:S(2)}) collective-permute-start(bf16[8,128,128]{2,1,0:T(8,128)(2,1)S(1)} %get-tuple-element.45), channel_id=1, source_target_pairs={{0,1},{1,0},{2,3},{3,2},{4,5},{5,4},{6,7},{7,6},{8,9},{9,8},{10,11... | collective-permute-start | bytes 786440 | tf_op jit(solution)/shard_map/ppermute | solution.py:28
  58.6 1.1 collective-permute-done.10
  59.7 4.5 %collective-permute-done.13.refs_5_ = f32[8,128]{1,0:T(8,128)S(1)} collective-permute-done((f32[8,128]{1,0:T(8,128)S(1)}, f32[8,128]{1,0:T(8,128)S(1)}, u32[]{:S(2)}, u32[]{:S(2)}) %collective-permute-start.13) | collective-permute-done | bytes 4128 | tf_op jit(solution)/shard_map/ppermute | solution.py:39
  64.2 2.0 %collective-permute-start.12 = (f32[8,128]{1,0:T(8,128)S(1)}, f32[8,128]{1,0:T(8,128)S(1)}, u32[]{:S(2)}, u32[]{:S(2)}) collective-permute-start(f32[8,128]{1,0:T(8,128)S(1)} %add.40.refs_2_), channel_id=1, source_target_pairs={{0,4},{1,5},{2,6},{3,7},{4,0},{5,1},{6,2},{7,3},{8,12},{9,13},{10,... | collective-permute-start | bytes 12296 | tf_op jit(solution)/shard_map/ppermute | solution.py:39
  66.2 1.6 %collective-permute-done.12.refs_4_ = f32[8,128]{1,0:T(8,128)S(1)} collective-permute-done((f32[8,128]{1,0:T(8,128)S(1)}, f32[8,128]{1,0:T(8,128)S(1)}, u32[]{:S(2)}, u32[]{:S(2)}) %collective-permute-start.12) | collective-permute-done | bytes 4128 | tf_op jit(solution)/shard_map/ppermute | solution.py:39
  68.1 3.3 %collective-permute-done.11.refs_3_ = f32[8,128]{1,0:T(8,128)S(1)} collective-permute-done((f32[8,128]{1,0:T(8,128)S(1)}, f32[8,128]{1,0:T(8,128)S(1)}, u32[]{:S(2)}, u32[]{:S(2)}) %collective-permute-start.11) | collective-permute-done | bytes 4128 | tf_op jit(solution)/shard_map/ppermute | solution.py:39
  71.4 4.6 %shard_map.117 = (f32[8,128,128]{2,1,0:T(8,128)S(1)}, f32[8,128,128]{2,1,0:T(8,128)S(1)}, f32[8,128]{1,0:T(8,128)S(1)}) custom-call(s32[8,16]{1,0:T(8,128)S(1)} %fusion.3.src.refs_0_, s32[8]{0:T(128)} %refs_1_.7, f32[8,128]{1,0:T(8,128)S(1)} %add.40.refs_2_, f32[8,128]{1,0:T(8,128)S(1)} %collective-permute-done.11.refs_3_, ...), custom_call_target="tpu_custom_call" | custom-call | tf_op jit(solution)/shard_map/pallas_call | solution.py:333
  76.1 1.2 collective-permute-done.16
  77.2 1.4 %collective-permute-start.19 = (f32[8,128]{1,0:T(8,128)S(1)}, f32[8,128]{1,0:T(8,128)S(1)}, u32[]{:S(2)}, u32[]{:S(2)}) collective-permute-start(f32[8,128]{1,0:T(8,128)S(1)} %add.41.refs_0_), channel_id=1, source_target_pairs={{0,6},{1,7},{2,4},{3,5},{4,2},{5,3},{6,0},{7,1},{8,14},{9,15},{10,... | collective-permute-start | bytes 12296 | tf_op jit(solution)/shard_map/ppermute | solution.py:39
  78.6 0.6 collective-permute-start.18
  79.2 1.5 %collective-permute-start.17 = (f32[8,128]{1,0:T(8,128)S(1)}, f32[8,128]{1,0:T(8,128)S(1)}, u32[]{:S(2)}, u32[]{:S(2)}) collective-permute-start(f32[8,128]{1,0:T(8,128)S(1)} %add.41.refs_0_), channel_id=1, source_target_pairs={{0,2},{1,3},{2,0},{3,1},{4,6},{5,7},{6,4},{7,5},{8,10},{9,11},{10,... | collective-permute-start | bytes 12296 | tf_op jit(solution)/shard_map/ppermute | solution.py:39
  80.7 1.0 collective-permute-done.19.refs_3_
  81.7 0.5 collective-permute-done.18.refs_2_
  82.2 0.6 collective-permute-done.17.refs_1_
  83.1 3.8 %collective-permute-start.20 = (bf16[8,128,128]{2,1,0:T(8,128)(2,1)S(1)}, bf16[8,128,128]{2,1,0:T(8,128)(2,1)S(1)}, u32[]{:S(2)}, u32[]{:S(2)}) collective-permute-start(bf16[8,128,128]{2,1,0:T(8,128)(2,1)S(1)} %shard_map.118), channel_id=1, source_target_pairs={{0,8},{8,16},{16,24},{1,9},{9,17},{17,25},{2,10},{10,18},{18,26},{... | collective-permute-start | bytes 786440 | tf_op jit(solution)/shard_map/ppermute | solution.py:461
  87.0 3.3 %shard_map.119 = (f32[8,128,128]{2,1,0:T(8,128)S(1)}, bf16[8,2048,128]{2,1,0:T(8,128)(2,1)S(1)}) custom-call(s32[8,16]{1,0:T(8,128)S(1)} %fusion.3.src.refs_0_, s32[8]{0:T(128)} %refs_1_.7, bf16[8,128,128]{2,1,0:T(8,128)(2,1)S(1)} %get-tuple-element.69.even.refs_11_, bf16[8,128,128]{2,1,0:T(8,128)(2,1)S(1)} %get-tuple-element.67.odd.refs_12_, ...), custom_call_target="tpu_custom_call" | custom-call | tf_op jit(solution)/shard_map/pallas_call | solution.py:333
  90.3 1.3 collective-permute-done.20.handed
  91.6 6.0 %shard_map.120 = (f32[8,128,128]{2,1,0:T(8,128)S(1)}, bf16[8,128,128]{2,1,0:T(8,128)(2,1)S(1)}, f32[8,128]{1,0:T(8,128)S(1)}, bf16[8,16,128,128]{3,2,1,0:T(8,128)(2,1)S(1)}) custom-call(s32[8]{0:T(128)} %refs_1_.7, bf16[8,128,128]{2,1,0:T(8,128)(2,1)S(1)} %collective-permute-done.20.handed, bf16[8,16,128,128]{3,2,1,0:T(8,128)(2,1)S(1)} %bitcast.30, ...), custom_call_target="tpu_custom_call" | custom-call | tf_op jit(solution)/shard_map/pallas_call | solution.py:333
  97.6 0.7 collective-permute-start.28
  98.3 2.6 %collective-permute-start.27 = (bf16[8,128,128]{2,1,0:T(8,128)(2,1)S(1)}, bf16[8,128,128]{2,1,0:T(8,128)(2,1)S(1)}, u32[]{:S(2)}, u32[]{:S(2)}) collective-permute-start(bf16[8,128,128]{2,1,0:T(8,128)(2,1)S(1)} %get-tuple-element.56), channel_id=1, source_target_pairs={{0,1},{1,0},{2,3},{3,2},{4,5},{5,4},{6,7},{7,6},{8,9},{9,8},{10,11... | collective-permute-start | bytes 786440 | tf_op jit(solution)/shard_map/ppermute | solution.py:28
  100.9 1.1 collective-permute-done.23
  102.0 1.4 %collective-permute-start.26 = (f32[8,128]{1,0:T(8,128)S(1)}, f32[8,128]{1,0:T(8,128)S(1)}, u32[]{:S(2)}, u32[]{:S(2)}) collective-permute-start(f32[8,128]{1,0:T(8,128)S(1)} %add.42.refs_2_), channel_id=1, source_target_pairs={{0,6},{1,7},{2,4},{3,5},{4,2},{5,3},{6,0},{7,1},{8,14},{9,15},{10,... | collective-permute-start | bytes 12296 | tf_op jit(solution)/shard_map/ppermute | solution.py:39
  103.5 1.5 %collective-permute-start.25 = (f32[8,128]{1,0:T(8,128)S(1)}, f32[8,128]{1,0:T(8,128)S(1)}, u32[]{:S(2)}, u32[]{:S(2)}) collective-permute-start(f32[8,128]{1,0:T(8,128)S(1)} %add.42.refs_2_), channel_id=1, source_target_pairs={{0,4},{1,5},{2,6},{3,7},{4,0},{5,1},{6,2},{7,3},{8,12},{9,13},{10,... | collective-permute-start | bytes 12296 | tf_op jit(solution)/shard_map/ppermute | solution.py:39
  105.0 0.6 collective-permute-start.24
  105.5 1.0 collective-permute-done.26.refs_5_
  106.5 0.5 collective-permute-done.25.refs_4_
  107.1 1.5 %collective-permute-done.24.refs_3_ = f32[8,128]{1,0:T(8,128)S(1)} collective-permute-done((f32[8,128]{1,0:T(8,128)S(1)}, f32[8,128]{1,0:T(8,128)S(1)}, u32[]{:S(2)}, u32[]{:S(2)}) %collective-permute-start.24) | collective-permute-done | bytes 4128 | tf_op jit(solution)/shard_map/ppermute | solution.py:39
  108.6 4.3 %shard_map.122 = (f32[8,128,128]{2,1,0:T(8,128)S(1)}, f32[8,128,128]{2,1,0:T(8,128)S(1)}, bf16[8,128,128]{2,1,0:T(8,128)(2,1)S(1)}, f32[8,128]{1,0:T(8,128)S(1)}...) custom-call(s32[8,16]{1,0:T(8,128)S(1)} %fusion.3.src.refs_0_, s32[8]{0:T(128)} %refs_1_.7, ...), custom_call_target="tpu_custom_call" | custom-call | tf_op jit(solution)/shard_map/pallas_call | solution.py:333
  112.9 0.9 collective-permute-start.34
  113.7 2.0 %collective-permute-start.33 = (bf16[8,128,128]{2,1,0:T(8,128)(2,1)S(1)}, bf16[8,128,128]{2,1,0:T(8,128)(2,1)S(1)}, u32[]{:S(2)}, u32[]{:S(2)}) collective-permute-start(bf16[8,128,128]{2,1,0:T(8,128)(2,1)S(1)} %get-tuple-element.62), channel_id=1, source_target_pairs={{0,1},{1,0},{2,3},{3,2},{4,5},{5,4},{6,7},{7,6},{8,9},{9,8},{10,11... | collective-permute-start | bytes 786440 | tf_op jit(solution)/shard_map/ppermute | solution.py:28
  115.8 1.1 collective-permute-done.29
  116.9 1.7 %collective-permute-start.32 = (f32[8,128]{1,0:T(8,128)S(1)}, f32[8,128]{1,0:T(8,128)S(1)}, u32[]{:S(2)}, u32[]{:S(2)}) collective-permute-start(f32[8,128]{1,0:T(8,128)S(1)} %add.43.refs_2_), channel_id=1, source_target_pairs={{0,6},{1,7},{2,4},{3,5},{4,2},{5,3},{6,0},{7,1},{8,14},{9,15},{10,... | collective-permute-start | bytes 12296 | tf_op jit(solution)/shard_map/ppermute | solution.py:39
  118.5 1.5 %collective-permute-start.31 = (f32[8,128]{1,0:T(8,128)S(1)}, f32[8,128]{1,0:T(8,128)S(1)}, u32[]{:S(2)}, u32[]{:S(2)}) collective-permute-start(f32[8,128]{1,0:T(8,128)S(1)} %add.43.refs_2_), channel_id=1, source_target_pairs={{0,4},{1,5},{2,6},{3,7},{4,0},{5,1},{6,2},{7,3},{8,12},{9,13},{10,... | collective-permute-start | bytes 12296 | tf_op jit(solution)/shard_map/ppermute | solution.py:39
  120.4 1.0 collective-permute-done.32.refs_5_
  121.4 0.8 collective-permute-done.31.refs_4_
  122.2 1.5 %collective-permute-done.30.refs_3_ = f32[8,128]{1,0:T(8,128)S(1)} collective-permute-done((f32[8,128]{1,0:T(8,128)S(1)}, f32[8,128]{1,0:T(8,128)S(1)}, u32[]{:S(2)}, u32[]{:S(2)}) %collective-permute-start.30) | collective-permute-done | bytes 4128 | tf_op jit(solution)/shard_map/ppermute | solution.py:39
  123.6 4.4 %shard_map.123 = (f32[8,128,128]{2,1,0:T(8,128)S(1)}, f32[8,128,128]{2,1,0:T(8,128)S(1)}, f32[8,128]{1,0:T(8,128)S(1)}) custom-call(s32[8,16]{1,0:T(8,128)S(1)} %fusion.3.src.refs_0_, s32[8]{0:T(128)} %refs_1_.7, f32[8,128]{1,0:T(8,128)S(1)} %add.43.refs_2_, f32[8,128]{1,0:T(8,128)S(1)} %collective-permute-done.30.refs_3_, ...), custom_call_target="tpu_custom_call" | custom-call | tf_op jit(solution)/shard_map/pallas_call | solution.py:333
  128.1 1.2 collective-permute-done.35
  129.3 1.6 %collective-permute-start.38 = (f32[8,128]{1,0:T(8,128)S(1)}, f32[8,128]{1,0:T(8,128)S(1)}, u32[]{:S(2)}, u32[]{:S(2)}) collective-permute-start(f32[8,128]{1,0:T(8,128)S(1)} %add.44.refs_0_), channel_id=1, source_target_pairs={{0,6},{1,7},{2,4},{3,5},{4,2},{5,3},{6,0},{7,1},{8,14},{9,15},{10,... | collective-permute-start | bytes 12296 | tf_op jit(solution)/shard_map/ppermute | solution.py:39
  130.9 1.4 %collective-permute-start.37 = (f32[8,128]{1,0:T(8,128)S(1)}, f32[8,128]{1,0:T(8,128)S(1)}, u32[]{:S(2)}, u32[]{:S(2)}) collective-permute-start(f32[8,128]{1,0:T(8,128)S(1)} %add.44.refs_0_), channel_id=1, source_target_pairs={{0,4},{1,5},{2,6},{3,7},{4,0},{5,1},{6,2},{7,3},{8,12},{9,13},{10,... | collective-permute-start | bytes 12296 | tf_op jit(solution)/shard_map/ppermute | solution.py:39
  132.8 1.0 shard_map.121
  133.8 0.7 collective-permute-done.37.refs_2_
  134.5 1.4 %collective-permute-done.36.refs_1_ = f32[8,128]{1,0:T(8,128)S(1)} collective-permute-done((f32[8,128]{1,0:T(8,128)S(1)}, f32[8,128]{1,0:T(8,128)S(1)}, u32[]{:S(2)}, u32[]{:S(2)}) %collective-permute-start.36) | collective-permute-done | bytes 4128 | tf_op jit(solution)/shard_map/ppermute | solution.py:39
  135.9 1.0 shard_map.124
  (49 shorter events, 1.9 us)
Async XLA Ops:
  2.4 11.6 %collective-permute-start.1 = (bf16[8,128,128]{2,1,0:T(8,128)(2,1)S(1)}, bf16[8,128,128]{2,1,0:T(8,128)(2,1)S(1)}, u32[]{:S(2)}, u32[]{:S(2)}) collective-permute-start(bf16[8,128,128]{2,1,0:T(8,128)(2,1)S(1)} %get-tuple-element.34.packed), channel_id=1, source_target_pairs={{1,2},{2,1},{3,4},{4,3},{5,6},{6,5},{9,10},{10,9},{11,12},{12,11},... | collective-permute-start | bytes 786440 | tf_op jit(solution)/shard_map/ppermute | solution.py:27
  3.1 11.0 %collective-permute-start = (bf16[8,128,128]{2,1,0:T(8,128)(2,1)S(1)}, bf16[8,128,128]{2,1,0:T(8,128)(2,1)S(1)}, u32[]{:S(2)}, u32[]{:S(2)}) collective-permute-start(bf16[8,128,128]{2,1,0:T(8,128)(2,1)S(1)} %get-tuple-element.34.packed), channel_id=1, source_target_pairs={{0,1},{1,0},{2,3},{3,2},{4,5},{5,4},{6,7},{7,6},{8,9},{9,8},{10,11... | collective-permute-start | bytes 786440 | tf_op jit(solution)/shard_map/ppermute | solution.py:28
  9.8 16.0 %collective-permute-start.9 = (bf16[8,128,128]{2,1,0:T(8,128)(2,1)S(1)}, bf16[8,128,128]{2,1,0:T(8,128)(2,1)S(1)}, u32[]{:S(2)}, u32[]{:S(2)}) collective-permute-start(bf16[8,128,128]{2,1,0:T(8,128)(2,1)S(1)} %get-tuple-element.39), channel_id=1, source_target_pairs={{1,2},{2,1},{3,4},{4,3},{5,6},{6,5},{9,10},{10,9},{11,12},{12,11},... | collective-permute-start | bytes 786440 | tf_op jit(solution)/shard_map/ppermute | solution.py:27
  10.5 20.2 %collective-permute-start.8 = (bf16[8,128,128]{2,1,0:T(8,128)(2,1)S(1)}, bf16[8,128,128]{2,1,0:T(8,128)(2,1)S(1)}, u32[]{:S(2)}, u32[]{:S(2)}) collective-permute-start(bf16[8,128,128]{2,1,0:T(8,128)(2,1)S(1)} %get-tuple-element.39), channel_id=1, source_target_pairs={{0,1},{1,0},{2,3},{3,2},{4,5},{5,4},{6,7},{7,6},{8,9},{9,8},{10,11... | collective-permute-start | bytes 786440 | tf_op jit(solution)/shard_map/ppermute | solution.py:28
  14.1 36.0 %copy-start = (bf16[1,8,16,128,128]{4,3,2,1,0:T(8,128)(2,1)S(1)}, bf16[1,8,16,128,128]{4,3,2,1,0:T(8,128)(2,1)}, u32[]{:S(2)}) copy-start(bf16[1,8,16,128,128]{4,3,2,1,0:T(8,128)(2,1)} %param.14) | copy-start | bytes 12582916
  14.1 36.0 %copy-start.1 = (bf16[1,8,16,128,128]{4,3,2,1,0:T(8,128)(2,1)S(1)}, bf16[1,8,16,128,128]{4,3,2,1,0:T(8,128)(2,1)}, u32[]{:S(2)}) copy-start(bf16[1,8,16,128,128]{4,3,2,1,0:T(8,128)(2,1)} %param.15) | copy-start | bytes 12582916
  14.1 36.0 %copy-start.3 = (f32[1,8,128,128]{3,2,1,0:T(8,128)S(1)}, f32[1,8,128,128]{3,2,1,0:T(8,128)}, u32[]{:S(2)}) copy-start(f32[1,8,128,128]{3,2,1,0:T(8,128)} %param.12) | copy-start | bytes 1572868
  20.4 29.7 %collective-permute-start.7 = (bf16[8,128,128]{2,1,0:T(8,128)(2,1)S(1)}, bf16[8,128,128]{2,1,0:T(8,128)(2,1)S(1)}, u32[]{:S(2)}, u32[]{:S(2)}) collective-permute-start(bf16[8,128,128]{2,1,0:T(8,128)(2,1)S(1)} %get-tuple-element.38), channel_id=1, source_target_pairs={{1,2},{2,1},{3,4},{4,3},{5,6},{6,5},{9,10},{10,9},{11,12},{12,11},... | collective-permute-start | bytes 786440 | tf_op jit(solution)/shard_map/ppermute | solution.py:27
  21.0 29.0 %collective-permute-start.6 = (bf16[8,128,128]{2,1,0:T(8,128)(2,1)S(1)}, bf16[8,128,128]{2,1,0:T(8,128)(2,1)S(1)}, u32[]{:S(2)}, u32[]{:S(2)}) collective-permute-start(bf16[8,128,128]{2,1,0:T(8,128)(2,1)S(1)} %get-tuple-element.38), channel_id=1, source_target_pairs={{0,1},{1,0},{2,3},{3,2},{4,5},{5,4},{6,7},{7,6},{8,9},{9,8},{10,11... | collective-permute-start | bytes 786440 | tf_op jit(solution)/shard_map/ppermute | solution.py:28
  23.9 1.2 collective-permute-start.2
  25.1 61.7 %collective-permute-start.22 = (bf16[16,128,128]{2,1,0:T(8,128)(2,1)S(1)}, bf16[16,128,128]{2,1,0:T(8,128)(2,1)S(1)}, u32[]{:S(2)}, u32[]{:S(2)}) collective-permute-start(bf16[16,128,128]{2,1,0:T(8,128)(2,1)S(1)} %get-tuple-element.49), channel_id=1, source_target_pairs={{1,2},{2,1},{3,4},{4,3},{5,6},{6,5},{9,10},{10,9},{11,12},{12,11},... | collective-permute-start | bytes 1572872 | tf_op jit(solution)/shard_map/ppermute | solution.py:27
  25.8 11.9 %collective-permute-start.5 = (f32[8,128]{1,0:T(8,128)S(1)}, f32[8,128]{1,0:T(8,128)S(1)}, u32[]{:S(2)}, u32[]{:S(2)}) collective-permute-start(f32[8,128]{1,0:T(8,128)S(1)} %add.39.refs_2_), channel_id=1, source_target_pairs={{0,6},{1,7},{2,4},{3,5},{4,2},{5,3},{6,0},{7,1},{8,14},{9,15},{10,... | collective-permute-start | bytes 12296 | tf_op jit(solution)/shard_map/ppermute | solution.py:39
  30.6 56.2 %collective-permute-start.21 = (bf16[16,128,128]{2,1,0:T(8,128)(2,1)S(1)}, bf16[16,128,128]{2,1,0:T(8,128)(2,1)S(1)}, u32[]{:S(2)}, u32[]{:S(2)}) collective-permute-start(bf16[16,128,128]{2,1,0:T(8,128)(2,1)S(1)} %get-tuple-element.49), channel_id=1, source_target_pairs={{0,1},{1,0},{2,3},{3,2},{4,5},{5,4},{6,7},{7,6},{8,9},{9,8},{10,11... | collective-permute-start | bytes 1572872 | tf_op jit(solution)/shard_map/ppermute | solution.py:28
  37.8 7.0 %collective-permute-start.4 = (f32[8,128]{1,0:T(8,128)S(1)}, f32[8,128]{1,0:T(8,128)S(1)}, u32[]{:S(2)}, u32[]{:S(2)}) collective-permute-start(f32[8,128]{1,0:T(8,128)S(1)} %add.39.refs_2_), channel_id=1, source_target_pairs={{0,4},{1,5},{2,6},{3,7},{4,0},{5,1},{6,2},{7,3},{8,12},{9,13},{10,... | collective-permute-start | bytes 12296 | tf_op jit(solution)/shard_map/ppermute | solution.py:39
  44.8 5.3 %collective-permute-start.3 = (f32[8,128]{1,0:T(8,128)S(1)}, f32[8,128]{1,0:T(8,128)S(1)}, u32[]{:S(2)}, u32[]{:S(2)}) collective-permute-start(f32[8,128]{1,0:T(8,128)S(1)} %add.39.refs_2_), channel_id=1, source_target_pairs={{0,2},{1,3},{2,0},{3,1},{4,6},{5,7},{6,4},{7,5},{8,10},{9,11},{10,... | collective-permute-start | bytes 12296 | tf_op jit(solution)/shard_map/ppermute | solution.py:39
  54.4 17.0 %collective-permute-start.15 = (bf16[8,128,128]{2,1,0:T(8,128)(2,1)S(1)}, bf16[8,128,128]{2,1,0:T(8,128)(2,1)S(1)}, u32[]{:S(2)}, u32[]{:S(2)}) collective-permute-start(bf16[8,128,128]{2,1,0:T(8,128)(2,1)S(1)} %get-tuple-element.45), channel_id=1, source_target_pairs={{1,2},{2,1},{3,4},{4,3},{5,6},{6,5},{9,10},{10,9},{11,12},{12,11},... | collective-permute-start | bytes 786440 | tf_op jit(solution)/shard_map/ppermute | solution.py:27
  55.1 16.3 %collective-permute-start.14 = (bf16[8,128,128]{2,1,0:T(8,128)(2,1)S(1)}, bf16[8,128,128]{2,1,0:T(8,128)(2,1)S(1)}, u32[]{:S(2)}, u32[]{:S(2)}) collective-permute-start(bf16[8,128,128]{2,1,0:T(8,128)(2,1)S(1)} %get-tuple-element.45), channel_id=1, source_target_pairs={{0,1},{1,0},{2,3},{3,2},{4,5},{5,4},{6,7},{7,6},{8,9},{9,8},{10,11... | collective-permute-start | bytes 786440 | tf_op jit(solution)/shard_map/ppermute | solution.py:28
  58.5 1.2 collective-permute-start.10
  59.7 4.5 %collective-permute-start.13 = (f32[8,128]{1,0:T(8,128)S(1)}, f32[8,128]{1,0:T(8,128)S(1)}, u32[]{:S(2)}, u32[]{:S(2)}) collective-permute-start(f32[8,128]{1,0:T(8,128)S(1)} %add.40.refs_2_), channel_id=1, source_target_pairs={{0,6},{1,7},{2,4},{3,5},{4,2},{5,3},{6,0},{7,1},{8,14},{9,15},{10,... | collective-permute-start | bytes 12296 | tf_op jit(solution)/shard_map/ppermute | solution.py:39
  64.2 3.6 %collective-permute-start.12 = (f32[8,128]{1,0:T(8,128)S(1)}, f32[8,128]{1,0:T(8,128)S(1)}, u32[]{:S(2)}, u32[]{:S(2)}) collective-permute-start(f32[8,128]{1,0:T(8,128)S(1)} %add.40.refs_2_), channel_id=1, source_target_pairs={{0,4},{1,5},{2,6},{3,7},{4,0},{5,1},{6,2},{7,3},{8,12},{9,13},{10,... | collective-permute-start | bytes 12296 | tf_op jit(solution)/shard_map/ppermute | solution.py:39
  67.8 3.6 %collective-permute-start.11 = (f32[8,128]{1,0:T(8,128)S(1)}, f32[8,128]{1,0:T(8,128)S(1)}, u32[]{:S(2)}, u32[]{:S(2)}) collective-permute-start(f32[8,128]{1,0:T(8,128)S(1)} %add.40.refs_2_), channel_id=1, source_target_pairs={{0,2},{1,3},{2,0},{3,1},{4,6},{5,7},{6,4},{7,5},{8,10},{9,11},{10,... | collective-permute-start | bytes 12296 | tf_op jit(solution)/shard_map/ppermute | solution.py:39
  71.4 15.5 %copy-start.2 = (bf16[1,8,16,128,128]{4,3,2,1,0:T(8,128)(2,1)S(1)}, bf16[1,8,16,128,128]{4,3,2,1,0:T(8,128)(2,1)}, u32[]{:S(2)}) copy-start(bf16[1,8,16,128,128]{4,3,2,1,0:T(8,128)(2,1)} %param.17) | copy-start | bytes 12582916
  76.0 10.9 %copy-start.6 = (f32[1,8,128,128]{3,2,1,0:T(8,128)S(1)}, f32[1,8,128,128]{3,2,1,0:T(8,128)}, u32[]{:S(2)}) copy-start(f32[1,8,128,128]{3,2,1,0:T(8,128)} %param.11) | copy-start | bytes 1572868
  76.0 1.2 collective-permute-start.16
  77.2 4.5 %collective-permute-start.19 = (f32[8,128]{1,0:T(8,128)S(1)}, f32[8,128]{1,0:T(8,128)S(1)}, u32[]{:S(2)}, u32[]{:S(2)}) collective-permute-start(f32[8,128]{1,0:T(8,128)S(1)} %add.41.refs_0_), channel_id=1, source_target_pairs={{0,6},{1,7},{2,4},{3,5},{4,2},{5,3},{6,0},{7,1},{8,14},{9,15},{10,... | collective-permute-start | bytes 12296 | tf_op jit(solution)/shard_map/ppermute | solution.py:39
  78.6 3.6 %collective-permute-start.18 = (f32[8,128]{1,0:T(8,128)S(1)}, f32[8,128]{1,0:T(8,128)S(1)}, u32[]{:S(2)}, u32[]{:S(2)}) collective-permute-start(f32[8,128]{1,0:T(8,128)S(1)} %add.41.refs_0_), channel_id=1, source_target_pairs={{0,4},{1,5},{2,6},{3,7},{4,0},{5,1},{6,2},{7,3},{8,12},{9,13},{10,... | collective-permute-start | bytes 12296 | tf_op jit(solution)/shard_map/ppermute | solution.py:39
  79.2 3.6 %collective-permute-start.17 = (f32[8,128]{1,0:T(8,128)S(1)}, f32[8,128]{1,0:T(8,128)S(1)}, u32[]{:S(2)}, u32[]{:S(2)}) collective-permute-start(f32[8,128]{1,0:T(8,128)S(1)} %add.41.refs_0_), channel_id=1, source_target_pairs={{0,2},{1,3},{2,0},{3,1},{4,6},{5,7},{6,4},{7,5},{8,10},{9,11},{10,... | collective-permute-start | bytes 12296 | tf_op jit(solution)/shard_map/ppermute | solution.py:39
  82.8 8.8 %copy-start.4 = (f32[1,8,128,128]{3,2,1,0:T(8,128)S(1)}, f32[1,8,128,128]{3,2,1,0:T(8,128)}, u32[]{:S(2)}) copy-start(f32[1,8,128,128]{3,2,1,0:T(8,128)} %param.13) | copy-start | bytes 1572868
  82.8 8.8 %copy-start.5 = (bf16[1,8,16,128,128]{4,3,2,1,0:T(8,128)(2,1)S(1)}, bf16[1,8,16,128,128]{4,3,2,1,0:T(8,128)(2,1)}, u32[]{:S(2)}) copy-start(bf16[1,8,16,128,128]{4,3,2,1,0:T(8,128)(2,1)} %param.16) | copy-start | bytes 12582916
  83.1 8.5 %collective-permute-start.20 = (bf16[8,128,128]{2,1,0:T(8,128)(2,1)S(1)}, bf16[8,128,128]{2,1,0:T(8,128)(2,1)S(1)}, u32[]{:S(2)}, u32[]{:S(2)}) collective-permute-start(bf16[8,128,128]{2,1,0:T(8,128)(2,1)S(1)} %shard_map.118), channel_id=1, source_target_pairs={{0,8},{8,16},{16,24},{1,9},{9,17},{17,25},{2,10},{10,18},{18,26},{... | collective-permute-start | bytes 786440 | tf_op jit(solution)/shard_map/ppermute | solution.py:461
  97.6 11.0 %collective-permute-start.28 = (bf16[8,128,128]{2,1,0:T(8,128)(2,1)S(1)}, bf16[8,128,128]{2,1,0:T(8,128)(2,1)S(1)}, u32[]{:S(2)}, u32[]{:S(2)}) collective-permute-start(bf16[8,128,128]{2,1,0:T(8,128)(2,1)S(1)} %get-tuple-element.56), channel_id=1, source_target_pairs={{1,2},{2,1},{3,4},{4,3},{5,6},{6,5},{9,10},{10,9},{11,12},{12,11},... | collective-permute-start | bytes 786440 | tf_op jit(solution)/shard_map/ppermute | solution.py:27
  98.3 10.3 %collective-permute-start.27 = (bf16[8,128,128]{2,1,0:T(8,128)(2,1)S(1)}, bf16[8,128,128]{2,1,0:T(8,128)(2,1)S(1)}, u32[]{:S(2)}, u32[]{:S(2)}) collective-permute-start(bf16[8,128,128]{2,1,0:T(8,128)(2,1)S(1)} %get-tuple-element.56), channel_id=1, source_target_pairs={{0,1},{1,0},{2,3},{3,2},{4,5},{5,4},{6,7},{7,6},{8,9},{9,8},{10,11... | collective-permute-start | bytes 786440 | tf_op jit(solution)/shard_map/ppermute | solution.py:28
  100.9 1.2 collective-permute-start.23
  102.0 4.5 %collective-permute-start.26 = (f32[8,128]{1,0:T(8,128)S(1)}, f32[8,128]{1,0:T(8,128)S(1)}, u32[]{:S(2)}, u32[]{:S(2)}) collective-permute-start(f32[8,128]{1,0:T(8,128)S(1)} %add.42.refs_2_), channel_id=1, source_target_pairs={{0,6},{1,7},{2,4},{3,5},{4,2},{5,3},{6,0},{7,1},{8,14},{9,15},{10,... | collective-permute-start | bytes 12296 | tf_op jit(solution)/shard_map/ppermute | solution.py:39
  103.5 3.6 %collective-permute-start.25 = (f32[8,128]{1,0:T(8,128)S(1)}, f32[8,128]{1,0:T(8,128)S(1)}, u32[]{:S(2)}, u32[]{:S(2)}) collective-permute-start(f32[8,128]{1,0:T(8,128)S(1)} %add.42.refs_2_), channel_id=1, source_target_pairs={{0,4},{1,5},{2,6},{3,7},{4,0},{5,1},{6,2},{7,3},{8,12},{9,13},{10,... | collective-permute-start | bytes 12296 | tf_op jit(solution)/shard_map/ppermute | solution.py:39
  105.0 3.6 %collective-permute-start.24 = (f32[8,128]{1,0:T(8,128)S(1)}, f32[8,128]{1,0:T(8,128)S(1)}, u32[]{:S(2)}, u32[]{:S(2)}) collective-permute-start(f32[8,128]{1,0:T(8,128)S(1)} %add.42.refs_2_), channel_id=1, source_target_pairs={{0,2},{1,3},{2,0},{3,1},{4,6},{5,7},{6,4},{7,5},{8,10},{9,11},{10,... | collective-permute-start | bytes 12296 | tf_op jit(solution)/shard_map/ppermute | solution.py:39
  112.9 10.8 %collective-permute-start.34 = (bf16[8,128,128]{2,1,0:T(8,128)(2,1)S(1)}, bf16[8,128,128]{2,1,0:T(8,128)(2,1)S(1)}, u32[]{:S(2)}, u32[]{:S(2)}) collective-permute-start(bf16[8,128,128]{2,1,0:T(8,128)(2,1)S(1)} %get-tuple-element.62), channel_id=1, source_target_pairs={{1,2},{2,1},{3,4},{4,3},{5,6},{6,5},{9,10},{10,9},{11,12},{12,11},... | collective-permute-start | bytes 786440 | tf_op jit(solution)/shard_map/ppermute | solution.py:27
  113.7 9.9 %collective-permute-start.33 = (bf16[8,128,128]{2,1,0:T(8,128)(2,1)S(1)}, bf16[8,128,128]{2,1,0:T(8,128)(2,1)S(1)}, u32[]{:S(2)}, u32[]{:S(2)}) collective-permute-start(bf16[8,128,128]{2,1,0:T(8,128)(2,1)S(1)} %get-tuple-element.62), channel_id=1, source_target_pairs={{0,1},{1,0},{2,3},{3,2},{4,5},{5,4},{6,7},{7,6},{8,9},{9,8},{10,11... | collective-permute-start | bytes 786440 | tf_op jit(solution)/shard_map/ppermute | solution.py:28
  115.7 1.2 collective-permute-start.29
  116.9 4.5 %collective-permute-start.32 = (f32[8,128]{1,0:T(8,128)S(1)}, f32[8,128]{1,0:T(8,128)S(1)}, u32[]{:S(2)}, u32[]{:S(2)}) collective-permute-start(f32[8,128]{1,0:T(8,128)S(1)} %add.43.refs_2_), channel_id=1, source_target_pairs={{0,6},{1,7},{2,4},{3,5},{4,2},{5,3},{6,0},{7,1},{8,14},{9,15},{10,... | collective-permute-start | bytes 12296 | tf_op jit(solution)/shard_map/ppermute | solution.py:39
  118.5 3.6 %collective-permute-start.31 = (f32[8,128]{1,0:T(8,128)S(1)}, f32[8,128]{1,0:T(8,128)S(1)}, u32[]{:S(2)}, u32[]{:S(2)}) collective-permute-start(f32[8,128]{1,0:T(8,128)S(1)} %add.43.refs_2_), channel_id=1, source_target_pairs={{0,4},{1,5},{2,6},{3,7},{4,0},{5,1},{6,2},{7,3},{8,12},{9,13},{10,... | collective-permute-start | bytes 12296 | tf_op jit(solution)/shard_map/ppermute | solution.py:39
  120.0 3.6 %collective-permute-start.30 = (f32[8,128]{1,0:T(8,128)S(1)}, f32[8,128]{1,0:T(8,128)S(1)}, u32[]{:S(2)}, u32[]{:S(2)}) collective-permute-start(f32[8,128]{1,0:T(8,128)S(1)} %add.43.refs_2_), channel_id=1, source_target_pairs={{0,2},{1,3},{2,0},{3,1},{4,6},{5,7},{6,4},{7,5},{8,10},{9,11},{10,... | collective-permute-start | bytes 12296 | tf_op jit(solution)/shard_map/ppermute | solution.py:39
  128.1 1.2 collective-permute-start.35
  129.3 4.5 %collective-permute-start.38 = (f32[8,128]{1,0:T(8,128)S(1)}, f32[8,128]{1,0:T(8,128)S(1)}, u32[]{:S(2)}, u32[]{:S(2)}) collective-permute-start(f32[8,128]{1,0:T(8,128)S(1)} %add.44.refs_0_), channel_id=1, source_target_pairs={{0,6},{1,7},{2,4},{3,5},{4,2},{5,3},{6,0},{7,1},{8,14},{9,15},{10,... | collective-permute-start | bytes 12296 | tf_op jit(solution)/shard_map/ppermute | solution.py:39
  130.9 3.6 %collective-permute-start.37 = (f32[8,128]{1,0:T(8,128)S(1)}, f32[8,128]{1,0:T(8,128)S(1)}, u32[]{:S(2)}, u32[]{:S(2)}) collective-permute-start(f32[8,128]{1,0:T(8,128)S(1)} %add.44.refs_0_), channel_id=1, source_target_pairs={{0,4},{1,5},{2,6},{3,7},{4,0},{5,1},{6,2},{7,3},{8,12},{9,13},{10,... | collective-permute-start | bytes 12296 | tf_op jit(solution)/shard_map/ppermute | solution.py:39
  132.3 3.6 %collective-permute-start.36 = (f32[8,128]{1,0:T(8,128)S(1)}, f32[8,128]{1,0:T(8,128)S(1)}, u32[]{:S(2)}, u32[]{:S(2)}) collective-permute-start(f32[8,128]{1,0:T(8,128)S(1)} %add.44.refs_0_), channel_id=1, source_target_pairs={{0,2},{1,3},{2,0},{3,1},{4,6},{5,7},{6,4},{7,5},{8,10},{9,11},{10,... | collective-permute-start | bytes 12296 | tf_op jit(solution)/shard_map/ppermute | solution.py:39

commit v2 on v1

--- a/solution.py
+++ b/solution.py
@@ -93,11 +93,12 @@
     lax.fori_loop(0, blocks // lanes, body, 0)
 
 
-def prepare_kernel(dims, wave, u, packed, sems):
+def prepare_kernel(ready, dims, wave, u, packed, sems):
     blocks, width, _ = u.shape
     copies = [pltpu.make_async_copy(wave.at[b], u.at[b], sems.at[b]) for b in range(blocks)]
     for copy in copies:
         copy.start()
+    ready()
     for b in range(blocks):
         copies[b].wait()
         value = jnp.where(live_of(dims[b], width), u[b], 0.0)
@@ -105,7 +106,7 @@
         packed[b] = value.astype(BF16)
 
 
-def send_kernel(dims, packed, onsite_hbm, later_hbm, wave_hbm, *rest):
+def send_kernel(ready, dims, packed, onsite_hbm, later_hbm, wave_hbm, *rest):
     weight, bundle, onsite, later, wave, sems = rest
     del packed
     pairs = ((onsite_hbm, onsite), (wave_hbm, wave), (later_hbm, later))
@@ -120,6 +121,7 @@
         return carry
 
     lax.fori_loop(0, blocks, first, 0)
+    ready()
     copies[1].wait()
     copies[2].wait()
 
@@ -131,7 +133,7 @@
     lax.fori_loop(0, blocks, second, 0)
 
 
-def start_kernel(src, dims, even, odd, u, onsite_hbm, left_hbm, right_hbm, *rest):
+def start_kernel(scalars, src, dims, even, odd, u, onsite_hbm, left_hbm, right_hbm, *rest):
     term, sent, stats, onsite, left, right, x, acc, sems, *lxs = rest
     blocks, terms, width, _ = left.shape
     lanes = len(lxs)
@@ -168,16 +170,18 @@
         for copy in copies_of(group):
             copy.wait()
 
+    scalars()
     apply_terms(src, dims, x, left, right, lxs, blocks, terms, width, emit, ready)
     stats[...] = jnp.zeros_like(stats)
     for row in range(2):
         put_row(stats, row, acc[row])
 
 
-def ahead_kernel(src, dims, even, odd, wave, right, u, y, x):
+def ahead_kernel(ready, src, dims, even, odd, wave, right, u, y, x):
     blocks, terms, width, _ = right.shape
     x[:blocks] = even[...]
     x[2 * blocks :] = odd[...]
+    ready()
 
     def first(b, carry):
         value = jnp.where(live_of(dims[b], width), wave[b], 0.0)
@@ -196,10 +200,11 @@
     lax.fori_loop(0, blocks, body, 0)
 
 
-def build_kernel(dims, handed, base, y, u, onsite, term, sent, stats, left, acc, *works):
+def build_kernel(ready, dims, handed, base, y, u, onsite, term, sent, stats, left, acc, *works):
     blocks, terms, width, _ = base.shape
     lanes = len(works)
     acc[...] = jnp.zeros_like(acc)
+    ready()
 
     def body(i, carry):
         for j in range(lanes):
@@ -234,7 +239,7 @@
         put_row(stats, row, acc[row])
 
 
-def next_kernel(n_parts, entries, share, first, last, *refs):
+def next_kernel(n_parts, entries, share, first, last, scalars, *refs):
     src, dims, *rest = refs
     parts, rest = rest[:n_parts], rest[n_parts:]
     (u, term, onsite, left, right, u_even, u_odd, t_even, t_odd, w_even, w_odd, *rest) = rest
@@ -282,6 +287,7 @@
         else:
             sent[b] = value.astype(BF16)
 
+    scalars()
     apply_terms(src, dims, x, left, right, lxs, blocks, terms, width, emit)
     stats[...] = jnp.zeros_like(stats)
     for row in range(5 if last else 2):
@@ -325,19 +331,38 @@
 
 
 VMEM = pl.BlockSpec(memory_space=pltpu.VMEM)
-SMEM = pl.BlockSpec(memory_space=pltpu.SMEM)
 HBM = pl.BlockSpec(memory_space=pltpu.HBM)
 
 
 def call(kernel, scalars, arrays, outs, scratch, far=(), out_spec=None):
+    count = len(scalars)
+
+    def body(*refs):
+        tables, sems = refs[-1 - count : -1], refs[-1]
+        copies = [pltpu.make_async_copy(refs[i], tables[i], sems.at[i]) for i in range(count)]
+        for copy in copies:
+            copy.start()
+
+        def ready():
+            for copy in copies:
+                copy.wait()
+
+        kernel(ready, *tables, *refs[count : -1 - count])
+
+    held = [pltpu.SMEM(a.shape, a.dtype) for a in scalars]
+    held += [pltpu.SemaphoreType.DMA((count,))] if count else []
     return pl.pallas_call(
-        kernel,
+        body if count else kernel,
         out_shape=outs,
-        in_specs=[SMEM] * len(scalars) + [VMEM] * len(arrays) + [HBM] * len(far),
+        in_specs=[HBM] * count + [VMEM] * len(arrays) + [HBM] * len(far),
         out_specs=[out_spec or VMEM] * len(outs),
-        scratch_shapes=scratch,
+        scratch_shapes=[*scratch, *held],
         compiler_params=pltpu.CompilerParams(vmem_limit_bytes=16 << 20),
-    )(*scalars, *arrays, *[pltpu.with_memory_space_constraint(a, pltpu.HBM) for a in far])
+    )(
+        *[pltpu.with_memory_space_constraint(a, pltpu.HBM) for a in scalars],
+        *arrays,
+        *[pltpu.with_memory_space_constraint(a, pltpu.HBM) for a in far],
+    )
 
 
 def like(shape, dtype):
@@ -357,7 +382,6 @@
         sources,
         block_dims,
     ) = [a[0] if a.ndim > 3 else a for a in args]
-    block_dims = pltpu.with_memory_space_constraint(block_dims, pltpu.HBM)
     blocks, width = wave_first.shape[0], wave_first.shape[1]
     terms = left_first.shape[1]
     count = lax.axis_size("sec")

time: 138 us -> 133 us (0.964)
  Pallas kernels: 39.5 us -> 34.5 us
    pallas_call x12, Pallas kernels: 39.5 us -> 34.5 us  [call(): pl.pallas_call(body if count else kernel, out_shape=outs, in_specs=[HBM]...]
  transfers between devices with their start and end apart: 39 -> 39, of which waited for: 24 -> 24; matrix products, arithmetic and copies ran while one was open for 1% -> 1% of each run, Pallas kernels for 16% -> 14%
where the time goes in v2:
time: 133 us
  starting transfers between devices  57.6 us (43%)
  waiting for transfers between devices  38.2 us (29%)
  Pallas kernels  34.5 us (26%)
    pallas_call x12, Pallas kernels, call(): pl.pallas_call(body if count else kernel, out_shape=outs, in_specs=[HBM]...  34.5 us
    ppermute x18, waiting for transfers between devices, gathered_parts(): parts += [lax.ppermute(pair, 'sec', [(i, i ^ 2 * m) for i in range(count)])]  30.2 us
    ppermute x18, starting transfers between devices, gathered_parts(): parts += [lax.ppermute(pair, 'sec', [(i, i ^ 2 * m) for i in range(count)])]  30.1 us
    ppermute x7, starting transfers between devices, swapped(): even = lax.ppermute(block, 'sec', even_pairs(count))  18.2 us
    ppermute x6, waiting for transfers between devices, gathered_parts(): pair = partial + lax.ppermute(partial, 'sec', even_pairs(count))  6.66 us
    ppermute x7, starting transfers between devices, swapped(): odd = lax.ppermute(block, 'sec', odd_pairs(count))  5.06 us
    ppermute x1, starting transfers between devices, both_updates(): handed = lax.ppermute(handed, 'seg', [(s, s + 1) for s in range(segs - 1)])  3.76 us
  transfers between devices with their start and end apart: 39, of which 24 were waited for; matrix products, arithmetic and copies ran while one was open for 1% of the time, Pallas kernels for 14%

profile of v2, /device:TPU:0, one launch (start us, length us, event | category | flops | bytes accessed | tf_op | source)
XLA Modules:
  0.0 132.8 jit_solution(12012864531114622611)
XLA Ops:
  0.6 1.2 shard_map.113
  1.8 0.7 collective-permute-start.1
  2.5 4.4 %collective-permute-start = (bf16[8,128,128]{2,1,0:T(8,128)(2,1)S(1)}, bf16[8,128,128]{2,1,0:T(8,128)(2,1)S(1)}, u32[]{:S(2)}, u32[]{:S(2)}) collective-permute-start(bf16[8,128,128]{2,1,0:T(8,128)(2,1)S(1)} %get-tuple-element.34.refs_1_), channel_id=1, source_target_pairs={{0,1},{1,0},{2,3},{3,2},{4,5},{5,4},{6,7},{7,6},{8,9},{9,8},{10,11... | collective-permute-start | bytes 786440 | tf_op jit(solution)/shard_map/ppermute | solution.py:28
  6.9 1.6 %shard_map.115 = (bf16[8,128,128]{2,1,0:T(8,128)(2,1)S(1)}, bf16[16,128,128]{2,1,0:T(8,128)(2,1)S(1)}) custom-call(s32[8]{0:T(128)} %refs_1_.11, bf16[8,128,128]{2,1,0:T(8,128)(2,1)S(1)} %get-tuple-element.34.refs_1_, f32[8,128,128]{2,1,0:T(8,128)} %bitcast.19, f32[8,128,128]{2,1,0:T(8,128)} %bitcast.25, f32[8,128,128]{2,1,0:T(8,128)} %bitcast.31), custom_call_target="tpu_custom_call" | custom-call | tf_op jit(solution)/shard_map/pallas_call | solution.py:354
  8.5 0.7 collective-permute-start.9
  9.2 2.9 %collective-permute-start.8 = (bf16[8,128,128]{2,1,0:T(8,128)(2,1)S(1)}, bf16[8,128,128]{2,1,0:T(8,128)(2,1)S(1)}, u32[]{:S(2)}, u32[]{:S(2)}) collective-permute-start(bf16[8,128,128]{2,1,0:T(8,128)(2,1)S(1)} %get-tuple-element.39), channel_id=1, source_target_pairs={{0,1},{1,0},{2,3},{3,2},{4,5},{5,4},{6,7},{7,6},{8,9},{9,8},{10,11... | collective-permute-start | bytes 786440 | tf_op jit(solution)/shard_map/ppermute | solution.py:28
  12.1 1.3 fusion.3.refs_0_
  13.4 5.0 %shard_map.114 = (f32[8,128,128]{2,1,0:T(8,128)S(1)}, bf16[8,128,128]{2,1,0:T(8,128)(2,1)S(1)}, f32[8,128]{1,0:T(8,128)S(1)}) custom-call(s32[8,16]{1,0:T(8,128)} %fusion.3.refs_0_, s32[8]{0:T(128)} %refs_1_.11, bf16[8,128,128]{2,1,0:T(8,128)(2,1)S(1)} %collective-permute-done.refs_2_.refs_11_, ...), custom_call_target="tpu_custom_call" | custom-call | tf_op jit(solution)/shard_map/pallas_call | solution.py:354
  18.4 0.8 collective-permute-start.7
  19.2 2.9 %collective-permute-start.6 = (bf16[8,128,128]{2,1,0:T(8,128)(2,1)S(1)}, bf16[8,128,128]{2,1,0:T(8,128)(2,1)S(1)}, u32[]{:S(2)}, u32[]{:S(2)}) collective-permute-start(bf16[8,128,128]{2,1,0:T(8,128)(2,1)S(1)} %get-tuple-element.38), channel_id=1, source_target_pairs={{0,1},{1,0},{2,3},{3,2},{4,5},{5,4},{6,7},{7,6},{8,9},{9,8},{10,11... | collective-permute-start | bytes 786440 | tf_op jit(solution)/shard_map/ppermute | solution.py:28
  22.2 1.1 collective-permute-done.2
  23.3 0.7 collective-permute-start.22
  24.0 4.9 %collective-permute-start.5 = (f32[8,128]{1,0:T(8,128)S(1)}, f32[8,128]{1,0:T(8,128)S(1)}, u32[]{:S(2)}, u32[]{:S(2)}) collective-permute-start(f32[8,128]{1,0:T(8,128)S(1)} %add.39.refs_2_), channel_id=1, source_target_pairs={{0,6},{1,7},{2,4},{3,5},{4,2},{5,3},{6,0},{7,1},{8,14},{9,15},{10,... | collective-permute-start | bytes 12296 | tf_op jit(solution)/shard_map/ppermute | solution.py:39
  28.9 7.1 %collective-permute-done.5.refs_5_ = f32[8,128]{1,0:T(8,128)S(1)} collective-permute-done((f32[8,128]{1,0:T(8,128)S(1)}, f32[8,128]{1,0:T(8,128)S(1)}, u32[]{:S(2)}, u32[]{:S(2)}) %collective-permute-start.5) | collective-permute-done | bytes 4128 | tf_op jit(solution)/shard_map/ppermute | solution.py:39
  36.0 5.2 %collective-permute-start.4 = (f32[8,128]{1,0:T(8,128)S(1)}, f32[8,128]{1,0:T(8,128)S(1)}, u32[]{:S(2)}, u32[]{:S(2)}) collective-permute-start(f32[8,128]{1,0:T(8,128)S(1)} %add.39.refs_2_), channel_id=1, source_target_pairs={{0,4},{1,5},{2,6},{3,7},{4,0},{5,1},{6,2},{7,3},{8,12},{9,13},{10,... | collective-permute-start | bytes 12296 | tf_op jit(solution)/shard_map/ppermute | solution.py:39
  41.3 1.6 %collective-permute-done.4.refs_4_ = f32[8,128]{1,0:T(8,128)S(1)} collective-permute-done((f32[8,128]{1,0:T(8,128)S(1)}, f32[8,128]{1,0:T(8,128)S(1)}, u32[]{:S(2)}, u32[]{:S(2)}) %collective-permute-start.4) | collective-permute-done | bytes 4128 | tf_op jit(solution)/shard_map/ppermute | solution.py:39
  42.8 3.9 %collective-permute-start.3 = (f32[8,128]{1,0:T(8,128)S(1)}, f32[8,128]{1,0:T(8,128)S(1)}, u32[]{:S(2)}, u32[]{:S(2)}) collective-permute-start(f32[8,128]{1,0:T(8,128)S(1)} %add.39.refs_2_), channel_id=1, source_target_pairs={{0,2},{1,3},{2,0},{3,1},{4,6},{5,7},{6,4},{7,5},{8,10},{9,11},{10,... | collective-permute-start | bytes 12296 | tf_op jit(solution)/shard_map/ppermute | solution.py:39
  46.8 1.6 %collective-permute-done.3.refs_3_ = f32[8,128]{1,0:T(8,128)S(1)} collective-permute-done((f32[8,128]{1,0:T(8,128)S(1)}, f32[8,128]{1,0:T(8,128)S(1)}, u32[]{:S(2)}, u32[]{:S(2)}) %collective-permute-start.3) | collective-permute-done | bytes 4128 | tf_op jit(solution)/shard_map/ppermute | solution.py:39
  48.4 3.7 %shard_map.116 = (f32[8,128,128]{2,1,0:T(8,128)S(1)}, f32[8,128,128]{2,1,0:T(8,128)S(1)}, bf16[8,128,128]{2,1,0:T(8,128)(2,1)S(1)}, f32[8,128]{1,0:T(8,128)S(1)}...) custom-call(s32[8,16]{1,0:T(8,128)} %fusion.3.refs_0_, s32[8]{0:T(128)} %refs_1_.11, f32[8,128]{1,0:T(8,128)S(1)} %add.39.refs_2_, ...), custom_call_target="tpu_custom_call" | custom-call | tf_op jit(solution)/shard_map/pallas_call | solution.py:354
  52.1 0.7 collective-permute-start.15
  52.8 3.4 %collective-permute-start.14 = (bf16[8,128,128]{2,1,0:T(8,128)(2,1)S(1)}, bf16[8,128,128]{2,1,0:T(8,128)(2,1)S(1)}, u32[]{:S(2)}, u32[]{:S(2)}) collective-permute-start(bf16[8,128,128]{2,1,0:T(8,128)(2,1)S(1)} %get-tuple-element.45), channel_id=1, source_target_pairs={{0,1},{1,0},{2,3},{3,2},{4,5},{5,4},{6,7},{7,6},{8,9},{9,8},{10,11... | collective-permute-start | bytes 786440 | tf_op jit(solution)/shard_map/ppermute | solution.py:28
  56.3 1.1 collective-permute-done.10
  57.4 4.5 %collective-permute-done.13.refs_5_ = f32[8,128]{1,0:T(8,128)S(1)} collective-permute-done((f32[8,128]{1,0:T(8,128)S(1)}, f32[8,128]{1,0:T(8,128)S(1)}, u32[]{:S(2)}, u32[]{:S(2)}) %collective-permute-start.13) | collective-permute-done | bytes 4128 | tf_op jit(solution)/shard_map/ppermute | solution.py:39
  61.9 1.8 %collective-permute-start.12 = (f32[8,128]{1,0:T(8,128)S(1)}, f32[8,128]{1,0:T(8,128)S(1)}, u32[]{:S(2)}, u32[]{:S(2)}) collective-permute-start(f32[8,128]{1,0:T(8,128)S(1)} %add.40.refs_2_), channel_id=1, source_target_pairs={{0,4},{1,5},{2,6},{3,7},{4,0},{5,1},{6,2},{7,3},{8,12},{9,13},{10,... | collective-permute-start | bytes 12296 | tf_op jit(solution)/shard_map/ppermute | solution.py:39
  63.7 1.8 %collective-permute-done.12.refs_4_ = f32[8,128]{1,0:T(8,128)S(1)} collective-permute-done((f32[8,128]{1,0:T(8,128)S(1)}, f32[8,128]{1,0:T(8,128)S(1)}, u32[]{:S(2)}, u32[]{:S(2)}) %collective-permute-start.12) | collective-permute-done | bytes 4128 | tf_op jit(solution)/shard_map/ppermute | solution.py:39
  65.8 3.3 %collective-permute-done.11.refs_3_ = f32[8,128]{1,0:T(8,128)S(1)} collective-permute-done((f32[8,128]{1,0:T(8,128)S(1)}, f32[8,128]{1,0:T(8,128)S(1)}, u32[]{:S(2)}, u32[]{:S(2)}) %collective-permute-start.11) | collective-permute-done | bytes 4128 | tf_op jit(solution)/shard_map/ppermute | solution.py:39
  69.1 4.0 %shard_map.117 = (f32[8,128,128]{2,1,0:T(8,128)S(1)}, f32[8,128,128]{2,1,0:T(8,128)S(1)}, f32[8,128]{1,0:T(8,128)S(1)}) custom-call(s32[8,16]{1,0:T(8,128)} %fusion.3.refs_0_, s32[8]{0:T(128)} %refs_1_.11, f32[8,128]{1,0:T(8,128)S(1)} %add.40.refs_2_, f32[8,128]{1,0:T(8,128)S(1)} %collective-permute-done.11.refs_3_, ...), custom_call_target="tpu_custom_call" | custom-call | tf_op jit(solution)/shard_map/pallas_call | solution.py:354
  73.2 1.2 collective-permute-done.16
  74.3 1.2 collective-permute-start.19
  75.5 0.6 collective-permute-start.18
  76.1 1.7 %collective-permute-start.17 = (f32[8,128]{1,0:T(8,128)S(1)}, f32[8,128]{1,0:T(8,128)S(1)}, u32[]{:S(2)}, u32[]{:S(2)}) collective-permute-start(f32[8,128]{1,0:T(8,128)S(1)} %add.41.refs_0_), channel_id=1, source_target_pairs={{0,2},{1,3},{2,0},{3,1},{4,6},{5,7},{6,4},{7,5},{8,10},{9,11},{10,... | collective-permute-start | bytes 12296 | tf_op jit(solution)/shard_map/ppermute | solution.py:39
  77.8 1.0 collective-permute-done.19.refs_3_
  79.2 0.6 collective-permute-done.17.refs_1_
  80.0 3.8 %collective-permute-start.20 = (bf16[8,128,128]{2,1,0:T(8,128)(2,1)S(1)}, bf16[8,128,128]{2,1,0:T(8,128)(2,1)S(1)}, u32[]{:S(2)}, u32[]{:S(2)}) collective-permute-start(bf16[8,128,128]{2,1,0:T(8,128)(2,1)S(1)} %shard_map.118), channel_id=1, source_target_pairs={{0,8},{8,16},{16,24},{1,9},{9,17},{17,25},{2,10},{10,18},{18,26},{... | collective-permute-start | bytes 786440 | tf_op jit(solution)/shard_map/ppermute | solution.py:485
  83.9 3.3 %shard_map.119 = (f32[8,128,128]{2,1,0:T(8,128)S(1)}, bf16[8,2048,128]{2,1,0:T(8,128)(2,1)S(1)}) custom-call(s32[8,16]{1,0:T(8,128)} %fusion.3.refs_0_, s32[8]{0:T(128)} %refs_1_.11, bf16[8,128,128]{2,1,0:T(8,128)(2,1)S(1)} %get-tuple-element.69.refs_2_.refs_11_, bf16[8,128,128]{2,1,0:T(8,128)(2,1)S(1)} %get-tuple-element.67.refs_3_.refs_12_, ...), custom_call_target="tpu_custom_call" | custom-call | tf_op jit(solution)/shard_map/pallas_call | solution.py:354
  87.2 1.3 collective-permute-done.20.refs_1_
  88.5 6.0 %shard_map.120 = (f32[8,128,128]{2,1,0:T(8,128)S(1)}, bf16[8,128,128]{2,1,0:T(8,128)(2,1)S(1)}, f32[8,128]{1,0:T(8,128)S(1)}, bf16[8,16,128,128]{3,2,1,0:T(8,128)(2,1)S(1)}) custom-call(s32[8]{0:T(128)} %refs_1_.11, bf16[8,128,128]{2,1,0:T(8,128)(2,1)S(1)} %collective-permute-done.20.refs_1_, bf16[8,16,128,128]{3,2,1,0:T(8,128)(2,1)S(1)} %bitcast.30, ...), custom_call_target="tpu_custom_call" | custom-call | tf_op jit(solution)/shard_map/pallas_call | solution.py:354
  94.5 0.7 collective-permute-start.28
  95.2 2.6 %collective-permute-start.27 = (bf16[8,128,128]{2,1,0:T(8,128)(2,1)S(1)}, bf16[8,128,128]{2,1,0:T(8,128)(2,1)S(1)}, u32[]{:S(2)}, u32[]{:S(2)}) collective-permute-start(bf16[8,128,128]{2,1,0:T(8,128)(2,1)S(1)} %get-tuple-element.56), channel_id=1, source_target_pairs={{0,1},{1,0},{2,3},{3,2},{4,5},{5,4},{6,7},{7,6},{8,9},{9,8},{10,11... | collective-permute-start | bytes 786440 | tf_op jit(solution)/shard_map/ppermute | solution.py:28
  97.9 1.1 collective-permute-done.23
  98.9 1.4 %collective-permute-start.26 = (f32[8,128]{1,0:T(8,128)S(1)}, f32[8,128]{1,0:T(8,128)S(1)}, u32[]{:S(2)}, u32[]{:S(2)}) collective-permute-start(f32[8,128]{1,0:T(8,128)S(1)} %add.42.refs_2_), channel_id=1, source_target_pairs={{0,6},{1,7},{2,4},{3,5},{4,2},{5,3},{6,0},{7,1},{8,14},{9,15},{10,... | collective-permute-start | bytes 12296 | tf_op jit(solution)/shard_map/ppermute | solution.py:39
  100.4 1.5 %collective-permute-start.25 = (f32[8,128]{1,0:T(8,128)S(1)}, f32[8,128]{1,0:T(8,128)S(1)}, u32[]{:S(2)}, u32[]{:S(2)}) collective-permute-start(f32[8,128]{1,0:T(8,128)S(1)} %add.42.refs_2_), channel_id=1, source_target_pairs={{0,4},{1,5},{2,6},{3,7},{4,0},{5,1},{6,2},{7,3},{8,12},{9,13},{10,... | collective-permute-start | bytes 12296 | tf_op jit(solution)/shard_map/ppermute | solution.py:39
  101.9 0.6 collective-permute-start.24
  102.4 1.0 collective-permute-done.26.refs_5_
  103.5 0.5 collective-permute-done.25.refs_4_
  104.0 1.5 %collective-permute-done.24.refs_3_ = f32[8,128]{1,0:T(8,128)S(1)} collective-permute-done((f32[8,128]{1,0:T(8,128)S(1)}, f32[8,128]{1,0:T(8,128)S(1)}, u32[]{:S(2)}, u32[]{:S(2)}) %collective-permute-start.24) | collective-permute-done | bytes 4128 | tf_op jit(solution)/shard_map/ppermute | solution.py:39
  105.5 3.6 %shard_map.122 = (f32[8,128,128]{2,1,0:T(8,128)S(1)}, f32[8,128,128]{2,1,0:T(8,128)S(1)}, bf16[8,128,128]{2,1,0:T(8,128)(2,1)S(1)}, f32[8,128]{1,0:T(8,128)S(1)}...) custom-call(s32[8,16]{1,0:T(8,128)} %fusion.3.refs_0_, s32[8]{0:T(128)} %refs_1_.11, f32[8,128]{1,0:T(8,128)S(1)} %add.42.refs_2_, ...), custom_call_target="tpu_custom_call" | custom-call | tf_op jit(solution)/shard_map/pallas_call | solution.py:354
  109.1 0.9 collective-permute-start.34
  110.0 2.0 %collective-permute-start.33 = (bf16[8,128,128]{2,1,0:T(8,128)(2,1)S(1)}, bf16[8,128,128]{2,1,0:T(8,128)(2,1)S(1)}, u32[]{:S(2)}, u32[]{:S(2)}) collective-permute-start(bf16[8,128,128]{2,1,0:T(8,128)(2,1)S(1)} %get-tuple-element.62), channel_id=1, source_target_pairs={{0,1},{1,0},{2,3},{3,2},{4,5},{5,4},{6,7},{7,6},{8,9},{9,8},{10,11... | collective-permute-start | bytes 786440 | tf_op jit(solution)/shard_map/ppermute | solution.py:28
  112.1 1.1 collective-permute-done.29
  113.2 1.7 %collective-permute-start.32 = (f32[8,128]{1,0:T(8,128)S(1)}, f32[8,128]{1,0:T(8,128)S(1)}, u32[]{:S(2)}, u32[]{:S(2)}) collective-permute-start(f32[8,128]{1,0:T(8,128)S(1)} %add.43.refs_2_), channel_id=1, source_target_pairs={{0,6},{1,7},{2,4},{3,5},{4,2},{5,3},{6,0},{7,1},{8,14},{9,15},{10,... | collective-permute-start | bytes 12296 | tf_op jit(solution)/shard_map/ppermute | solution.py:39
  114.8 1.5 %collective-permute-start.31 = (f32[8,128]{1,0:T(8,128)S(1)}, f32[8,128]{1,0:T(8,128)S(1)}, u32[]{:S(2)}, u32[]{:S(2)}) collective-permute-start(f32[8,128]{1,0:T(8,128)S(1)} %add.43.refs_2_), channel_id=1, source_target_pairs={{0,4},{1,5},{2,6},{3,7},{4,0},{5,1},{6,2},{7,3},{8,12},{9,13},{10,... | collective-permute-start | bytes 12296 | tf_op jit(solution)/shard_map/ppermute | solution.py:39
  116.6 1.0 collective-permute-done.32.refs_5_
  117.7 0.8 collective-permute-done.31.refs_4_
  118.4 1.5 %collective-permute-done.30.refs_3_ = f32[8,128]{1,0:T(8,128)S(1)} collective-permute-done((f32[8,128]{1,0:T(8,128)S(1)}, f32[8,128]{1,0:T(8,128)S(1)}, u32[]{:S(2)}, u32[]{:S(2)}) %collective-permute-start.30) | collective-permute-done | bytes 4128 | tf_op jit(solution)/shard_map/ppermute | solution.py:39
  119.9 3.8 %shard_map.123 = (f32[8,128,128]{2,1,0:T(8,128)S(1)}, f32[8,128,128]{2,1,0:T(8,128)S(1)}, f32[8,128]{1,0:T(8,128)S(1)}) custom-call(s32[8,16]{1,0:T(8,128)} %fusion.3.refs_0_, s32[8]{0:T(128)} %refs_1_.11, f32[8,128]{1,0:T(8,128)S(1)} %add.43.refs_2_, f32[8,128]{1,0:T(8,128)S(1)} %collective-permute-done.30.refs_3_, ...), custom_call_target="tpu_custom_call" | custom-call | tf_op jit(solution)/shard_map/pallas_call | solution.py:354
  123.8 1.2 collective-permute-done.35
  125.0 1.6 %collective-permute-start.38 = (f32[8,128]{1,0:T(8,128)S(1)}, f32[8,128]{1,0:T(8,128)S(1)}, u32[]{:S(2)}, u32[]{:S(2)}) collective-permute-start(f32[8,128]{1,0:T(8,128)S(1)} %add.44.refs_0_), channel_id=1, source_target_pairs={{0,6},{1,7},{2,4},{3,5},{4,2},{5,3},{6,0},{7,1},{8,14},{9,15},{10,... | collective-permute-start | bytes 12296 | tf_op jit(solution)/shard_map/ppermute | solution.py:39
  126.6 1.4 %collective-permute-start.37 = (f32[8,128]{1,0:T(8,128)S(1)}, f32[8,128]{1,0:T(8,128)S(1)}, u32[]{:S(2)}, u32[]{:S(2)}) collective-permute-start(f32[8,128]{1,0:T(8,128)S(1)} %add.44.refs_0_), channel_id=1, source_target_pairs={{0,4},{1,5},{2,6},{3,7},{4,0},{5,1},{6,2},{7,3},{8,12},{9,13},{10,... | collective-permute-start | bytes 12296 | tf_op jit(solution)/shard_map/ppermute | solution.py:39
  128.0 0.5 collective-permute-start.36
  128.5 1.0 shard_map.121
  129.5 0.7 collective-permute-done.37.refs_2_
  130.2 1.4 %collective-permute-done.36.refs_1_ = f32[8,128]{1,0:T(8,128)S(1)} collective-permute-done((f32[8,128]{1,0:T(8,128)S(1)}, f32[8,128]{1,0:T(8,128)S(1)}, u32[]{:S(2)}, u32[]{:S(2)}) %collective-permute-start.36) | collective-permute-done | bytes 4128 | tf_op jit(solution)/shard_map/ppermute | solution.py:39
  131.6 1.0 shard_map.124
  (49 shorter events, 1.8 us)
Async XLA Ops:
  1.8 11.6 %collective-permute-start.1 = (bf16[8,128,128]{2,1,0:T(8,128)(2,1)S(1)}, bf16[8,128,128]{2,1,0:T(8,128)(2,1)S(1)}, u32[]{:S(2)}, u32[]{:S(2)}) collective-permute-start(bf16[8,128,128]{2,1,0:T(8,128)(2,1)S(1)} %get-tuple-element.34.refs_1_), channel_id=1, source_target_pairs={{1,2},{2,1},{3,4},{4,3},{5,6},{6,5},{9,10},{10,9},{11,12},{12,11},... | collective-permute-start | bytes 786440 | tf_op jit(solution)/shard_map/ppermute | solution.py:27
  2.5 10.9 %collective-permute-start = (bf16[8,128,128]{2,1,0:T(8,128)(2,1)S(1)}, bf16[8,128,128]{2,1,0:T(8,128)(2,1)S(1)}, u32[]{:S(2)}, u32[]{:S(2)}) collective-permute-start(bf16[8,128,128]{2,1,0:T(8,128)(2,1)S(1)} %get-tuple-element.34.refs_1_), channel_id=1, source_target_pairs={{0,1},{1,0},{2,3},{3,2},{4,5},{5,4},{6,7},{7,6},{8,9},{9,8},{10,11... | collective-permute-start | bytes 786440 | tf_op jit(solution)/shard_map/ppermute | solution.py:28
  8.5 15.5 %collective-permute-start.9 = (bf16[8,128,128]{2,1,0:T(8,128)(2,1)S(1)}, bf16[8,128,128]{2,1,0:T(8,128)(2,1)S(1)}, u32[]{:S(2)}, u32[]{:S(2)}) collective-permute-start(bf16[8,128,128]{2,1,0:T(8,128)(2,1)S(1)} %get-tuple-element.39), channel_id=1, source_target_pairs={{1,2},{2,1},{3,4},{4,3},{5,6},{6,5},{9,10},{10,9},{11,12},{12,11},... | collective-permute-start | bytes 786440 | tf_op jit(solution)/shard_map/ppermute | solution.py:27
  9.2 19.7 %collective-permute-start.8 = (bf16[8,128,128]{2,1,0:T(8,128)(2,1)S(1)}, bf16[8,128,128]{2,1,0:T(8,128)(2,1)S(1)}, u32[]{:S(2)}, u32[]{:S(2)}) collective-permute-start(bf16[8,128,128]{2,1,0:T(8,128)(2,1)S(1)} %get-tuple-element.39), channel_id=1, source_target_pairs={{0,1},{1,0},{2,3},{3,2},{4,5},{5,4},{6,7},{7,6},{8,9},{9,8},{10,11... | collective-permute-start | bytes 786440 | tf_op jit(solution)/shard_map/ppermute | solution.py:28
  13.4 35.0 %copy-start = (bf16[1,8,16,128,128]{4,3,2,1,0:T(8,128)(2,1)S(1)}, bf16[1,8,16,128,128]{4,3,2,1,0:T(8,128)(2,1)}, u32[]{:S(2)}) copy-start(bf16[1,8,16,128,128]{4,3,2,1,0:T(8,128)(2,1)} %param.14) | copy-start | bytes 12582916
  13.4 35.0 %copy-start.1 = (bf16[1,8,16,128,128]{4,3,2,1,0:T(8,128)(2,1)S(1)}, bf16[1,8,16,128,128]{4,3,2,1,0:T(8,128)(2,1)}, u32[]{:S(2)}) copy-start(bf16[1,8,16,128,128]{4,3,2,1,0:T(8,128)(2,1)} %param.15) | copy-start | bytes 12582916
  13.4 35.0 %copy-start.3 = (f32[1,8,128,128]{3,2,1,0:T(8,128)S(1)}, f32[1,8,128,128]{3,2,1,0:T(8,128)}, u32[]{:S(2)}) copy-start(f32[1,8,128,128]{3,2,1,0:T(8,128)} %param.12) | copy-start | bytes 1572868
  18.4 30.0 %collective-permute-start.7 = (bf16[8,128,128]{2,1,0:T(8,128)(2,1)S(1)}, bf16[8,128,128]{2,1,0:T(8,128)(2,1)S(1)}, u32[]{:S(2)}, u32[]{:S(2)}) collective-permute-start(bf16[8,128,128]{2,1,0:T(8,128)(2,1)S(1)} %get-tuple-element.38), channel_id=1, source_target_pairs={{1,2},{2,1},{3,4},{4,3},{5,6},{6,5},{9,10},{10,9},{11,12},{12,11},... | collective-permute-start | bytes 786440 | tf_op jit(solution)/shard_map/ppermute | solution.py:27
  19.2 29.2 %collective-permute-start.6 = (bf16[8,128,128]{2,1,0:T(8,128)(2,1)S(1)}, bf16[8,128,128]{2,1,0:T(8,128)(2,1)S(1)}, u32[]{:S(2)}, u32[]{:S(2)}) collective-permute-start(bf16[8,128,128]{2,1,0:T(8,128)(2,1)S(1)} %get-tuple-element.38), channel_id=1, source_target_pairs={{0,1},{1,0},{2,3},{3,2},{4,5},{5,4},{6,7},{7,6},{8,9},{9,8},{10,11... | collective-permute-start | bytes 786440 | tf_op jit(solution)/shard_map/ppermute | solution.py:28
  22.1 1.2 collective-permute-start.2
  23.3 60.5 %collective-permute-start.22 = (bf16[16,128,128]{2,1,0:T(8,128)(2,1)S(1)}, bf16[16,128,128]{2,1,0:T(8,128)(2,1)S(1)}, u32[]{:S(2)}, u32[]{:S(2)}) collective-permute-start(bf16[16,128,128]{2,1,0:T(8,128)(2,1)S(1)} %get-tuple-element.49), channel_id=1, source_target_pairs={{1,2},{2,1},{3,4},{4,3},{5,6},{6,5},{9,10},{10,9},{11,12},{12,11},... | collective-permute-start | bytes 1572872 | tf_op jit(solution)/shard_map/ppermute | solution.py:27
  24.0 12.0 %collective-permute-start.5 = (f32[8,128]{1,0:T(8,128)S(1)}, f32[8,128]{1,0:T(8,128)S(1)}, u32[]{:S(2)}, u32[]{:S(2)}) collective-permute-start(f32[8,128]{1,0:T(8,128)S(1)} %add.39.refs_2_), channel_id=1, source_target_pairs={{0,6},{1,7},{2,4},{3,5},{4,2},{5,3},{6,0},{7,1},{8,14},{9,15},{10,... | collective-permute-start | bytes 12296 | tf_op jit(solution)/shard_map/ppermute | solution.py:39
  28.9 54.9 %collective-permute-start.21 = (bf16[16,128,128]{2,1,0:T(8,128)(2,1)S(1)}, bf16[16,128,128]{2,1,0:T(8,128)(2,1)S(1)}, u32[]{:S(2)}, u32[]{:S(2)}) collective-permute-start(bf16[16,128,128]{2,1,0:T(8,128)(2,1)S(1)} %get-tuple-element.49), channel_id=1, source_target_pairs={{0,1},{1,0},{2,3},{3,2},{4,5},{5,4},{6,7},{7,6},{8,9},{9,8},{10,11... | collective-permute-start | bytes 1572872 | tf_op jit(solution)/shard_map/ppermute | solution.py:28
  36.0 6.8 %collective-permute-start.4 = (f32[8,128]{1,0:T(8,128)S(1)}, f32[8,128]{1,0:T(8,128)S(1)}, u32[]{:S(2)}, u32[]{:S(2)}) collective-permute-start(f32[8,128]{1,0:T(8,128)S(1)} %add.39.refs_2_), channel_id=1, source_target_pairs={{0,4},{1,5},{2,6},{3,7},{4,0},{5,1},{6,2},{7,3},{8,12},{9,13},{10,... | collective-permute-start | bytes 12296 | tf_op jit(solution)/shard_map/ppermute | solution.py:39
  42.8 5.5 %collective-permute-start.3 = (f32[8,128]{1,0:T(8,128)S(1)}, f32[8,128]{1,0:T(8,128)S(1)}, u32[]{:S(2)}, u32[]{:S(2)}) collective-permute-start(f32[8,128]{1,0:T(8,128)S(1)} %add.39.refs_2_), channel_id=1, source_target_pairs={{0,2},{1,3},{2,0},{3,1},{4,6},{5,7},{6,4},{7,5},{8,10},{9,11},{10,... | collective-permute-start | bytes 12296 | tf_op jit(solution)/shard_map/ppermute | solution.py:39
  52.1 17.0 %collective-permute-start.15 = (bf16[8,128,128]{2,1,0:T(8,128)(2,1)S(1)}, bf16[8,128,128]{2,1,0:T(8,128)(2,1)S(1)}, u32[]{:S(2)}, u32[]{:S(2)}) collective-permute-start(bf16[8,128,128]{2,1,0:T(8,128)(2,1)S(1)} %get-tuple-element.45), channel_id=1, source_target_pairs={{1,2},{2,1},{3,4},{4,3},{5,6},{6,5},{9,10},{10,9},{11,12},{12,11},... | collective-permute-start | bytes 786440 | tf_op jit(solution)/shard_map/ppermute | solution.py:27
  52.8 16.3 %collective-permute-start.14 = (bf16[8,128,128]{2,1,0:T(8,128)(2,1)S(1)}, bf16[8,128,128]{2,1,0:T(8,128)(2,1)S(1)}, u32[]{:S(2)}, u32[]{:S(2)}) collective-permute-start(bf16[8,128,128]{2,1,0:T(8,128)(2,1)S(1)} %get-tuple-element.45), channel_id=1, source_target_pairs={{0,1},{1,0},{2,3},{3,2},{4,5},{5,4},{6,7},{7,6},{8,9},{9,8},{10,11... | collective-permute-start | bytes 786440 | tf_op jit(solution)/shard_map/ppermute | solution.py:28
  56.2 1.2 collective-permute-start.10
  57.4 4.5 %collective-permute-start.13 = (f32[8,128]{1,0:T(8,128)S(1)}, f32[8,128]{1,0:T(8,128)S(1)}, u32[]{:S(2)}, u32[]{:S(2)}) collective-permute-start(f32[8,128]{1,0:T(8,128)S(1)} %add.40.refs_2_), channel_id=1, source_target_pairs={{0,6},{1,7},{2,4},{3,5},{4,2},{5,3},{6,0},{7,1},{8,14},{9,15},{10,... | collective-permute-start | bytes 12296 | tf_op jit(solution)/shard_map/ppermute | solution.py:39
  61.9 3.6 %collective-permute-start.12 = (f32[8,128]{1,0:T(8,128)S(1)}, f32[8,128]{1,0:T(8,128)S(1)}, u32[]{:S(2)}, u32[]{:S(2)}) collective-permute-start(f32[8,128]{1,0:T(8,128)S(1)} %add.40.refs_2_), channel_id=1, source_target_pairs={{0,4},{1,5},{2,6},{3,7},{4,0},{5,1},{6,2},{7,3},{8,12},{9,13},{10,... | collective-permute-start | bytes 12296 | tf_op jit(solution)/shard_map/ppermute | solution.py:39
  65.5 3.6 %collective-permute-start.11 = (f32[8,128]{1,0:T(8,128)S(1)}, f32[8,128]{1,0:T(8,128)S(1)}, u32[]{:S(2)}, u32[]{:S(2)}) collective-permute-start(f32[8,128]{1,0:T(8,128)S(1)} %add.40.refs_2_), channel_id=1, source_target_pairs={{0,2},{1,3},{2,0},{3,1},{4,6},{5,7},{6,4},{7,5},{8,10},{9,11},{10,... | collective-permute-start | bytes 12296 | tf_op jit(solution)/shard_map/ppermute | solution.py:39
  69.1 14.8 %copy-start.2 = (bf16[1,8,16,128,128]{4,3,2,1,0:T(8,128)(2,1)S(1)}, bf16[1,8,16,128,128]{4,3,2,1,0:T(8,128)(2,1)}, u32[]{:S(2)}) copy-start(bf16[1,8,16,128,128]{4,3,2,1,0:T(8,128)(2,1)} %param.17) | copy-start | bytes 12582916
  73.1 10.8 %copy-start.6 = (f32[1,8,128,128]{3,2,1,0:T(8,128)S(1)}, f32[1,8,128,128]{3,2,1,0:T(8,128)}, u32[]{:S(2)}) copy-start(f32[1,8,128,128]{3,2,1,0:T(8,128)} %param.11) | copy-start | bytes 1572868
  73.1 1.2 collective-permute-start.16
  74.3 4.5 %collective-permute-start.19 = (f32[8,128]{1,0:T(8,128)S(1)}, f32[8,128]{1,0:T(8,128)S(1)}, u32[]{:S(2)}, u32[]{:S(2)}) collective-permute-start(f32[8,128]{1,0:T(8,128)S(1)} %add.41.refs_0_), channel_id=1, source_target_pairs={{0,6},{1,7},{2,4},{3,5},{4,2},{5,3},{6,0},{7,1},{8,14},{9,15},{10,... | collective-permute-start | bytes 12296 | tf_op jit(solution)/shard_map/ppermute | solution.py:39
  75.5 3.6 %collective-permute-start.18 = (f32[8,128]{1,0:T(8,128)S(1)}, f32[8,128]{1,0:T(8,128)S(1)}, u32[]{:S(2)}, u32[]{:S(2)}) collective-permute-start(f32[8,128]{1,0:T(8,128)S(1)} %add.41.refs_0_), channel_id=1, source_target_pairs={{0,4},{1,5},{2,6},{3,7},{4,0},{5,1},{6,2},{7,3},{8,12},{9,13},{10,... | collective-permute-start | bytes 12296 | tf_op jit(solution)/shard_map/ppermute | solution.py:39
  76.1 3.6 %collective-permute-start.17 = (f32[8,128]{1,0:T(8,128)S(1)}, f32[8,128]{1,0:T(8,128)S(1)}, u32[]{:S(2)}, u32[]{:S(2)}) collective-permute-start(f32[8,128]{1,0:T(8,128)S(1)} %add.41.refs_0_), channel_id=1, source_target_pairs={{0,2},{1,3},{2,0},{3,1},{4,6},{5,7},{6,4},{7,5},{8,10},{9,11},{10,... | collective-permute-start | bytes 12296 | tf_op jit(solution)/shard_map/ppermute | solution.py:39
  79.7 8.8 %copy-start.4 = (f32[1,8,128,128]{3,2,1,0:T(8,128)S(1)}, f32[1,8,128,128]{3,2,1,0:T(8,128)}, u32[]{:S(2)}) copy-start(f32[1,8,128,128]{3,2,1,0:T(8,128)} %param.13) | copy-start | bytes 1572868
  79.7 8.8 %copy-start.5 = (bf16[1,8,16,128,128]{4,3,2,1,0:T(8,128)(2,1)S(1)}, bf16[1,8,16,128,128]{4,3,2,1,0:T(8,128)(2,1)}, u32[]{:S(2)}) copy-start(bf16[1,8,16,128,128]{4,3,2,1,0:T(8,128)(2,1)} %param.16) | copy-start | bytes 12582916
  80.0 8.5 %collective-permute-start.20 = (bf16[8,128,128]{2,1,0:T(8,128)(2,1)S(1)}, bf16[8,128,128]{2,1,0:T(8,128)(2,1)S(1)}, u32[]{:S(2)}, u32[]{:S(2)}) collective-permute-start(bf16[8,128,128]{2,1,0:T(8,128)(2,1)S(1)} %shard_map.118), channel_id=1, source_target_pairs={{0,8},{8,16},{16,24},{1,9},{9,17},{17,25},{2,10},{10,18},{18,26},{... | collective-permute-start | bytes 786440 | tf_op jit(solution)/shard_map/ppermute | solution.py:485
  94.5 11.0 %collective-permute-start.28 = (bf16[8,128,128]{2,1,0:T(8,128)(2,1)S(1)}, bf16[8,128,128]{2,1,0:T(8,128)(2,1)S(1)}, u32[]{:S(2)}, u32[]{:S(2)}) collective-permute-start(bf16[8,128,128]{2,1,0:T(8,128)(2,1)S(1)} %get-tuple-element.56), channel_id=1, source_target_pairs={{1,2},{2,1},{3,4},{4,3},{5,6},{6,5},{9,10},{10,9},{11,12},{12,11},... | collective-permute-start | bytes 786440 | tf_op jit(solution)/shard_map/ppermute | solution.py:27
  95.2 10.3 %collective-permute-start.27 = (bf16[8,128,128]{2,1,0:T(8,128)(2,1)S(1)}, bf16[8,128,128]{2,1,0:T(8,128)(2,1)S(1)}, u32[]{:S(2)}, u32[]{:S(2)}) collective-permute-start(bf16[8,128,128]{2,1,0:T(8,128)(2,1)S(1)} %get-tuple-element.56), channel_id=1, source_target_pairs={{0,1},{1,0},{2,3},{3,2},{4,5},{5,4},{6,7},{7,6},{8,9},{9,8},{10,11... | collective-permute-start | bytes 786440 | tf_op jit(solution)/shard_map/ppermute | solution.py:28
  97.8 1.2 collective-permute-start.23
  98.9 4.5 %collective-permute-start.26 = (f32[8,128]{1,0:T(8,128)S(1)}, f32[8,128]{1,0:T(8,128)S(1)}, u32[]{:S(2)}, u32[]{:S(2)}) collective-permute-start(f32[8,128]{1,0:T(8,128)S(1)} %add.42.refs_2_), channel_id=1, source_target_pairs={{0,6},{1,7},{2,4},{3,5},{4,2},{5,3},{6,0},{7,1},{8,14},{9,15},{10,... | collective-permute-start | bytes 12296 | tf_op jit(solution)/shard_map/ppermute | solution.py:39
  100.4 3.6 %collective-permute-start.25 = (f32[8,128]{1,0:T(8,128)S(1)}, f32[8,128]{1,0:T(8,128)S(1)}, u32[]{:S(2)}, u32[]{:S(2)}) collective-permute-start(f32[8,128]{1,0:T(8,128)S(1)} %add.42.refs_2_), channel_id=1, source_target_pairs={{0,4},{1,5},{2,6},{3,7},{4,0},{5,1},{6,2},{7,3},{8,12},{9,13},{10,... | collective-permute-start | bytes 12296 | tf_op jit(solution)/shard_map/ppermute | solution.py:39
  101.9 3.6 %collective-permute-start.24 = (f32[8,128]{1,0:T(8,128)S(1)}, f32[8,128]{1,0:T(8,128)S(1)}, u32[]{:S(2)}, u32[]{:S(2)}) collective-permute-start(f32[8,128]{1,0:T(8,128)S(1)} %add.42.refs_2_), channel_id=1, source_target_pairs={{0,2},{1,3},{2,0},{3,1},{4,6},{5,7},{6,4},{7,5},{8,10},{9,11},{10,... | collective-permute-start | bytes 12296 | tf_op jit(solution)/shard_map/ppermute | solution.py:39
  109.1 10.8 %collective-permute-start.34 = (bf16[8,128,128]{2,1,0:T(8,128)(2,1)S(1)}, bf16[8,128,128]{2,1,0:T(8,128)(2,1)S(1)}, u32[]{:S(2)}, u32[]{:S(2)}) collective-permute-start(bf16[8,128,128]{2,1,0:T(8,128)(2,1)S(1)} %get-tuple-element.62), channel_id=1, source_target_pairs={{1,2},{2,1},{3,4},{4,3},{5,6},{6,5},{9,10},{10,9},{11,12},{12,11},... | collective-permute-start | bytes 786440 | tf_op jit(solution)/shard_map/ppermute | solution.py:27
  110.0 9.9 %collective-permute-start.33 = (bf16[8,128,128]{2,1,0:T(8,128)(2,1)S(1)}, bf16[8,128,128]{2,1,0:T(8,128)(2,1)S(1)}, u32[]{:S(2)}, u32[]{:S(2)}) collective-permute-start(bf16[8,128,128]{2,1,0:T(8,128)(2,1)S(1)} %get-tuple-element.62), channel_id=1, source_target_pairs={{0,1},{1,0},{2,3},{3,2},{4,5},{5,4},{6,7},{7,6},{8,9},{9,8},{10,11... | collective-permute-start | bytes 786440 | tf_op jit(solution)/shard_map/ppermute | solution.py:28
  112.0 1.2 collective-permute-start.29
  113.2 4.5 %collective-permute-start.32 = (f32[8,128]{1,0:T(8,128)S(1)}, f32[8,128]{1,0:T(8,128)S(1)}, u32[]{:S(2)}, u32[]{:S(2)}) collective-permute-start(f32[8,128]{1,0:T(8,128)S(1)} %add.43.refs_2_), channel_id=1, source_target_pairs={{0,6},{1,7},{2,4},{3,5},{4,2},{5,3},{6,0},{7,1},{8,14},{9,15},{10,... | collective-permute-start | bytes 12296 | tf_op jit(solution)/shard_map/ppermute | solution.py:39
  114.8 3.6 %collective-permute-start.31 = (f32[8,128]{1,0:T(8,128)S(1)}, f32[8,128]{1,0:T(8,128)S(1)}, u32[]{:S(2)}, u32[]{:S(2)}) collective-permute-start(f32[8,128]{1,0:T(8,128)S(1)} %add.43.refs_2_), channel_id=1, source_target_pairs={{0,4},{1,5},{2,6},{3,7},{4,0},{5,1},{6,2},{7,3},{8,12},{9,13},{10,... | collective-permute-start | bytes 12296 | tf_op jit(solution)/shard_map/ppermute | solution.py:39
  116.3 3.6 %collective-permute-start.30 = (f32[8,128]{1,0:T(8,128)S(1)}, f32[8,128]{1,0:T(8,128)S(1)}, u32[]{:S(2)}, u32[]{:S(2)}) collective-permute-start(f32[8,128]{1,0:T(8,128)S(1)} %add.43.refs_2_), channel_id=1, source_target_pairs={{0,2},{1,3},{2,0},{3,1},{4,6},{5,7},{6,4},{7,5},{8,10},{9,11},{10,... | collective-permute-start | bytes 12296 | tf_op jit(solution)/shard_map/ppermute | solution.py:39
  123.8 1.2 collective-permute-start.35
  125.0 4.5 %collective-permute-start.38 = (f32[8,128]{1,0:T(8,128)S(1)}, f32[8,128]{1,0:T(8,128)S(1)}, u32[]{:S(2)}, u32[]{:S(2)}) collective-permute-start(f32[8,128]{1,0:T(8,128)S(1)} %add.44.refs_0_), channel_id=1, source_target_pairs={{0,6},{1,7},{2,4},{3,5},{4,2},{5,3},{6,0},{7,1},{8,14},{9,15},{10,... | collective-permute-start | bytes 12296 | tf_op jit(solution)/shard_map/ppermute | solution.py:39
  126.6 3.6 %collective-permute-start.37 = (f32[8,128]{1,0:T(8,128)S(1)}, f32[8,128]{1,0:T(8,128)S(1)}, u32[]{:S(2)}, u32[]{:S(2)}) collective-permute-start(f32[8,128]{1,0:T(8,128)S(1)} %add.44.refs_0_), channel_id=1, source_target_pairs={{0,4},{1,5},{2,6},{3,7},{4,0},{5,1},{6,2},{7,3},{8,12},{9,13},{10,... | collective-permute-start | bytes 12296 | tf_op jit(solution)/shard_map/ppermute | solution.py:39
  128.0 3.6 %collective-permute-start.36 = (f32[8,128]{1,0:T(8,128)S(1)}, f32[8,128]{1,0:T(8,128)S(1)}, u32[]{:S(2)}, u32[]{:S(2)}) collective-permute-start(f32[8,128]{1,0:T(8,128)S(1)} %add.44.refs_0_), channel_id=1, source_target_pairs={{0,2},{1,3},{2,0},{3,1},{4,6},{5,7},{6,4},{7,5},{8,10},{9,11},{10,... | collective-permute-start | bytes 12296 | tf_op jit(solution)/shard_map/ppermute | solution.py:39

commit v3 on v2

--- a/solution.py
+++ b/solution.py
@@ -200,10 +200,12 @@
     lax.fori_loop(0, blocks, body, 0)
 
 
-def build_kernel(ready, dims, handed, base, y, u, onsite, term, sent, stats, left, acc, *works):
+def build_kernel(ready, dims, handed, base, y, u, onsite, term, sent, stats, left, acc, flip, *works):
     blocks, terms, width, _ = base.shape
     lanes = len(works)
     acc[...] = jnp.zeros_like(acc)
+    for b in range(blocks):
+        flip[b] = (handed[b].astype(F32).T * (1.0 / width)).astype(BF16)
     ready()
 
     def body(i, carry):
@@ -211,7 +213,7 @@
             b = i * lanes + j
             work = works[j]
             block = handed[b]
-            flipped = (block.astype(F32).T * (1.0 / width)).astype(BF16)
+            flipped = flip[b]
             carried = jnp.dot(
                 base[b].reshape(terms * width, width), block, preferred_element_type=F32
             )
@@ -498,7 +500,7 @@
         [block_dims],
         [handed, left_base, y, u, onsite_second],
         [like(vec, F32), like(vec, BF16), stats_shape, like(left_base.shape, BF16)],
-        [acc_shape] + [pltpu.VMEM((terms * width, width), BF16)] * lanes,
+        [acc_shape, pltpu.VMEM(vec, BF16)] + [pltpu.VMEM((terms * width, width), BF16)] * lanes,
     )
     u_first, term_first, parts_first, onsite = ended
     result_first = final(after(u_first, stats), term_first, parts_first, onsite, False)

time: 133 us -> 133 us (level)
  no operation moved by 1% of the time
where the time goes in v3:
time: 133 us
  starting transfers between devices  57.6 us (43%)
  waiting for transfers between devices  38.2 us (29%)
  Pallas kernels  34.5 us (26%)
    pallas_call x12, Pallas kernels, call(): pl.pallas_call(body if count else kernel, out_shape=outs, in_specs=[HBM]...  34.5 us
    ppermute x18, waiting for transfers between devices, gathered_parts(): parts += [lax.ppermute(pair, 'sec', [(i, i ^ 2 * m) for i in range(count)])]  30.2 us
    ppermute x18, starting transfers between devices, gathered_parts(): parts += [lax.ppermute(pair, 'sec', [(i, i ^ 2 * m) for i in range(count)])]  30.1 us
    ppermute x7, starting transfers between devices, swapped(): even = lax.ppermute(block, 'sec', even_pairs(count))  18.2 us
    ppermute x6, waiting for transfers between devices, gathered_parts(): pair = partial + lax.ppermute(partial, 'sec', even_pairs(count))  6.66 us
    ppermute x7, starting transfers between devices, swapped(): odd = lax.ppermute(block, 'sec', odd_pairs(count))  5.06 us
    ppermute x1, starting transfers between devices, both_updates(): handed = lax.ppermute(handed, 'seg', [(s, s + 1) for s in range(segs - 1)])  3.76 us
  transfers between devices with their start and end apart: 39, of which 24 were waited for; matrix products, arithmetic and copies ran while one was open for 1% of the time, Pallas kernels for 14%

profile of v3, /device:TPU:0, one launch (start us, length us, event | category | flops | bytes accessed | tf_op | source)
XLA Modules:
  0.0 132.8 jit_solution(13402411921974370228)
XLA Ops:
  0.6 1.2 shard_map.113
  1.8 0.7 collective-permute-start.1
  2.5 4.4 %collective-permute-start = (bf16[8,128,128]{2,1,0:T(8,128)(2,1)S(1)}, bf16[8,128,128]{2,1,0:T(8,128)(2,1)S(1)}, u32[]{:S(2)}, u32[]{:S(2)}) collective-permute-start(bf16[8,128,128]{2,1,0:T(8,128)(2,1)S(1)} %get-tuple-element.34.refs_1_), channel_id=1, source_target_pairs={{0,1},{1,0},{2,3},{3,2},{4,5},{5,4},{6,7},{7,6},{8,9},{9,8},{10,11... | collective-permute-start | bytes 786440 | tf_op jit(solution)/shard_map/ppermute | solution.py:28
  6.9 1.6 %shard_map.115 = (bf16[8,128,128]{2,1,0:T(8,128)(2,1)S(1)}, bf16[16,128,128]{2,1,0:T(8,128)(2,1)S(1)}) custom-call(s32[8]{0:T(128)} %refs_1_.11, bf16[8,128,128]{2,1,0:T(8,128)(2,1)S(1)} %get-tuple-element.34.refs_1_, f32[8,128,128]{2,1,0:T(8,128)} %bitcast.19, f32[8,128,128]{2,1,0:T(8,128)} %bitcast.25, f32[8,128,128]{2,1,0:T(8,128)} %bitcast.31), custom_call_target="tpu_custom_call" | custom-call | tf_op jit(solution)/shard_map/pallas_call | solution.py:356
  8.5 0.7 collective-permute-start.9
  9.2 2.9 %collective-permute-start.8 = (bf16[8,128,128]{2,1,0:T(8,128)(2,1)S(1)}, bf16[8,128,128]{2,1,0:T(8,128)(2,1)S(1)}, u32[]{:S(2)}, u32[]{:S(2)}) collective-permute-start(bf16[8,128,128]{2,1,0:T(8,128)(2,1)S(1)} %get-tuple-element.39), channel_id=1, source_target_pairs={{0,1},{1,0},{2,3},{3,2},{4,5},{5,4},{6,7},{7,6},{8,9},{9,8},{10,11... | collective-permute-start | bytes 786440 | tf_op jit(solution)/shard_map/ppermute | solution.py:28
  12.1 1.3 fusion.3.refs_0_
  13.4 5.0 %shard_map.114 = (f32[8,128,128]{2,1,0:T(8,128)S(1)}, bf16[8,128,128]{2,1,0:T(8,128)(2,1)S(1)}, f32[8,128]{1,0:T(8,128)S(1)}) custom-call(s32[8,16]{1,0:T(8,128)} %fusion.3.refs_0_, s32[8]{0:T(128)} %refs_1_.11, bf16[8,128,128]{2,1,0:T(8,128)(2,1)S(1)} %collective-permute-done.refs_2_.refs_11_, ...), custom_call_target="tpu_custom_call" | custom-call | tf_op jit(solution)/shard_map/pallas_call | solution.py:356
  18.4 0.8 collective-permute-start.7
  19.2 2.9 %collective-permute-start.6 = (bf16[8,128,128]{2,1,0:T(8,128)(2,1)S(1)}, bf16[8,128,128]{2,1,0:T(8,128)(2,1)S(1)}, u32[]{:S(2)}, u32[]{:S(2)}) collective-permute-start(bf16[8,128,128]{2,1,0:T(8,128)(2,1)S(1)} %get-tuple-element.38), channel_id=1, source_target_pairs={{0,1},{1,0},{2,3},{3,2},{4,5},{5,4},{6,7},{7,6},{8,9},{9,8},{10,11... | collective-permute-start | bytes 786440 | tf_op jit(solution)/shard_map/ppermute | solution.py:28
  22.2 1.1 collective-permute-done.2
  23.3 0.7 collective-permute-start.22
  24.0 4.9 %collective-permute-start.5 = (f32[8,128]{1,0:T(8,128)S(1)}, f32[8,128]{1,0:T(8,128)S(1)}, u32[]{:S(2)}, u32[]{:S(2)}) collective-permute-start(f32[8,128]{1,0:T(8,128)S(1)} %add.39.refs_2_), channel_id=1, source_target_pairs={{0,6},{1,7},{2,4},{3,5},{4,2},{5,3},{6,0},{7,1},{8,14},{9,15},{10,... | collective-permute-start | bytes 12296 | tf_op jit(solution)/shard_map/ppermute | solution.py:39
  28.9 7.1 %collective-permute-done.5.refs_5_ = f32[8,128]{1,0:T(8,128)S(1)} collective-permute-done((f32[8,128]{1,0:T(8,128)S(1)}, f32[8,128]{1,0:T(8,128)S(1)}, u32[]{:S(2)}, u32[]{:S(2)}) %collective-permute-start.5) | collective-permute-done | bytes 4128 | tf_op jit(solution)/shard_map/ppermute | solution.py:39
  36.0 5.2 %collective-permute-start.4 = (f32[8,128]{1,0:T(8,128)S(1)}, f32[8,128]{1,0:T(8,128)S(1)}, u32[]{:S(2)}, u32[]{:S(2)}) collective-permute-start(f32[8,128]{1,0:T(8,128)S(1)} %add.39.refs_2_), channel_id=1, source_target_pairs={{0,4},{1,5},{2,6},{3,7},{4,0},{5,1},{6,2},{7,3},{8,12},{9,13},{10,... | collective-permute-start | bytes 12296 | tf_op jit(solution)/shard_map/ppermute | solution.py:39
  41.3 1.6 %collective-permute-done.4.refs_4_ = f32[8,128]{1,0:T(8,128)S(1)} collective-permute-done((f32[8,128]{1,0:T(8,128)S(1)}, f32[8,128]{1,0:T(8,128)S(1)}, u32[]{:S(2)}, u32[]{:S(2)}) %collective-permute-start.4) | collective-permute-done | bytes 4128 | tf_op jit(solution)/shard_map/ppermute | solution.py:39
  42.8 3.9 %collective-permute-start.3 = (f32[8,128]{1,0:T(8,128)S(1)}, f32[8,128]{1,0:T(8,128)S(1)}, u32[]{:S(2)}, u32[]{:S(2)}) collective-permute-start(f32[8,128]{1,0:T(8,128)S(1)} %add.39.refs_2_), channel_id=1, source_target_pairs={{0,2},{1,3},{2,0},{3,1},{4,6},{5,7},{6,4},{7,5},{8,10},{9,11},{10,... | collective-permute-start | bytes 12296 | tf_op jit(solution)/shard_map/ppermute | solution.py:39
  46.8 1.6 %collective-permute-done.3.refs_3_ = f32[8,128]{1,0:T(8,128)S(1)} collective-permute-done((f32[8,128]{1,0:T(8,128)S(1)}, f32[8,128]{1,0:T(8,128)S(1)}, u32[]{:S(2)}, u32[]{:S(2)}) %collective-permute-start.3) | collective-permute-done | bytes 4128 | tf_op jit(solution)/shard_map/ppermute | solution.py:39
  48.4 3.7 %shard_map.116 = (f32[8,128,128]{2,1,0:T(8,128)S(1)}, f32[8,128,128]{2,1,0:T(8,128)S(1)}, bf16[8,128,128]{2,1,0:T(8,128)(2,1)S(1)}, f32[8,128]{1,0:T(8,128)S(1)}...) custom-call(s32[8,16]{1,0:T(8,128)} %fusion.3.refs_0_, s32[8]{0:T(128)} %refs_1_.11, f32[8,128]{1,0:T(8,128)S(1)} %add.39.refs_2_, ...), custom_call_target="tpu_custom_call" | custom-call | tf_op jit(solution)/shard_map/pallas_call | solution.py:356
  52.1 0.7 collective-permute-start.15
  52.8 3.4 %collective-permute-start.14 = (bf16[8,128,128]{2,1,0:T(8,128)(2,1)S(1)}, bf16[8,128,128]{2,1,0:T(8,128)(2,1)S(1)}, u32[]{:S(2)}, u32[]{:S(2)}) collective-permute-start(bf16[8,128,128]{2,1,0:T(8,128)(2,1)S(1)} %get-tuple-element.45), channel_id=1, source_target_pairs={{0,1},{1,0},{2,3},{3,2},{4,5},{5,4},{6,7},{7,6},{8,9},{9,8},{10,11... | collective-permute-start | bytes 786440 | tf_op jit(solution)/shard_map/ppermute | solution.py:28
  56.3 1.1 collective-permute-done.10
  57.4 4.5 %collective-permute-done.13.refs_5_ = f32[8,128]{1,0:T(8,128)S(1)} collective-permute-done((f32[8,128]{1,0:T(8,128)S(1)}, f32[8,128]{1,0:T(8,128)S(1)}, u32[]{:S(2)}, u32[]{:S(2)}) %collective-permute-start.13) | collective-permute-done | bytes 4128 | tf_op jit(solution)/shard_map/ppermute | solution.py:39
  61.9 1.8 %collective-permute-start.12 = (f32[8,128]{1,0:T(8,128)S(1)}, f32[8,128]{1,0:T(8,128)S(1)}, u32[]{:S(2)}, u32[]{:S(2)}) collective-permute-start(f32[8,128]{1,0:T(8,128)S(1)} %add.40.refs_2_), channel_id=1, source_target_pairs={{0,4},{1,5},{2,6},{3,7},{4,0},{5,1},{6,2},{7,3},{8,12},{9,13},{10,... | collective-permute-start | bytes 12296 | tf_op jit(solution)/shard_map/ppermute | solution.py:39
  63.7 1.8 %collective-permute-done.12.refs_4_ = f32[8,128]{1,0:T(8,128)S(1)} collective-permute-done((f32[8,128]{1,0:T(8,128)S(1)}, f32[8,128]{1,0:T(8,128)S(1)}, u32[]{:S(2)}, u32[]{:S(2)}) %collective-permute-start.12) | collective-permute-done | bytes 4128 | tf_op jit(solution)/shard_map/ppermute | solution.py:39
  65.8 3.3 %collective-permute-done.11.refs_3_ = f32[8,128]{1,0:T(8,128)S(1)} collective-permute-done((f32[8,128]{1,0:T(8,128)S(1)}, f32[8,128]{1,0:T(8,128)S(1)}, u32[]{:S(2)}, u32[]{:S(2)}) %collective-permute-start.11) | collective-permute-done | bytes 4128 | tf_op jit(solution)/shard_map/ppermute | solution.py:39
  69.1 4.0 %shard_map.117 = (f32[8,128,128]{2,1,0:T(8,128)S(1)}, f32[8,128,128]{2,1,0:T(8,128)S(1)}, f32[8,128]{1,0:T(8,128)S(1)}) custom-call(s32[8,16]{1,0:T(8,128)} %fusion.3.refs_0_, s32[8]{0:T(128)} %refs_1_.11, f32[8,128]{1,0:T(8,128)S(1)} %add.40.refs_2_, f32[8,128]{1,0:T(8,128)S(1)} %collective-permute-done.11.refs_3_, ...), custom_call_target="tpu_custom_call" | custom-call | tf_op jit(solution)/shard_map/pallas_call | solution.py:356
  73.2 1.2 collective-permute-done.16
  74.3 1.2 collective-permute-start.19
  75.5 0.6 collective-permute-start.18
  76.1 1.7 %collective-permute-start.17 = (f32[8,128]{1,0:T(8,128)S(1)}, f32[8,128]{1,0:T(8,128)S(1)}, u32[]{:S(2)}, u32[]{:S(2)}) collective-permute-start(f32[8,128]{1,0:T(8,128)S(1)} %add.41.refs_0_), channel_id=1, source_target_pairs={{0,2},{1,3},{2,0},{3,1},{4,6},{5,7},{6,4},{7,5},{8,10},{9,11},{10,... | collective-permute-start | bytes 12296 | tf_op jit(solution)/shard_map/ppermute | solution.py:39
  77.8 1.0 collective-permute-done.19.refs_3_
  79.2 0.6 collective-permute-done.17.refs_1_
  80.0 3.8 %collective-permute-start.20 = (bf16[8,128,128]{2,1,0:T(8,128)(2,1)S(1)}, bf16[8,128,128]{2,1,0:T(8,128)(2,1)S(1)}, u32[]{:S(2)}, u32[]{:S(2)}) collective-permute-start(bf16[8,128,128]{2,1,0:T(8,128)(2,1)S(1)} %shard_map.118), channel_id=1, source_target_pairs={{0,8},{8,16},{16,24},{1,9},{9,17},{17,25},{2,10},{10,18},{18,26},{... | collective-permute-start | bytes 786440 | tf_op jit(solution)/shard_map/ppermute | solution.py:487
  83.9 3.3 %shard_map.119 = (f32[8,128,128]{2,1,0:T(8,128)S(1)}, bf16[8,2048,128]{2,1,0:T(8,128)(2,1)S(1)}) custom-call(s32[8,16]{1,0:T(8,128)} %fusion.3.refs_0_, s32[8]{0:T(128)} %refs_1_.11, bf16[8,128,128]{2,1,0:T(8,128)(2,1)S(1)} %get-tuple-element.69.refs_2_.refs_11_, bf16[8,128,128]{2,1,0:T(8,128)(2,1)S(1)} %get-tuple-element.67.refs_3_.refs_12_, ...), custom_call_target="tpu_custom_call" | custom-call | tf_op jit(solution)/shard_map/pallas_call | solution.py:356
  87.2 1.3 collective-permute-done.20.refs_1_
  88.5 6.0 %shard_map.120 = (f32[8,128,128]{2,1,0:T(8,128)S(1)}, bf16[8,128,128]{2,1,0:T(8,128)(2,1)S(1)}, f32[8,128]{1,0:T(8,128)S(1)}, bf16[8,16,128,128]{3,2,1,0:T(8,128)(2,1)S(1)}) custom-call(s32[8]{0:T(128)} %refs_1_.11, bf16[8,128,128]{2,1,0:T(8,128)(2,1)S(1)} %collective-permute-done.20.refs_1_, bf16[8,16,128,128]{3,2,1,0:T(8,128)(2,1)S(1)} %bitcast.30, ...), custom_call_target="tpu_custom_call" | custom-call | tf_op jit(solution)/shard_map/pallas_call | solution.py:356
  94.5 0.7 collective-permute-start.28
  95.2 2.6 %collective-permute-start.27 = (bf16[8,128,128]{2,1,0:T(8,128)(2,1)S(1)}, bf16[8,128,128]{2,1,0:T(8,128)(2,1)S(1)}, u32[]{:S(2)}, u32[]{:S(2)}) collective-permute-start(bf16[8,128,128]{2,1,0:T(8,128)(2,1)S(1)} %get-tuple-element.56), channel_id=1, source_target_pairs={{0,1},{1,0},{2,3},{3,2},{4,5},{5,4},{6,7},{7,6},{8,9},{9,8},{10,11... | collective-permute-start | bytes 786440 | tf_op jit(solution)/shard_map/ppermute | solution.py:28
  97.9 1.1 collective-permute-done.23
  99.0 1.4 %collective-permute-start.26 = (f32[8,128]{1,0:T(8,128)S(1)}, f32[8,128]{1,0:T(8,128)S(1)}, u32[]{:S(2)}, u32[]{:S(2)}) collective-permute-start(f32[8,128]{1,0:T(8,128)S(1)} %add.42.refs_2_), channel_id=1, source_target_pairs={{0,6},{1,7},{2,4},{3,5},{4,2},{5,3},{6,0},{7,1},{8,14},{9,15},{10,... | collective-permute-start | bytes 12296 | tf_op jit(solution)/shard_map/ppermute | solution.py:39
  100.4 1.5 %collective-permute-start.25 = (f32[8,128]{1,0:T(8,128)S(1)}, f32[8,128]{1,0:T(8,128)S(1)}, u32[]{:S(2)}, u32[]{:S(2)}) collective-permute-start(f32[8,128]{1,0:T(8,128)S(1)} %add.42.refs_2_), channel_id=1, source_target_pairs={{0,4},{1,5},{2,6},{3,7},{4,0},{5,1},{6,2},{7,3},{8,12},{9,13},{10,... | collective-permute-start | bytes 12296 | tf_op jit(solution)/shard_map/ppermute | solution.py:39
  101.9 0.6 collective-permute-start.24
  102.5 1.0 collective-permute-done.26.refs_5_
  103.5 0.5 collective-permute-done.25.refs_4_
  104.0 1.5 %collective-permute-done.24.refs_3_ = f32[8,128]{1,0:T(8,128)S(1)} collective-permute-done((f32[8,128]{1,0:T(8,128)S(1)}, f32[8,128]{1,0:T(8,128)S(1)}, u32[]{:S(2)}, u32[]{:S(2)}) %collective-permute-start.24) | collective-permute-done | bytes 4128 | tf_op jit(solution)/shard_map/ppermute | solution.py:39
  105.5 3.6 %shard_map.122 = (f32[8,128,128]{2,1,0:T(8,128)S(1)}, f32[8,128,128]{2,1,0:T(8,128)S(1)}, bf16[8,128,128]{2,1,0:T(8,128)(2,1)S(1)}, f32[8,128]{1,0:T(8,128)S(1)}...) custom-call(s32[8,16]{1,0:T(8,128)} %fusion.3.refs_0_, s32[8]{0:T(128)} %refs_1_.11, f32[8,128]{1,0:T(8,128)S(1)} %add.42.refs_2_, ...), custom_call_target="tpu_custom_call" | custom-call | tf_op jit(solution)/shard_map/pallas_call | solution.py:356
  109.2 0.9 collective-permute-start.34
  110.0 2.0 %collective-permute-start.33 = (bf16[8,128,128]{2,1,0:T(8,128)(2,1)S(1)}, bf16[8,128,128]{2,1,0:T(8,128)(2,1)S(1)}, u32[]{:S(2)}, u32[]{:S(2)}) collective-permute-start(bf16[8,128,128]{2,1,0:T(8,128)(2,1)S(1)} %get-tuple-element.62), channel_id=1, source_target_pairs={{0,1},{1,0},{2,3},{3,2},{4,5},{5,4},{6,7},{7,6},{8,9},{9,8},{10,11... | collective-permute-start | bytes 786440 | tf_op jit(solution)/shard_map/ppermute | solution.py:28
  112.1 1.1 collective-permute-done.29
  113.2 1.7 %collective-permute-start.32 = (f32[8,128]{1,0:T(8,128)S(1)}, f32[8,128]{1,0:T(8,128)S(1)}, u32[]{:S(2)}, u32[]{:S(2)}) collective-permute-start(f32[8,128]{1,0:T(8,128)S(1)} %add.43.refs_2_), channel_id=1, source_target_pairs={{0,6},{1,7},{2,4},{3,5},{4,2},{5,3},{6,0},{7,1},{8,14},{9,15},{10,... | collective-permute-start | bytes 12296 | tf_op jit(solution)/shard_map/ppermute | solution.py:39
  114.8 1.5 %collective-permute-start.31 = (f32[8,128]{1,0:T(8,128)S(1)}, f32[8,128]{1,0:T(8,128)S(1)}, u32[]{:S(2)}, u32[]{:S(2)}) collective-permute-start(f32[8,128]{1,0:T(8,128)S(1)} %add.43.refs_2_), channel_id=1, source_target_pairs={{0,4},{1,5},{2,6},{3,7},{4,0},{5,1},{6,2},{7,3},{8,12},{9,13},{10,... | collective-permute-start | bytes 12296 | tf_op jit(solution)/shard_map/ppermute | solution.py:39
  116.7 1.0 collective-permute-done.32.refs_5_
  117.7 0.8 collective-permute-done.31.refs_4_
  118.4 1.5 %collective-permute-done.30.refs_3_ = f32[8,128]{1,0:T(8,128)S(1)} collective-permute-done((f32[8,128]{1,0:T(8,128)S(1)}, f32[8,128]{1,0:T(8,128)S(1)}, u32[]{:S(2)}, u32[]{:S(2)}) %collective-permute-start.30) | collective-permute-done | bytes 4128 | tf_op jit(solution)/shard_map/ppermute | solution.py:39
  120.0 3.8 %shard_map.123 = (f32[8,128,128]{2,1,0:T(8,128)S(1)}, f32[8,128,128]{2,1,0:T(8,128)S(1)}, f32[8,128]{1,0:T(8,128)S(1)}) custom-call(s32[8,16]{1,0:T(8,128)} %fusion.3.refs_0_, s32[8]{0:T(128)} %refs_1_.11, f32[8,128]{1,0:T(8,128)S(1)} %add.43.refs_2_, f32[8,128]{1,0:T(8,128)S(1)} %collective-permute-done.30.refs_3_, ...), custom_call_target="tpu_custom_call" | custom-call | tf_op jit(solution)/shard_map/pallas_call | solution.py:356
  123.9 1.2 collective-permute-done.35
  125.0 1.6 %collective-permute-start.38 = (f32[8,128]{1,0:T(8,128)S(1)}, f32[8,128]{1,0:T(8,128)S(1)}, u32[]{:S(2)}, u32[]{:S(2)}) collective-permute-start(f32[8,128]{1,0:T(8,128)S(1)} %add.44.refs_0_), channel_id=1, source_target_pairs={{0,6},{1,7},{2,4},{3,5},{4,2},{5,3},{6,0},{7,1},{8,14},{9,15},{10,... | collective-permute-start | bytes 12296 | tf_op jit(solution)/shard_map/ppermute | solution.py:39
  126.6 1.4 %collective-permute-start.37 = (f32[8,128]{1,0:T(8,128)S(1)}, f32[8,128]{1,0:T(8,128)S(1)}, u32[]{:S(2)}, u32[]{:S(2)}) collective-permute-start(f32[8,128]{1,0:T(8,128)S(1)} %add.44.refs_0_), channel_id=1, source_target_pairs={{0,4},{1,5},{2,6},{3,7},{4,0},{5,1},{6,2},{7,3},{8,12},{9,13},{10,... | collective-permute-start | bytes 12296 | tf_op jit(solution)/shard_map/ppermute | solution.py:39
  128.0 0.5 collective-permute-start.36
  128.5 1.0 shard_map.121
  129.6 0.7 collective-permute-done.37.refs_2_
  130.2 1.4 %collective-permute-done.36.refs_1_ = f32[8,128]{1,0:T(8,128)S(1)} collective-permute-done((f32[8,128]{1,0:T(8,128)S(1)}, f32[8,128]{1,0:T(8,128)S(1)}, u32[]{:S(2)}, u32[]{:S(2)}) %collective-permute-start.36) | collective-permute-done | bytes 4128 | tf_op jit(solution)/shard_map/ppermute | solution.py:39
  131.6 1.0 shard_map.124
  (49 shorter events, 1.8 us)
Async XLA Ops:
  1.8 11.6 %collective-permute-start.1 = (bf16[8,128,128]{2,1,0:T(8,128)(2,1)S(1)}, bf16[8,128,128]{2,1,0:T(8,128)(2,1)S(1)}, u32[]{:S(2)}, u32[]{:S(2)}) collective-permute-start(bf16[8,128,128]{2,1,0:T(8,128)(2,1)S(1)} %get-tuple-element.34.refs_1_), channel_id=1, source_target_pairs={{1,2},{2,1},{3,4},{4,3},{5,6},{6,5},{9,10},{10,9},{11,12},{12,11},... | collective-permute-start | bytes 786440 | tf_op jit(solution)/shard_map/ppermute | solution.py:27
  2.5 10.9 %collective-permute-start = (bf16[8,128,128]{2,1,0:T(8,128)(2,1)S(1)}, bf16[8,128,128]{2,1,0:T(8,128)(2,1)S(1)}, u32[]{:S(2)}, u32[]{:S(2)}) collective-permute-start(bf16[8,128,128]{2,1,0:T(8,128)(2,1)S(1)} %get-tuple-element.34.refs_1_), channel_id=1, source_target_pairs={{0,1},{1,0},{2,3},{3,2},{4,5},{5,4},{6,7},{7,6},{8,9},{9,8},{10,11... | collective-permute-start | bytes 786440 | tf_op jit(solution)/shard_map/ppermute | solution.py:28
  8.5 15.5 %collective-permute-start.9 = (bf16[8,128,128]{2,1,0:T(8,128)(2,1)S(1)}, bf16[8,128,128]{2,1,0:T(8,128)(2,1)S(1)}, u32[]{:S(2)}, u32[]{:S(2)}) collective-permute-start(bf16[8,128,128]{2,1,0:T(8,128)(2,1)S(1)} %get-tuple-element.39), channel_id=1, source_target_pairs={{1,2},{2,1},{3,4},{4,3},{5,6},{6,5},{9,10},{10,9},{11,12},{12,11},... | collective-permute-start | bytes 786440 | tf_op jit(solution)/shard_map/ppermute | solution.py:27
  9.2 19.7 %collective-permute-start.8 = (bf16[8,128,128]{2,1,0:T(8,128)(2,1)S(1)}, bf16[8,128,128]{2,1,0:T(8,128)(2,1)S(1)}, u32[]{:S(2)}, u32[]{:S(2)}) collective-permute-start(bf16[8,128,128]{2,1,0:T(8,128)(2,1)S(1)} %get-tuple-element.39), channel_id=1, source_target_pairs={{0,1},{1,0},{2,3},{3,2},{4,5},{5,4},{6,7},{7,6},{8,9},{9,8},{10,11... | collective-permute-start | bytes 786440 | tf_op jit(solution)/shard_map/ppermute | solution.py:28
  13.4 35.0 %copy-start = (bf16[1,8,16,128,128]{4,3,2,1,0:T(8,128)(2,1)S(1)}, bf16[1,8,16,128,128]{4,3,2,1,0:T(8,128)(2,1)}, u32[]{:S(2)}) copy-start(bf16[1,8,16,128,128]{4,3,2,1,0:T(8,128)(2,1)} %param.14) | copy-start | bytes 12582916
  13.4 35.0 %copy-start.1 = (bf16[1,8,16,128,128]{4,3,2,1,0:T(8,128)(2,1)S(1)}, bf16[1,8,16,128,128]{4,3,2,1,0:T(8,128)(2,1)}, u32[]{:S(2)}) copy-start(bf16[1,8,16,128,128]{4,3,2,1,0:T(8,128)(2,1)} %param.15) | copy-start | bytes 12582916
  13.4 35.0 %copy-start.3 = (f32[1,8,128,128]{3,2,1,0:T(8,128)S(1)}, f32[1,8,128,128]{3,2,1,0:T(8,128)}, u32[]{:S(2)}) copy-start(f32[1,8,128,128]{3,2,1,0:T(8,128)} %param.12) | copy-start | bytes 1572868
  18.4 30.0 %collective-permute-start.7 = (bf16[8,128,128]{2,1,0:T(8,128)(2,1)S(1)}, bf16[8,128,128]{2,1,0:T(8,128)(2,1)S(1)}, u32[]{:S(2)}, u32[]{:S(2)}) collective-permute-start(bf16[8,128,128]{2,1,0:T(8,128)(2,1)S(1)} %get-tuple-element.38), channel_id=1, source_target_pairs={{1,2},{2,1},{3,4},{4,3},{5,6},{6,5},{9,10},{10,9},{11,12},{12,11},... | collective-permute-start | bytes 786440 | tf_op jit(solution)/shard_map/ppermute | solution.py:27
  19.2 29.2 %collective-permute-start.6 = (bf16[8,128,128]{2,1,0:T(8,128)(2,1)S(1)}, bf16[8,128,128]{2,1,0:T(8,128)(2,1)S(1)}, u32[]{:S(2)}, u32[]{:S(2)}) collective-permute-start(bf16[8,128,128]{2,1,0:T(8,128)(2,1)S(1)} %get-tuple-element.38), channel_id=1, source_target_pairs={{0,1},{1,0},{2,3},{3,2},{4,5},{5,4},{6,7},{7,6},{8,9},{9,8},{10,11... | collective-permute-start | bytes 786440 | tf_op jit(solution)/shard_map/ppermute | solution.py:28
  22.1 1.2 collective-permute-start.2
  23.3 60.5 %collective-permute-start.22 = (bf16[16,128,128]{2,1,0:T(8,128)(2,1)S(1)}, bf16[16,128,128]{2,1,0:T(8,128)(2,1)S(1)}, u32[]{:S(2)}, u32[]{:S(2)}) collective-permute-start(bf16[16,128,128]{2,1,0:T(8,128)(2,1)S(1)} %get-tuple-element.49), channel_id=1, source_target_pairs={{1,2},{2,1},{3,4},{4,3},{5,6},{6,5},{9,10},{10,9},{11,12},{12,11},... | collective-permute-start | bytes 1572872 | tf_op jit(solution)/shard_map/ppermute | solution.py:27
  24.0 12.0 %collective-permute-start.5 = (f32[8,128]{1,0:T(8,128)S(1)}, f32[8,128]{1,0:T(8,128)S(1)}, u32[]{:S(2)}, u32[]{:S(2)}) collective-permute-start(f32[8,128]{1,0:T(8,128)S(1)} %add.39.refs_2_), channel_id=1, source_target_pairs={{0,6},{1,7},{2,4},{3,5},{4,2},{5,3},{6,0},{7,1},{8,14},{9,15},{10,... | collective-permute-start | bytes 12296 | tf_op jit(solution)/shard_map/ppermute | solution.py:39
  28.9 54.9 %collective-permute-start.21 = (bf16[16,128,128]{2,1,0:T(8,128)(2,1)S(1)}, bf16[16,128,128]{2,1,0:T(8,128)(2,1)S(1)}, u32[]{:S(2)}, u32[]{:S(2)}) collective-permute-start(bf16[16,128,128]{2,1,0:T(8,128)(2,1)S(1)} %get-tuple-element.49), channel_id=1, source_target_pairs={{0,1},{1,0},{2,3},{3,2},{4,5},{5,4},{6,7},{7,6},{8,9},{9,8},{10,11... | collective-permute-start | bytes 1572872 | tf_op jit(solution)/shard_map/ppermute | solution.py:28
  36.0 6.8 %collective-permute-start.4 = (f32[8,128]{1,0:T(8,128)S(1)}, f32[8,128]{1,0:T(8,128)S(1)}, u32[]{:S(2)}, u32[]{:S(2)}) collective-permute-start(f32[8,128]{1,0:T(8,128)S(1)} %add.39.refs_2_), channel_id=1, source_target_pairs={{0,4},{1,5},{2,6},{3,7},{4,0},{5,1},{6,2},{7,3},{8,12},{9,13},{10,... | collective-permute-start | bytes 12296 | tf_op jit(solution)/shard_map/ppermute | solution.py:39
  42.8 5.5 %collective-permute-start.3 = (f32[8,128]{1,0:T(8,128)S(1)}, f32[8,128]{1,0:T(8,128)S(1)}, u32[]{:S(2)}, u32[]{:S(2)}) collective-permute-start(f32[8,128]{1,0:T(8,128)S(1)} %add.39.refs_2_), channel_id=1, source_target_pairs={{0,2},{1,3},{2,0},{3,1},{4,6},{5,7},{6,4},{7,5},{8,10},{9,11},{10,... | collective-permute-start | bytes 12296 | tf_op jit(solution)/shard_map/ppermute | solution.py:39
  52.1 17.0 %collective-permute-start.15 = (bf16[8,128,128]{2,1,0:T(8,128)(2,1)S(1)}, bf16[8,128,128]{2,1,0:T(8,128)(2,1)S(1)}, u32[]{:S(2)}, u32[]{:S(2)}) collective-permute-start(bf16[8,128,128]{2,1,0:T(8,128)(2,1)S(1)} %get-tuple-element.45), channel_id=1, source_target_pairs={{1,2},{2,1},{3,4},{4,3},{5,6},{6,5},{9,10},{10,9},{11,12},{12,11},... | collective-permute-start | bytes 786440 | tf_op jit(solution)/shard_map/ppermute | solution.py:27
  52.8 16.3 %collective-permute-start.14 = (bf16[8,128,128]{2,1,0:T(8,128)(2,1)S(1)}, bf16[8,128,128]{2,1,0:T(8,128)(2,1)S(1)}, u32[]{:S(2)}, u32[]{:S(2)}) collective-permute-start(bf16[8,128,128]{2,1,0:T(8,128)(2,1)S(1)} %get-tuple-element.45), channel_id=1, source_target_pairs={{0,1},{1,0},{2,3},{3,2},{4,5},{5,4},{6,7},{7,6},{8,9},{9,8},{10,11... | collective-permute-start | bytes 786440 | tf_op jit(solution)/shard_map/ppermute | solution.py:28
  56.2 1.2 collective-permute-start.10
  57.4 4.5 %collective-permute-start.13 = (f32[8,128]{1,0:T(8,128)S(1)}, f32[8,128]{1,0:T(8,128)S(1)}, u32[]{:S(2)}, u32[]{:S(2)}) collective-permute-start(f32[8,128]{1,0:T(8,128)S(1)} %add.40.refs_2_), channel_id=1, source_target_pairs={{0,6},{1,7},{2,4},{3,5},{4,2},{5,3},{6,0},{7,1},{8,14},{9,15},{10,... | collective-permute-start | bytes 12296 | tf_op jit(solution)/shard_map/ppermute | solution.py:39
  61.9 3.6 %collective-permute-start.12 = (f32[8,128]{1,0:T(8,128)S(1)}, f32[8,128]{1,0:T(8,128)S(1)}, u32[]{:S(2)}, u32[]{:S(2)}) collective-permute-start(f32[8,128]{1,0:T(8,128)S(1)} %add.40.refs_2_), channel_id=1, source_target_pairs={{0,4},{1,5},{2,6},{3,7},{4,0},{5,1},{6,2},{7,3},{8,12},{9,13},{10,... | collective-permute-start | bytes 12296 | tf_op jit(solution)/shard_map/ppermute | solution.py:39
  65.5 3.6 %collective-permute-start.11 = (f32[8,128]{1,0:T(8,128)S(1)}, f32[8,128]{1,0:T(8,128)S(1)}, u32[]{:S(2)}, u32[]{:S(2)}) collective-permute-start(f32[8,128]{1,0:T(8,128)S(1)} %add.40.refs_2_), channel_id=1, source_target_pairs={{0,2},{1,3},{2,0},{3,1},{4,6},{5,7},{6,4},{7,5},{8,10},{9,11},{10,... | collective-permute-start | bytes 12296 | tf_op jit(solution)/shard_map/ppermute | solution.py:39
  69.1 14.8 %copy-start.2 = (bf16[1,8,16,128,128]{4,3,2,1,0:T(8,128)(2,1)S(1)}, bf16[1,8,16,128,128]{4,3,2,1,0:T(8,128)(2,1)}, u32[]{:S(2)}) copy-start(bf16[1,8,16,128,128]{4,3,2,1,0:T(8,128)(2,1)} %param.17) | copy-start | bytes 12582916
  73.1 10.8 %copy-start.6 = (f32[1,8,128,128]{3,2,1,0:T(8,128)S(1)}, f32[1,8,128,128]{3,2,1,0:T(8,128)}, u32[]{:S(2)}) copy-start(f32[1,8,128,128]{3,2,1,0:T(8,128)} %param.11) | copy-start | bytes 1572868
  73.1 1.2 collective-permute-start.16
  74.3 4.5 %collective-permute-start.19 = (f32[8,128]{1,0:T(8,128)S(1)}, f32[8,128]{1,0:T(8,128)S(1)}, u32[]{:S(2)}, u32[]{:S(2)}) collective-permute-start(f32[8,128]{1,0:T(8,128)S(1)} %add.41.refs_0_), channel_id=1, source_target_pairs={{0,6},{1,7},{2,4},{3,5},{4,2},{5,3},{6,0},{7,1},{8,14},{9,15},{10,... | collective-permute-start | bytes 12296 | tf_op jit(solution)/shard_map/ppermute | solution.py:39
  75.5 3.6 %collective-permute-start.18 = (f32[8,128]{1,0:T(8,128)S(1)}, f32[8,128]{1,0:T(8,128)S(1)}, u32[]{:S(2)}, u32[]{:S(2)}) collective-permute-start(f32[8,128]{1,0:T(8,128)S(1)} %add.41.refs_0_), channel_id=1, source_target_pairs={{0,4},{1,5},{2,6},{3,7},{4,0},{5,1},{6,2},{7,3},{8,12},{9,13},{10,... | collective-permute-start | bytes 12296 | tf_op jit(solution)/shard_map/ppermute | solution.py:39
  76.1 3.6 %collective-permute-start.17 = (f32[8,128]{1,0:T(8,128)S(1)}, f32[8,128]{1,0:T(8,128)S(1)}, u32[]{:S(2)}, u32[]{:S(2)}) collective-permute-start(f32[8,128]{1,0:T(8,128)S(1)} %add.41.refs_0_), channel_id=1, source_target_pairs={{0,2},{1,3},{2,0},{3,1},{4,6},{5,7},{6,4},{7,5},{8,10},{9,11},{10,... | collective-permute-start | bytes 12296 | tf_op jit(solution)/shard_map/ppermute | solution.py:39
  79.7 8.8 %copy-start.4 = (f32[1,8,128,128]{3,2,1,0:T(8,128)S(1)}, f32[1,8,128,128]{3,2,1,0:T(8,128)}, u32[]{:S(2)}) copy-start(f32[1,8,128,128]{3,2,1,0:T(8,128)} %param.13) | copy-start | bytes 1572868
  79.7 8.8 %copy-start.5 = (bf16[1,8,16,128,128]{4,3,2,1,0:T(8,128)(2,1)S(1)}, bf16[1,8,16,128,128]{4,3,2,1,0:T(8,128)(2,1)}, u32[]{:S(2)}) copy-start(bf16[1,8,16,128,128]{4,3,2,1,0:T(8,128)(2,1)} %param.16) | copy-start | bytes 12582916
  80.0 8.5 %collective-permute-start.20 = (bf16[8,128,128]{2,1,0:T(8,128)(2,1)S(1)}, bf16[8,128,128]{2,1,0:T(8,128)(2,1)S(1)}, u32[]{:S(2)}, u32[]{:S(2)}) collective-permute-start(bf16[8,128,128]{2,1,0:T(8,128)(2,1)S(1)} %shard_map.118), channel_id=1, source_target_pairs={{0,8},{8,16},{16,24},{1,9},{9,17},{17,25},{2,10},{10,18},{18,26},{... | collective-permute-start | bytes 786440 | tf_op jit(solution)/shard_map/ppermute | solution.py:487
  94.5 11.0 %collective-permute-start.28 = (bf16[8,128,128]{2,1,0:T(8,128)(2,1)S(1)}, bf16[8,128,128]{2,1,0:T(8,128)(2,1)S(1)}, u32[]{:S(2)}, u32[]{:S(2)}) collective-permute-start(bf16[8,128,128]{2,1,0:T(8,128)(2,1)S(1)} %get-tuple-element.56), channel_id=1, source_target_pairs={{1,2},{2,1},{3,4},{4,3},{5,6},{6,5},{9,10},{10,9},{11,12},{12,11},... | collective-permute-start | bytes 786440 | tf_op jit(solution)/shard_map/ppermute | solution.py:27
  95.2 10.3 %collective-permute-start.27 = (bf16[8,128,128]{2,1,0:T(8,128)(2,1)S(1)}, bf16[8,128,128]{2,1,0:T(8,128)(2,1)S(1)}, u32[]{:S(2)}, u32[]{:S(2)}) collective-permute-start(bf16[8,128,128]{2,1,0:T(8,128)(2,1)S(1)} %get-tuple-element.56), channel_id=1, source_target_pairs={{0,1},{1,0},{2,3},{3,2},{4,5},{5,4},{6,7},{7,6},{8,9},{9,8},{10,11... | collective-permute-start | bytes 786440 | tf_op jit(solution)/shard_map/ppermute | solution.py:28
  97.8 1.2 collective-permute-start.23
  99.0 4.5 %collective-permute-start.26 = (f32[8,128]{1,0:T(8,128)S(1)}, f32[8,128]{1,0:T(8,128)S(1)}, u32[]{:S(2)}, u32[]{:S(2)}) collective-permute-start(f32[8,128]{1,0:T(8,128)S(1)} %add.42.refs_2_), channel_id=1, source_target_pairs={{0,6},{1,7},{2,4},{3,5},{4,2},{5,3},{6,0},{7,1},{8,14},{9,15},{10,... | collective-permute-start | bytes 12296 | tf_op jit(solution)/shard_map/ppermute | solution.py:39
  100.4 3.6 %collective-permute-start.25 = (f32[8,128]{1,0:T(8,128)S(1)}, f32[8,128]{1,0:T(8,128)S(1)}, u32[]{:S(2)}, u32[]{:S(2)}) collective-permute-start(f32[8,128]{1,0:T(8,128)S(1)} %add.42.refs_2_), channel_id=1, source_target_pairs={{0,4},{1,5},{2,6},{3,7},{4,0},{5,1},{6,2},{7,3},{8,12},{9,13},{10,... | collective-permute-start | bytes 12296 | tf_op jit(solution)/shard_map/ppermute | solution.py:39
  101.9 3.6 %collective-permute-start.24 = (f32[8,128]{1,0:T(8,128)S(1)}, f32[8,128]{1,0:T(8,128)S(1)}, u32[]{:S(2)}, u32[]{:S(2)}) collective-permute-start(f32[8,128]{1,0:T(8,128)S(1)} %add.42.refs_2_), channel_id=1, source_target_pairs={{0,2},{1,3},{2,0},{3,1},{4,6},{5,7},{6,4},{7,5},{8,10},{9,11},{10,... | collective-permute-start | bytes 12296 | tf_op jit(solution)/shard_map/ppermute | solution.py:39
  109.2 10.8 %collective-permute-start.34 = (bf16[8,128,128]{2,1,0:T(8,128)(2,1)S(1)}, bf16[8,128,128]{2,1,0:T(8,128)(2,1)S(1)}, u32[]{:S(2)}, u32[]{:S(2)}) collective-permute-start(bf16[8,128,128]{2,1,0:T(8,128)(2,1)S(1)} %get-tuple-element.62), channel_id=1, source_target_pairs={{1,2},{2,1},{3,4},{4,3},{5,6},{6,5},{9,10},{10,9},{11,12},{12,11},... | collective-permute-start | bytes 786440 | tf_op jit(solution)/shard_map/ppermute | solution.py:27
  110.0 9.9 %collective-permute-start.33 = (bf16[8,128,128]{2,1,0:T(8,128)(2,1)S(1)}, bf16[8,128,128]{2,1,0:T(8,128)(2,1)S(1)}, u32[]{:S(2)}, u32[]{:S(2)}) collective-permute-start(bf16[8,128,128]{2,1,0:T(8,128)(2,1)S(1)} %get-tuple-element.62), channel_id=1, source_target_pairs={{0,1},{1,0},{2,3},{3,2},{4,5},{5,4},{6,7},{7,6},{8,9},{9,8},{10,11... | collective-permute-start | bytes 786440 | tf_op jit(solution)/shard_map/ppermute | solution.py:28
  112.0 1.2 collective-permute-start.29
  113.2 4.5 %collective-permute-start.32 = (f32[8,128]{1,0:T(8,128)S(1)}, f32[8,128]{1,0:T(8,128)S(1)}, u32[]{:S(2)}, u32[]{:S(2)}) collective-permute-start(f32[8,128]{1,0:T(8,128)S(1)} %add.43.refs_2_), channel_id=1, source_target_pairs={{0,6},{1,7},{2,4},{3,5},{4,2},{5,3},{6,0},{7,1},{8,14},{9,15},{10,... | collective-permute-start | bytes 12296 | tf_op jit(solution)/shard_map/ppermute | solution.py:39
  114.8 3.6 %collective-permute-start.31 = (f32[8,128]{1,0:T(8,128)S(1)}, f32[8,128]{1,0:T(8,128)S(1)}, u32[]{:S(2)}, u32[]{:S(2)}) collective-permute-start(f32[8,128]{1,0:T(8,128)S(1)} %add.43.refs_2_), channel_id=1, source_target_pairs={{0,4},{1,5},{2,6},{3,7},{4,0},{5,1},{6,2},{7,3},{8,12},{9,13},{10,... | collective-permute-start | bytes 12296 | tf_op jit(solution)/shard_map/ppermute | solution.py:39
  116.3 3.6 %collective-permute-start.30 = (f32[8,128]{1,0:T(8,128)S(1)}, f32[8,128]{1,0:T(8,128)S(1)}, u32[]{:S(2)}, u32[]{:S(2)}) collective-permute-start(f32[8,128]{1,0:T(8,128)S(1)} %add.43.refs_2_), channel_id=1, source_target_pairs={{0,2},{1,3},{2,0},{3,1},{4,6},{5,7},{6,4},{7,5},{8,10},{9,11},{10,... | collective-permute-start | bytes 12296 | tf_op jit(solution)/shard_map/ppermute | solution.py:39
  123.8 1.2 collective-permute-start.35
  125.0 4.5 %collective-permute-start.38 = (f32[8,128]{1,0:T(8,128)S(1)}, f32[8,128]{1,0:T(8,128)S(1)}, u32[]{:S(2)}, u32[]{:S(2)}) collective-permute-start(f32[8,128]{1,0:T(8,128)S(1)} %add.44.refs_0_), channel_id=1, source_target_pairs={{0,6},{1,7},{2,4},{3,5},{4,2},{5,3},{6,0},{7,1},{8,14},{9,15},{10,... | collective-permute-start | bytes 12296 | tf_op jit(solution)/shard_map/ppermute | solution.py:39
  126.6 3.6 %collective-permute-start.37 = (f32[8,128]{1,0:T(8,128)S(1)}, f32[8,128]{1,0:T(8,128)S(1)}, u32[]{:S(2)}, u32[]{:S(2)}) collective-permute-start(f32[8,128]{1,0:T(8,128)S(1)} %add.44.refs_0_), channel_id=1, source_target_pairs={{0,4},{1,5},{2,6},{3,7},{4,0},{5,1},{6,2},{7,3},{8,12},{9,13},{10,... | collective-permute-start | bytes 12296 | tf_op jit(solution)/shard_map/ppermute | solution.py:39
  128.0 3.6 %collective-permute-start.36 = (f32[8,128]{1,0:T(8,128)S(1)}, f32[8,128]{1,0:T(8,128)S(1)}, u32[]{:S(2)}, u32[]{:S(2)}) collective-permute-start(f32[8,128]{1,0:T(8,128)S(1)} %add.44.refs_0_), channel_id=1, source_target_pairs={{0,2},{1,3},{2,0},{3,1},{4,6},{5,7},{6,4},{7,5},{8,10},{9,11},{10,... | collective-permute-start | bytes 12296 | tf_op jit(solution)/shard_map/ppermute | solution.py:39
